TPU v7x, 256 devices: a whole 4x4x8 slice. The times are simulated.
256 devices in a mesh: lon: 16 (over x, y_lo, core), lat: 8 (over z), tm: 2 (over y_hi).
Axes of the slice: x: 4, y: 4 (y_hi: 2, y_lo: 2; y = y_hi * 2 + y_lo), z: 8, core: 2. Of those that a mesh axis runs over, the one named last changes fastest.
Arguments:
- snapshots: float32 [16, 8, 128, 2048], P('tm', None, 'lat', 'lon'), may hold values from -6 to 6
- basis: float32 [64, 8, 128, 2048], P(None, None, 'lat', 'lon'), may hold values from -6 to 6
Outputs:
- new_basis: float32 [64, 8, 128, 2048], P(None, None, 'lat', 'lon')
- coeffs: float32 [64, 16], P(None, 'tm')
All inputs are finite; a program needn't handle non-finite values.
Results may differ from a plain program's by a relative error of at most 0.00011.
Values sent between devices are 32-bit elements; how exact they have to be, the bound alone decides.
No kernel may reach another device: no remote copies, remote signals or barrier semaphores. Data moves between devices by JAX's collectives and lax.ppermute only.
A program may use at most 64 MiB of HBM per device.

v0:
```python
import math

import jax
import jax.numpy as jnp
from jax import lax
from jax.sharding import PartitionSpec as P

SMOOTH_RATE = 0.1
STEP_SIZE = 0.25


def with_halo(cells, sides, width, closed):
    for axis, dim in sides:
        count = lax.axis_size(axis)
        ends = count if closed else count - 1
        head = lax.slice_in_dim(cells, 0, width, axis=dim)
        tail = lax.slice_in_dim(cells, cells.shape[dim] - width, cells.shape[dim], axis=dim)
        cells = jnp.concatenate(
            [
                lax.ppermute(tail, axis, [(i, (i + 1) % count) for i in range(ends)]),
                cells,
                lax.ppermute(head, axis, [((i + 1) % count, i) for i in range(ends)]),
            ],
            axis=dim,
        )
    return cells


def product(left, right):
    return jnp.dot(left, right, precision=lax.Precision.HIGHEST, preferred_element_type=jnp.float32)


def laplace_step(extended):
    padded = jnp.pad(extended, ((0, 0), (1, 1), (0, 0), (0, 0)))
    center = extended[:, :, 1:-1, 1:-1]
    neighbours = padded[:, 2:, 1:-1, 1:-1] + padded[:, :-2, 1:-1, 1:-1]
    neighbours = neighbours + extended[:, :, 2:, 1:-1] + extended[:, :, :-2, 1:-1]
    neighbours = neighbours + extended[:, :, 1:-1, 2:] + extended[:, :, 1:-1, :-2]
    return center + SMOOTH_RATE * (neighbours - 6.0 * center)


def finish(grown, gram_matrix):
    factor = jnp.linalg.cholesky(gram_matrix)
    return jax.scipy.linalg.solve_triangular(factor, grown, lower=True)


def shards(snapshots, basis):
    snap_count, levels, rows_lat, cols_lon = snapshots.shape
    eof_count = basis.shape[0]
    total_cells = levels * rows_lat * cols_lon * lax.axis_size("lat") * lax.axis_size("lon")
    inv_root = 1.0 / math.sqrt(total_cells)
    smoothed = snapshots
    for sweep in range(3):
        lat_wide = with_halo(smoothed, (("lat", 2),), 1, False)
        extended = with_halo(lat_wide, (("lon", 3),), 1, True)
        smoothed = laplace_step(extended)
    flattened = smoothed.reshape(snap_count, -1)
    columns = basis.reshape(eof_count, -1)
    coeffs = lax.psum(product(columns, flattened.T), ("lon", "lat")) * inv_root
    update_term = STEP_SIZE * product(coeffs, flattened)
    grown = columns + lax.psum(update_term, "tm")
    gram_matrix = lax.psum(product(grown, grown.T), ("lon", "lat")) / total_cells
    new_basis = finish(grown, gram_matrix)
    return (new_basis.reshape(basis.shape), coeffs)


def solution(mesh):
    placed = (P("tm", None, "lat", "lon"), P(None, None, "lat", "lon"))
    return jax.shard_map(
        shards,
        mesh=mesh,
        in_specs=placed,
        out_specs=(P(None, None, "lat", "lon"), P(None, "tm")),
        check_vma=False,
    )
```

profile of v0, /device:TPU:1, one launch (start us, length us, event | category | flops | bytes accessed | tf_op | source)
XLA Modules:
  0.0 1084.9 jit_solution(14280274604795155072)
XLA Ops:
  9.7 5.0 collective-permute-start
  14.7 3.5 copy.78
  18.2 2.7 copy.79
  20.9 2.6 copy.77
  23.6 6.9 pad_maximum_fusion
  35.3 2.9 copy.81
  41.1 3.4 collective-permute-start.4
  45.8 3.5 collective-permute-done.5
  50.1 3.5 collective-permute-start.7
  58.9 4.8 collective-permute-start.8
  65.1 3.4 collective-permute-done.9
  69.2 6.1 collective-permute-start.11
  81.0 5.3 fusion.7
  86.3 269.8 %psum.21 = f32[64,8]{0,1:T(8,128)S(1)} all-reduce(f32[64,8]{0,1:T(8,128)S(1)} %fusion.7), channel_id=1, replica_groups=mesh['lon'=16,'lat'=8,'tm'=2] {'lon','lat'}, use_global_device_ids=true, to_apply=%region_0.1 | all-reduce | flops 512 | bytes 4096 | tf_op jit(solution)/shard_map/psum | solution.py:59
  356.1 5.1 convolution_multiply_fusion
  361.2 127.4 %all-reduce.5.cloned.1.call-done = f32[64,16384]{1,0:T(8,128)} async-done(((f32[64,16384]{1,0:T(8,128)}), f32[64,16384]{1,0:T(8,128)}) %all-reduce.5.cloned.1.call-update) | async-done | bytes 4194320 | tf_op jit(solution)/shard_map/psum | solution.py:61
  488.6 14.0 %fusion.6 = f32[64,64]{0,1:T(8,128)S(1)} fusion(f32[64,16384]{1,0:T(8,128)} %all-reduce.5.cloned.1.call-done, f32[8,8,128,128]{3,2,1,0:T(8,128)} %bitcast.37), kind=kOutput, calls=%fused_computation.21 | convolution fusion | flops 806354944 | bytes 8404992 | tf_op jit(solution)/shard_map/dot_general | solution.py:30
  502.6 541.3 %psum.23 = f32[64,64]{0,1:T(8,128)S(1)} all-reduce(f32[64,64]{0,1:T(8,128)S(1)} %fusion.6), channel_id=1, replica_groups=mesh['lon'=16,'lat'=8,'tm'=2] {'lon','lat'}, use_global_device_ids=true, to_apply=%region_2.3 | all-reduce | flops 4096 | bytes 32768 | tf_op jit(solution)/shard_map/psum | solution.py:62
  1043.9 6.1 fusion.5
  1050.0 2.8 copy.121
  1052.9 5.8 cholesky.16
  1060.1 4.9 custom-call.7
  1065.0 8.4 fusion
  1073.4 4.4 copy.110
  (58 shorter events, 26.6 us)
Async XLA Ops:
  7.2 481.5 %all-reduce.5.cloned.1.call-start = ((), (), s32[]{:S(2)}) async-start(), calls=%async_computation | async-start | bytes 8388608 | tf_op jit(solution)/shard_map/psum | solution.py:61
  8.4 9.8 collective-permute-start.1
  9.7 11.2 %collective-permute-start = (f32[8,8,1,128]{3,1,2,0:T(8,128)S(1)}, f32[8,8,1,128]{3,1,2,0:T(8,128)S(1)}, u32[]{:S(2)}, u32[]{:S(2)}) collective-permute-start(f32[8,8,1,128]{3,1,2,0:T(8,128)S(1)} %get-tuple-element.22), channel_id=1, source_target_pairs={{0,2},{2,4},{4,6},{6,8},{8,10},{10,12},{12,14},{1,3},{3,5},{5,7},{... | collective-permute-start | bytes 98312 | tf_op jit(solution)/shard_map/ppermute | solution.py:20
  30.4 2.0 copy-start.1
  32.5 5.7 collective-permute-start.2
  34.7 4.0 collective-permute-start.3
  41.1 4.7 collective-permute-start.4
  44.5 4.8 collective-permute-start.5
  50.1 4.5 collective-permute-start.7
  54.1 2.4 collective-permute-start.6
  58.9 6.2 collective-permute-start.8
  63.7 4.7 collective-permute-start.9
  69.2 7.0 collective-permute-start.11
  75.9 1.3 collective-permute-start.10
  78.8 2.2 copy-start
  356.1 5.1 copy-start.2
Sparse Core Ops, SparseCore 0:
  361.3 127.2 all-reduce.4
where the time goes:
time: 1100 us; the launch traced here: 1080 us
  blocking collectives  811 us (74%)
  waiting for transfers between devices  136 us (12%)
  matrix products  32.8 us (3%)
  other arithmetic  30.9 us (3%)
  starting transfers between devices  30.2 us (3%)
  local copies, waits for them, and re-layouts  29 us (3%)
  between operations  14.5 us (1%)
    psum x1, blocking collectives, shards(): lax.psum(product(grown, grown.T), ('lon', 'lat')) / total_cells  541 us
    psum x1, blocking collectives, shards(): coeffs = lax.psum(product(columns, flattened.T), ('lon', 'lat')) * inv_root  270 us
    psum x1, waiting for transfers between devices, shards(): grown = columns + lax.psum(update_term, 'tm')  127 us
    dot_general x3, matrix products, product(): jnp.dot(left, right, precision=lax.Precision.HIGHEST, preferred_element_t...  24.4 us
  transfers between devices with their start and end apart: 13, of which 6 were waited for; matrix products, arithmetic and copies ran while one was open for 1% of the time, Pallas kernels for 0%

commit v1 on v0

v1 whole, which is shorter than its diff:
```python
import functools
import math

import jax
import jax.numpy as jnp
from jax import lax
from jax.experimental import pallas as pl
from jax.experimental.pallas import tpu as pltpu
from jax.sharding import PartitionSpec as P

SMOOTH_RATE = 0.1
STEP_SIZE = 0.25
SNAPS = 8
LEVELS = 8
ROWS = 16
LANES = 128
EOFS = 64
CELL_ROWS = LEVELS * ROWS
HALF_ROWS = CELL_ROWS // 2
SLOTS = 16
PAYLOAD = 48
F32 = jnp.float32
BF16 = jnp.bfloat16
HIGHEST = lax.Precision.HIGHEST


def lanes_of(shape):
    return lax.broadcasted_iota(jnp.int32, shape, len(shape) - 1)


def pack_kernel(x_ref, packed_ref):
    lane = lanes_of((64, LANES))
    packed = jnp.zeros((64, LANES), F32)
    for slot in range(SLOTS):
        turned = pltpu.roll(x_ref[pl.ds(64 * slot, 64), :], (3 + 8 * slot) % LANES, 1)
        packed = jnp.where((lane >= 8 * slot) & (lane < 8 * slot + 6), turned, packed)
    packed_ref[...] = packed


def edges_kernel(x_ref, west_ref, east_ref, ghosts_ref, low_ref, high_ref):
    lane = lanes_of((64, LANES))
    ghosts = jnp.where(lane % 8 < 3, west_ref[...], east_ref[...])
    ghosts_ref[...] = ghosts
    for row in range(3):
        low_ref[pl.ds(64 * row, 64), :] = x_ref[pl.ds(row, 64, stride=ROWS), :]
        high_ref[pl.ds(64 * row, 64), :] = x_ref[pl.ds(ROWS - 3 + row, 64, stride=ROWS), :]
    low_ref[pl.ds(192, 64), :] = ghosts
    high_ref[pl.ds(192, 64), :] = ghosts


def smooth_kernel(flags_ref, x_ref, ghosts_ref, south_ref, north_ref, keep_ref, send_ref, own, ghost):
    half = flags_ref[0]
    row = lax.broadcasted_iota(jnp.int32, (32, LANES), 0)
    lane = lanes_of((32, LANES))
    first, last = lane == 0, lane == LANES - 1
    outside = ((row < 8) & (flags_ref[1] == 1)) | ((row >= 24) & (flags_ref[2] == 1))

    def snapshot(snap, carry):
        for level in range(LEVELS):
            own[pl.ds(32 * level + 8, ROWS), :] = x_ref[pl.ds(pl.multiple_of(snap * 128 + 16 * level, 16), ROWS), :]
        for edge in range(3):
            at = pl.ds(pl.multiple_of(64 * edge + 8 * snap, 8), LEVELS)
            own[pl.ds(5 + edge, LEVELS, stride=32), :] = south_ref[at, :]
            own[pl.ds(24 + edge, LEVELS, stride=32), :] = north_ref[at, :]
        for level in range(LEVELS):
            slot = 2 * snap + level // 4
            shift = lax.rem(253 - 8 * slot, LANES)
            at = 16 * (level % 4)
            strip = jnp.concatenate(
                [
                    south_ref[pl.ds(192 + at + 8, 8), :],
                    ghosts_ref[pl.ds(at, 16), :],
                    north_ref[pl.ds(192 + at, 8), :],
                ],
                axis=0,
            )
            ghost[pl.ds(32 * level, 32), :] = pltpu.roll(strip, shift, 1)
        for sweep in range(3):
            below_own = below_ghost = None
            for level in range(LEVELS):
                at = pl.ds(32 * level, 32)
                here_own, here_ghost = own[at, :], ghost[at, :]
                left_own, left_ghost = pltpu.roll(here_own, 1, 1), pltpu.roll(here_ghost, 1, 1)
                right_own, right_ghost = pltpu.roll(here_own, LANES - 1, 1), pltpu.roll(here_ghost, LANES - 1, 1)
                sums = []
                for here, below, ref, left, other_left, right, other_right in (
                    (here_own, below_own, own, left_own, left_ghost, right_own, right_ghost),
                    (here_ghost, below_ghost, ghost, left_ghost, left_own, right_ghost, right_own),
                ):
                    near = pltpu.roll(here, 1, 0) + pltpu.roll(here, 31, 0)
                    if level < LEVELS - 1:
                        near = near + ref[pl.ds(32 * level + 32, 32), :]
                    if level > 0:
                        near = near + below
                    near = near + jnp.where(first, other_left, left) + jnp.where(last, other_right, right)
                    fresh = here + SMOOTH_RATE * (near - 6.0 * here)
                    if sweep < 2:
                        fresh = jnp.where(outside, 0.0, fresh)
                    sums.append(fresh)
                below_own, below_ghost = here_own, here_ghost
                own[at, :] = sums[0]
                if sweep < 2:
                    ghost[at, :] = sums[1]
        for level in range(LEVELS // 2):
            to = pl.ds(pl.multiple_of(64 * snap + 16 * level, 16), ROWS)
            keep_at = pl.multiple_of(32 * (4 * half + level) + 8, 8)
            send_at = pl.multiple_of(32 * (4 * (1 - half) + level) + 8, 8)
            keep_ref[to, :] = own[pl.ds(keep_at, ROWS), :]
            send_ref[to, :] = own[pl.ds(send_at, ROWS), :]
        return carry

    lax.fori_loop(0, SNAPS, snapshot, 0)


def in_order(flags_ref, mine, other):
    early = jnp.where(flags_ref[0] == 0, mine, other)
    late = jnp.where(flags_ref[0] == 0, other, mine)
    return early, late


def take(ref, row):
    fields, rows, lanes = ref.shape
    return ref.reshape(fields * rows, lanes)[pl.ds(row, fields, stride=rows), :]


def put(ref, row, values):
    fields, rows, lanes = ref.shape
    ref.reshape(fields * rows, lanes)[pl.ds(row, fields, stride=rows), :] = values


def pieces(values, count):
    out = []
    for index in range(count):
        piece = values.astype(BF16)
        out.append(piece)
        if index < count - 1:
            values = values - piece.astype(F32)
    return out


def gram_kernel(flags_ref, q_ref, mine_ref, other_ref, out_ref, stack, total):
    total[...] = jnp.zeros_like(total)

    def block(step, carry):
        for inner in range(8):
            row = 8 * step + inner
            early, late = in_order(
                flags_ref,
                mine_ref[pl.ds(row, SNAPS, stride=HALF_ROWS), :],
                other_ref[pl.ds(row, SNAPS, stride=HALF_ROWS), :],
            )
            joined = jnp.concatenate([take(q_ref, row), early, late], axis=0)
            for index, piece in enumerate(pieces(joined, 3)):
                stack[pl.ds(80 * index, 80), pl.ds(LANES * inner, LANES)] = piece
        total[...] += lax.dot_general(
            stack[...], stack[...], (((1,), (1,)), ((), ())), preferred_element_type=F32
        )
        return carry

    lax.fori_loop(0, HALF_ROWS // 8, block, 0)
    down = total[pl.ds(0, 80), :] + total[pl.ds(80, 80), :] + total[pl.ds(160, 80), :]
    gram = down[:, 0:80] + down[:, 80:160] + down[:, 160:240]
    out_ref[pl.ds(0, 32), pl.ds(0, 64)] = gram[0:32, 0:64]
    out_ref[pl.ds(0, 32), pl.ds(64, 64)] = gram[32:64, 0:64]
    out_ref[pl.ds(32, 16), :] = jnp.concatenate([gram[64:80, :], jnp.zeros((16, 48), F32)], axis=1)


def factor_kernel(cells, flags_ref, sums_ref, maps_ref, coeffs_ref):
    totals = sums_ref[0]
    for index in range(1, sums_ref.shape[0]):
        totals = totals + sums_ref[index]
    basis_gram = jnp.concatenate([totals[0:32, 0:64], totals[0:32, 64:128]], axis=0)
    root = math.sqrt(cells)
    coeffs_t = totals[32:48, 0:64] * (1.0 / root)
    snap_gram = totals[32:48, 64:80]
    half = flags_ref[0]
    coeffs_ref[...] = jnp.where(half == 0, coeffs_t[0:8, :], coeffs_t[8:16, :])
    mixed = (2.0 * STEP_SIZE * root) * coeffs_t + (STEP_SIZE * STEP_SIZE) * jnp.dot(
        snap_gram, coeffs_t, precision=HIGHEST, preferred_element_type=F32
    )
    grown = lax.dot_general(
        coeffs_t, mixed, (((0,), (0,)), ((), ())), precision=HIGHEST, preferred_element_type=F32
    )
    gram = (basis_gram + grown) * (1.0 / cells)
    rows = lax.broadcasted_iota(jnp.int32, (EOFS, EOFS), 0)
    columns = lax.broadcasted_iota(jnp.int32, (EOFS, EOFS), 1)
    work = jnp.concatenate([gram, (rows == columns).astype(F32)], axis=1)
    row_index = lax.broadcasted_iota(jnp.int32, (EOFS, LANES), 0)
    scale = jnp.zeros((EOFS, LANES), F32)
    for step in range(EOFS):
        row = work[step : step + 1, :]
        pivot = work[step : step + 1, step : step + 1]
        column = work[:, step : step + 1]
        scaled = row * (1.0 / pivot)
        work = work - jnp.where(row_index > step, column * scaled, 0.0)
        scale = jnp.where(row_index == step, lax.rsqrt(pivot), scale)
    inverse = (work * scale)[:, EOFS:]
    update = lax.dot_general(
        inverse, coeffs_t, (((1,), (1,)), ((), ())), precision=HIGHEST, preferred_element_type=F32
    )
    maps = jnp.concatenate([inverse, STEP_SIZE * update], axis=1)
    high, low = pieces(maps, 2)
    maps_ref[pl.ds(0, EOFS), :] = jnp.concatenate([high, high], axis=1)
    maps_ref[pl.ds(EOFS, EOFS), :] = jnp.concatenate([low, low], axis=1)


FINAL_ROWS = 16


def final_kernel(flags_ref, maps_ref, q_ref, keep_ref, here_ref, send_ref, late_ref, out_ref, stack):
    step = pl.program_id(0)
    per_half = HALF_ROWS // FINAL_ROWS

    def work(mine_ref, other_ref):
        base = lax.rem(step, per_half) * FINAL_ROWS
        for inner in range(FINAL_ROWS):
            at = pl.ds(base + inner, SNAPS, stride=HALF_ROWS)
            early, late = in_order(flags_ref, mine_ref[at, :], other_ref[at, :])
            joined = jnp.concatenate([take(q_ref, inner), early, late], axis=0)
            for index, piece in enumerate(pieces(joined, 2)):
                stack[pl.ds(80 * index, 80), pl.ds(LANES * inner, LANES)] = piece

    @pl.when(step < per_half)
    def _():
        work(keep_ref, here_ref)

    @pl.when(step >= per_half)
    def _():
        work(send_ref, late_ref)

    both = jnp.dot(maps_ref[...], stack[...], preferred_element_type=F32)
    result = both[0:EOFS, :] + both[EOFS:, :]
    for inner in range(FINAL_ROWS):
        put(out_ref, inner, result[:, LANES * inner : LANES * (inner + 1)])


SMEM = pl.BlockSpec(memory_space=pltpu.SMEM)
VMEM = pl.BlockSpec(memory_space=pltpu.VMEM)


def call(kernel, inputs, outputs, scratch=(), flops=1000000, traffic=1000000):
    return pl.pallas_call(
        kernel,
        out_shape=outputs,
        in_specs=inputs,
        out_specs=jax.tree.map(lambda _: VMEM, outputs),
        scratch_shapes=scratch,
        cost_estimate=pl.CostEstimate(flops=flops, bytes_accessed=traffic, transcendentals=0),
    )


def shape(*dims, dtype=F32):
    return jax.ShapeDtypeStruct(dims, dtype)


def neighbours(values_up, values_down, axis, closed):
    count = lax.axis_size(axis)
    ends = count if closed else count - 1
    from_below = lax.ppermute(values_up, axis, [(i, (i + 1) % count) for i in range(ends)])
    from_above = lax.ppermute(values_down, axis, [((i + 1) % count, i) for i in range(ends)])
    return from_below, from_above


def across_tm(values):
    return lax.ppermute(values, "tm", [(0, 1), (1, 0)])


def gathered(values, axes, count):
    return lax.all_to_all(jnp.broadcast_to(values, (count,) + values.shape), axes, 0, 0)


def shards(snapshots, basis):
    lat_count, lon_count = lax.axis_size("lat"), lax.axis_size("lon")
    cells = LEVELS * ROWS * LANES * lat_count * lon_count
    lat = lax.axis_index("lat")
    flags = jnp.stack([lax.axis_index("tm"), (lat == 0).astype(jnp.int32), (lat == lat_count - 1).astype(jnp.int32)]).astype(jnp.int32)
    x = snapshots.reshape(SNAPS * CELL_ROWS, LANES)
    q = basis.reshape(EOFS, CELL_ROWS, LANES)

    packed = call(pack_kernel, [VMEM], shape(64, LANES))(x)
    west, east = neighbours(packed, packed, "lon", True)
    ghosts, low, high = call(edges_kernel, [VMEM] * 3, (shape(64, LANES), shape(256, LANES), shape(256, LANES)))(x, west, east)
    south, north = neighbours(high, low, "lat", False)
    keep, send = call(
        smooth_kernel,
        [SMEM] + [VMEM] * 4,
        (shape(SNAPS * HALF_ROWS, LANES),) * 2,
        [pltpu.VMEM((32 * LEVELS, LANES), F32)] * 2,
    )(flags, x, ghosts, south, north)
    here = across_tm(send)
    late = across_tm(keep)
    partial = pl.pallas_call(
        gram_kernel,
        grid_spec=pltpu.PrefetchScalarGridSpec(
            num_scalar_prefetch=1,
            grid=(1,),
            in_specs=[
                pl.BlockSpec((EOFS, HALF_ROWS, LANES), lambda i, flags: (0, flags[0], 0)),
                pl.BlockSpec((SNAPS * HALF_ROWS, LANES), lambda i, flags: (0, 0)),
                pl.BlockSpec((SNAPS * HALF_ROWS, LANES), lambda i, flags: (0, 0)),
            ],
            out_specs=pl.BlockSpec((PAYLOAD, LANES), lambda i, flags: (0, 0)),
            scratch_shapes=[pltpu.VMEM((240, 1024), BF16), pltpu.VMEM((240, 240), F32)],
        ),
        out_shape=shape(PAYLOAD, LANES),
    )(flags, q, keep, here)
    first = gathered(partial, ("lon", "tm"), lon_count * 2).sum(0)
    second = gathered(first, "lat", lat_count)
    maps, coeffs_t = call(
        functools.partial(factor_kernel, cells), [SMEM, VMEM], (shape(2 * EOFS, 160, dtype=BF16), shape(SNAPS, EOFS))
    )(flags, second)
    per_half = HALF_ROWS // FINAL_ROWS
    whole = pl.BlockSpec((SNAPS * HALF_ROWS, LANES), lambda i, flags: (0, 0))

    def basis_block(i, flags):
        half = jnp.where(i < per_half, flags[0], 1 - flags[0])
        return (0, half * per_half + lax.rem(i, per_half), 0)

    new_basis = pl.pallas_call(
        final_kernel,
        grid_spec=pltpu.PrefetchScalarGridSpec(
            num_scalar_prefetch=1,
            grid=(2 * per_half,),
            in_specs=[
                pl.BlockSpec((2 * EOFS, 160), lambda i, flags: (0, 0)),
                pl.BlockSpec((EOFS, FINAL_ROWS, LANES), basis_block),
                whole,
                whole,
                whole,
                whole,
            ],
            out_specs=pl.BlockSpec((EOFS, FINAL_ROWS, LANES), basis_block),
            scratch_shapes=[pltpu.VMEM((160, FINAL_ROWS * LANES), BF16)],
        ),
        out_shape=shape(EOFS, CELL_ROWS, LANES),
    )(flags, maps, q, keep, here, send, late)
    return (new_basis.reshape(basis.shape), coeffs_t.T)


def solution(mesh):
    placed = (P("tm", None, "lat", "lon"), P(None, None, "lat", "lon"))
    return jax.shard_map(
        shards,
        mesh=mesh,
        in_specs=placed,
        out_specs=(P(None, None, "lat", "lon"), P(None, "tm")),
        check_vma=False,
    )
```

time: 1100 us -> 107 us (0.10); the launches traced: 1080 us -> 106 us
  blocking collectives: 811 us -> 26.7 us
  waiting for transfers between devices: 136 us -> 19.3 us
  Pallas kernels: 0 us -> 35.1 us
  matrix products: 32.8 us -> 0 us
  other arithmetic: 30.9 us -> 0.72 us
  local copies, waits for them, and re-layouts: 29 us -> 4.86 us
  between operations: 14.5 us -> 0.68 us
  starting transfers between devices: 30.2 us -> 18.7 us
    psum x2 -> x0, blocking collectives: 811 us -> none  [the longest x1 541 us: shards(): lax.psum(product(grown, grown.T), ('lon', 'lat')) / total_cells]
    psum x1 -> x0, waiting for transfers between devices: 127 us -> none  [shards(): grown = columns + lax.psum(update_term, 'tm')]
    pallas_call x0 -> x6, Pallas kernels: none -> 35.1 us  [the longest x1 9.97 us: shards(): pl.pallas_call(final_kernel, grid_spec=pltpu.PrefetchScalarGridSpec(num_s...]
    all_to_all x0 -> x1, blocking collectives: none -> 26.7 us  [gathered(): lax.all_to_all(jnp.broadcast_to(values, (count,) + values.shape), axes, 0...]
    dot_general x3 -> x0, matrix products: 24.4 us -> none  [product(): jnp.dot(left, right, precision=lax.Precision.HIGHEST, preferred_element_t...]
    ppermute x12 -> x6, starting transfers between devices: 30.2 us -> 10.8 us  [the longest x2 4.49 us: neighbours(): lax.ppermute(values_down, axis, [((i + 1) % count, i) for i in range(ends)])]
    unnamed x14 -> x16, local copies, waits for them, and re-layouts: 17.2 us -> 3.38 us
    another operation x5 -> x1, other arithmetic: 12.1 us -> 0.65 us  [shards(): jnp.stack([lax.axis_index('tm'), (lat == 0).astype(jnp.int32), (lat == la...]
  transfers between devices with their start and end apart: 13 -> 7, of which waited for: 6 -> 6; matrix products, arithmetic and copies ran while one was open for 1% -> 1% of each run, Pallas kernels for 0% -> 7%
where the time goes in v1:
time: 107 us; the launch traced here: 106 us
  Pallas kernels  35.1 us (33%)
  blocking collectives  26.7 us (25%)
  waiting for transfers between devices  19.3 us (18%)
  starting transfers between devices  18.7 us (17%)
  local copies, waits for them, and re-layouts  4.86 us (5%)
    all_to_all x1, blocking collectives, gathered(): lax.all_to_all(jnp.broadcast_to(values, (count,) + values.shape), axes, 0...  26.7 us
    pallas_call x1, Pallas kernels, shards(): pl.pallas_call(final_kernel, grid_spec=pltpu.PrefetchScalarGridSpec(num_s...  9.97 us
    all_to_all x1, waiting for transfers between devices, gathered(): lax.all_to_all(jnp.broadcast_to(values, (count,) + values.shape), axes, 0...  8.45 us
    all_to_all x1, starting transfers between devices, gathered(): lax.all_to_all(jnp.broadcast_to(values, (count,) + values.shape), axes, 0...  7.94 us
    pallas_call x1, Pallas kernels, shards(): call(functools.partial(factor_kernel, cells), [SMEM, VMEM], (shape(2 * EO...  7.73 us
    pallas_call x1, Pallas kernels, shards(): pl.pallas_call(gram_kernel, grid_spec=pltpu.PrefetchScalarGridSpec(num_sc...  7.43 us
    pallas_call x1, Pallas kernels, shards(): call(smooth_kernel, [SMEM] + [VMEM] * 4, (shape(SNAPS * HALF_ROWS, LANES)...  6.3 us
    ppermute x2, waiting for transfers between devices, neighbours(): lax.ppermute(values_down, axis, [((i + 1) % count, i) for i in range(ends)])  5.14 us
  transfers between devices with their start and end apart: 7, of which 6 were waited for; matrix products, arithmetic and copies ran while one was open for 1% of the time, Pallas kernels for 7%

profile of v1, /device:TPU:1, one launch (start us, length us, event | category | flops | bytes accessed | tf_op | source)
XLA Modules:
  0.0 106.1 jit_solution(6463628799956485216)
XLA Ops:
  0.6 1.9 %shard_map.41 = f32[64,128]{1,0:T(8,128)} custom-call(f32[1024,128]{1,0:T(8,128)} %bitcast.9), custom_call_target="tpu_custom_call" | custom-call | flops 1000000 | bytes 1000000 | tf_op jit(solution)/shard_map/pallas_call | solution.py:280
  2.5 3.2 %collective-permute-start.1 = (f32[64,128]{1,0:T(8,128)}, f32[64,128]{1,0:T(8,128)S(1)}, u32[]{:S(2)}, u32[]{:S(2)}) collective-permute-start(f32[64,128]{1,0:T(8,128)} %shard_map.41), channel_id=1, source_target_pairs={{16,0},{32,16},{48,32},{64,48},{80,64},{96,80},{112,96},{128,112},... | collective-permute-start | bytes 98312 | tf_op jit(solution)/shard_map/ppermute | solution.py:260
  5.7 1.3 %collective-permute-done.1.east_ref = f32[64,128]{1,0:T(8,128)S(1)} collective-permute-done((f32[64,128]{1,0:T(8,128)}, f32[64,128]{1,0:T(8,128)S(1)}, u32[]{:S(2)}, u32[]{:S(2)}) %collective-permute-start.1) | collective-permute-done | bytes 32800 | tf_op jit(solution)/shard_map/ppermute | solution.py:260
  7.0 1.1 %collective-permute-done.west_ref = f32[64,128]{1,0:T(8,128)S(1)} collective-permute-done((f32[64,128]{1,0:T(8,128)}, f32[64,128]{1,0:T(8,128)S(1)}, u32[]{:S(2)}, u32[]{:S(2)}) %collective-permute-start) | collective-permute-done | bytes 32800 | tf_op jit(solution)/shard_map/ppermute | solution.py:259
  8.7 1.8 %shard_map.42 = (f32[64,128]{1,0:T(8,128)}, f32[256,128]{1,0:T(8,128)}, f32[256,128]{1,0:T(8,128)}) custom-call(f32[1024,128]{1,0:T(8,128)} %bitcast.10, f32[64,128]{1,0:T(8,128)} %copy-done.7, f32[64,128]{1,0:T(8,128)} %copy-done.6), custom_call_target="tpu_custom_call" | custom-call | flops 1000000 | bytes 1000000 | tf_op jit(solution)/shard_map/pallas_call | solution.py:282
  10.5 3.5 %collective-permute-start.2 = (f32[256,128]{1,0:T(8,128)}, f32[256,128]{1,0:T(8,128)S(1)}, u32[]{:S(2)}, u32[]{:S(2)}) collective-permute-start(f32[256,128]{1,0:T(8,128)} %get-tuple-element.10), channel_id=1, source_target_pairs={{0,2},{2,4},{4,6},{6,8},{8,10},{10,12},{12,14},{1,3},{3,5},{5,7},{... | collective-permute-start | bytes 393224 | tf_op jit(solution)/shard_map/ppermute | solution.py:259
  14.1 1.3 %collective-permute-start.3 = (f32[256,128]{1,0:T(8,128)}, f32[256,128]{1,0:T(8,128)S(1)}, u32[]{:S(2)}, u32[]{:S(2)}) collective-permute-start(f32[256,128]{1,0:T(8,128)} %get-tuple-element.11), channel_id=1, source_target_pairs={{2,0},{4,2},{6,4},{8,6},{10,8},{12,10},{14,12},{3,1},{5,3},{7,5},{... | collective-permute-start | bytes 393224 | tf_op jit(solution)/shard_map/ppermute | solution.py:260
  15.4 0.7 pad_add_fusion.flags_ref
  16.3 3.9 %collective-permute-done.3.north_ref = f32[256,128]{1,0:T(8,128)S(1)} collective-permute-done((f32[256,128]{1,0:T(8,128)}, f32[256,128]{1,0:T(8,128)S(1)}, u32[]{:S(2)}, u32[]{:S(2)}) %collective-permute-start.3) | collective-permute-done | bytes 131104 | tf_op jit(solution)/shard_map/ppermute | solution.py:260
  20.2 0.7 copy-done.5
  20.8 6.3 %shard_map.43 = (f32[512,128]{1,0:T(8,128)}, f32[512,128]{1,0:T(8,128)}) custom-call(s32[3]{0:T(128)} %pad_add_fusion.flags_ref, f32[1024,128]{1,0:T(8,128)} %bitcast.11, f32[64,128]{1,0:T(8,128)} %get-tuple-element.9.ghosts_ref, f32[256,128]{1,0:T(8,128)} %copy-done.4, f32[256,128]{1,0:T(8,128)} %copy-done.5), custom_call_target="tpu_custom_call" | custom-call | flops 1000000 | bytes 1000000 | tf_op jit(solution)/shard_map/pallas_call | solution.py:284
  27.2 2.6 %collective-permute-start.4 = (f32[512,128]{1,0:T(8,128)}, f32[512,128]{1,0:T(8,128)S(1)}, u32[]{:S(2)}, u32[]{:S(2)}) collective-permute-start(f32[512,128]{1,0:T(8,128)} %get-tuple-element.13.send_ref), channel_id=1, source_target_pairs={{0,1},{1,0},{2,3},{3,2},{4,5},{5,4},{6,7},{7,6},{8,9},{9,8},{10,11... | collective-permute-start | bytes 786440 | tf_op jit(solution)/shard_map/ppermute | solution.py:265
  29.8 4.3 %collective-permute-done.4.other_ref.here_ref = f32[512,128]{1,0:T(8,128)S(1)} collective-permute-done((f32[512,128]{1,0:T(8,128)}, f32[512,128]{1,0:T(8,128)S(1)}, u32[]{:S(2)}, u32[]{:S(2)}) %collective-permute-start.4) | collective-permute-done | bytes 262176 | tf_op jit(solution)/shard_map/ppermute | solution.py:265
  34.1 0.7 copy-done.1
  34.8 7.4 %shard_map.44 = f32[48,128]{1,0:T(8,128)} custom-call(s32[3]{0:T(128)} %pad_add_fusion.flags_ref, f32[64,128,128]{2,1,0:T(8,128)} %bitcast.7, f32[512,128]{1,0:T(8,128)} %get-tuple-element.12.mine_ref.keep_ref, f32[512,128]{1,0:T(8,128)} %copy-done.1), custom_call_target="tpu_custom_call" | custom-call | tf_op jit(solution)/shard_map/pallas_call | solution.py:292
  42.2 0.8 broadcast_in_dim.6
  43.0 26.7 %all_to_all.10 = f32[32,48,128]{2,1,0:T(8,128)S(1)} all-to-all(f32[32,48,128]{2,1,0:T(8,128)S(1)} %broadcast_in_dim.6), channel_id=1, replica_groups=mesh['lon'=16,'lat'=8,'tm'=2] {'lon','tm'}, dimensions={0} | all-to-all | bytes 1572864 | tf_op jit(solution)/shard_map/all_to_all | solution.py:269
  69.7 0.7 broadcast_in_dim.7
  70.4 7.9 %all-to-all-start.1 = ((f32[8,48,128]{2,1,0:T(8,128)}), f32[8,48,128]{2,1,0:T(8,128)S(1)}, u32[]{:S(2)}, u32[]{:S(2)}) async-start(f32[8,48,128]{2,1,0:T(8,128)} %broadcast_in_dim.7), calls=%async_computation.1 | async-start | bytes 393216 | tf_op jit(solution)/shard_map/all_to_all | solution.py:269
  78.5 8.5 %all-to-all-done.1.sums_ref = f32[8,48,128]{2,1,0:T(8,128)S(1)} async-done(((f32[8,48,128]{2,1,0:T(8,128)}), f32[8,48,128]{2,1,0:T(8,128)S(1)}, u32[]{:S(2)}, u32[]{:S(2)}) %all-to-all-start.1) | async-done | bytes 196640 | tf_op jit(solution)/shard_map/all_to_all | solution.py:269
  87.0 0.7 copy-done.2
  87.7 7.7 %shard_map.45 = (bf16[128,160]{1,0:T(8,128)(2,1)}, f32[8,64]{1,0:T(8,128)}) custom-call(s32[3]{0:T(128)} %pad_add_fusion.flags_ref, f32[8,48,128]{2,1,0:T(8,128)} %copy-done.2), custom_call_target="tpu_custom_call" | custom-call | flops 1000000 | bytes 1000000 | tf_op jit(solution)/shard_map/pallas_call | solution.py:309
  95.4 0.7 copy-done.3
  96.1 10.0 %shard_map.46 = f32[64,128,128]{2,1,0:T(8,128)} custom-call(s32[3]{0:T(128)} %pad_add_fusion.flags_ref, bf16[128,160]{1,0:T(8,128)(2,1)} %get-tuple-element.14.maps_ref, f32[64,128,128]{2,1,0:T(8,128)} %bitcast.8, f32[512,128]{1,0:T(8,128)} %get-tuple-element.12.mine_ref.keep_ref, f32[512,128]{1,0:T(8,128)} %copy-done.1, ...), custom_call_target="tpu_custom_call" | custom-call | tf_op jit(solution)/shard_map/pallas_call | solution.py:319
  (17 shorter events, 1.1 us)
Async XLA Ops:
  2.5 4.5 %collective-permute-start.1 = (f32[64,128]{1,0:T(8,128)}, f32[64,128]{1,0:T(8,128)S(1)}, u32[]{:S(2)}, u32[]{:S(2)}) collective-permute-start(f32[64,128]{1,0:T(8,128)} %shard_map.41), channel_id=1, source_target_pairs={{16,0},{32,16},{48,32},{64,48},{80,64},{96,80},{112,96},{128,112},... | collective-permute-start | bytes 98312 | tf_op jit(solution)/shard_map/ppermute | solution.py:260
  5.7 2.4 %collective-permute-start = (f32[64,128]{1,0:T(8,128)}, f32[64,128]{1,0:T(8,128)S(1)}, u32[]{:S(2)}, u32[]{:S(2)}) collective-permute-start(f32[64,128]{1,0:T(8,128)} %shard_map.41), channel_id=1, source_target_pairs={{0,16},{16,32},{32,48},{48,64},{64,80},{80,96},{96,112},{112,128},... | collective-permute-start | bytes 98312 | tf_op jit(solution)/shard_map/ppermute | solution.py:259
  7.0 1.1 %copy-start.6 = (f32[64,128]{1,0:T(8,128)}, f32[64,128]{1,0:T(8,128)S(1)}, u32[]{:S(2)}) copy-start(f32[64,128]{1,0:T(8,128)S(1)} %collective-permute-done.1.east_ref) | copy-start | bytes 98308
  8.1 0.6 copy-start.7
  10.5 5.8 %collective-permute-start.2 = (f32[256,128]{1,0:T(8,128)}, f32[256,128]{1,0:T(8,128)S(1)}, u32[]{:S(2)}, u32[]{:S(2)}) collective-permute-start(f32[256,128]{1,0:T(8,128)} %get-tuple-element.10), channel_id=1, source_target_pairs={{0,2},{2,4},{4,6},{6,8},{8,10},{10,12},{12,14},{1,3},{3,5},{5,7},{... | collective-permute-start | bytes 393224 | tf_op jit(solution)/shard_map/ppermute | solution.py:259
  14.1 6.1 %collective-permute-start.3 = (f32[256,128]{1,0:T(8,128)}, f32[256,128]{1,0:T(8,128)S(1)}, u32[]{:S(2)}, u32[]{:S(2)}) collective-permute-start(f32[256,128]{1,0:T(8,128)} %get-tuple-element.11), channel_id=1, source_target_pairs={{2,0},{4,2},{6,4},{8,6},{10,8},{12,10},{14,12},{3,1},{5,3},{7,5},{... | collective-permute-start | bytes 393224 | tf_op jit(solution)/shard_map/ppermute | solution.py:260
  16.3 3.9 %copy-start.4 = (f32[256,128]{1,0:T(8,128)}, f32[256,128]{1,0:T(8,128)S(1)}, u32[]{:S(2)}) copy-start(f32[256,128]{1,0:T(8,128)S(1)} %collective-permute-done.2.south_ref) | copy-start | bytes 393220
  20.2 0.7 copy-start.5
  27.2 6.9 %collective-permute-start.4 = (f32[512,128]{1,0:T(8,128)}, f32[512,128]{1,0:T(8,128)S(1)}, u32[]{:S(2)}, u32[]{:S(2)}) collective-permute-start(f32[512,128]{1,0:T(8,128)} %get-tuple-element.13.send_ref), channel_id=1, source_target_pairs={{0,1},{1,0},{2,3},{3,2},{4,5},{5,4},{6,7},{7,6},{8,9},{9,8},{10,11... | collective-permute-start | bytes 786440 | tf_op jit(solution)/shard_map/ppermute | solution.py:265
  34.1 0.7 copy-start.1
  34.8 43.6 %copy-start = (f32[512,128]{1,0:T(8,128)S(1)}, f32[512,128]{1,0:T(8,128)}, u32[]{:S(2)}) copy-start(f32[512,128]{1,0:T(8,128)} %get-tuple-element.12.mine_ref.keep_ref) | copy-start | bytes 786436
  70.4 16.6 %all-to-all-start.1 = ((f32[8,48,128]{2,1,0:T(8,128)}), f32[8,48,128]{2,1,0:T(8,128)S(1)}, u32[]{:S(2)}, u32[]{:S(2)}) async-start(f32[8,48,128]{2,1,0:T(8,128)} %broadcast_in_dim.7), calls=%async_computation.1 | async-start | bytes 393216 | tf_op jit(solution)/shard_map/all_to_all | solution.py:269
  78.4 17.0 %collective-permute-start.5 = (f32[512,128]{1,0:T(8,128)S(1)}, f32[512,128]{1,0:T(8,128)S(1)}, u32[]{:S(2)}, u32[]{:S(2)}) collective-permute-start(f32[512,128]{1,0:T(8,128)S(1)} %copy-done), channel_id=1, source_target_pairs={{0,1},{1,0},{2,3},{3,2},{4,5},{5,4},{6,7},{7,6},{8,9},{9,8},{10,11... | collective-permute-start | bytes 786440 | tf_op jit(solution)/shard_map/ppermute | solution.py:265
  87.0 0.7 copy-start.2
  95.4 0.7 copy-start.3

commit v2 on v0

v2 whole, which is shorter than its diff:
```python
import functools
import math

import jax
import jax.numpy as jnp
from jax import lax
from jax.experimental import pallas as pl
from jax.experimental.pallas import tpu as pltpu
from jax.sharding import Mesh, PartitionSpec as P

SMOOTH_RATE = 0.1
STEP_SIZE = 0.25
SNAPS = 8
LEVELS = 8
ROWS = 16
LANES = 128
EOFS = 64
CELL_ROWS = LEVELS * ROWS
HALF_ROWS = CELL_ROWS // 2
HALF_CELLS = HALF_ROWS * LANES
CHUNK = 8
PAYLOAD = 48
LON = ("pair", "core")
F32 = jnp.float32
BF16 = jnp.bfloat16
HIGHEST = lax.Precision.HIGHEST
SMEM = pl.BlockSpec(memory_space=pltpu.SMEM)
VMEM = pl.BlockSpec(memory_space=pltpu.VMEM)


def lanes_of(shape):
    return lax.broadcasted_iota(jnp.int32, shape, len(shape) - 1)


def shape(*dims, dtype=F32):
    return jax.ShapeDtypeStruct(dims, dtype)


def call(kernel, inputs, outputs, scratch=(), flops=1000000, traffic=1000000, megabytes=8):
    return pl.pallas_call(
        kernel,
        out_shape=outputs,
        in_specs=inputs,
        out_specs=jax.tree.map(lambda _: VMEM, outputs),
        scratch_shapes=scratch,
        cost_estimate=pl.CostEstimate(flops=flops, bytes_accessed=traffic, transcendentals=0),
        compiler_params=pltpu.CompilerParams(vmem_limit_bytes=megabytes << 20),
    )


def pack_kernel(x_ref, packed_ref, low_ref, high_ref):
    lane = lanes_of((ROWS, LANES))
    for snap in range(SNAPS):
        packed = jnp.zeros((ROWS, LANES), F32)
        for level in range(LEVELS):
            turned = pltpu.roll(x_ref[snap, level], 16 * level + 3, 1)
            packed = jnp.where((lane >= 16 * level) & (lane < 16 * level + 6), turned, packed)
        packed_ref[pl.ds(ROWS * snap, ROWS), :] = packed
        low = jnp.swapaxes(x_ref[snap, :, pl.ds(0, 8), :], 0, 1)
        high = jnp.swapaxes(x_ref[snap, :, pl.ds(8, 8), :], 0, 1)
        for row in range(3):
            low_ref[row, pl.ds(LEVELS * snap, LEVELS), :] = low[row]
            high_ref[row, pl.ds(LEVELS * snap, LEVELS), :] = high[5 + row]


def seam_kernel(packed_ref, west_ref, east_ref, seam_ref, low_ref, high_ref):
    packed = packed_ref[...]
    lane = lanes_of(packed.shape) % 16
    west = jnp.where(lane < 3, west_ref[...] - packed, 0.0)
    east = pltpu.roll(jnp.where((lane >= 3) & (lane < 6), east_ref[...] - packed, 0.0), 8, 1)
    seam_ref[...] = west + east
    for snap in range(SNAPS):
        low_ref[pl.ds(8 * snap, 8), :] = seam_ref[pl.ds(ROWS * snap, 8), :]
        high_ref[pl.ds(8 * snap, 8), :] = seam_ref[pl.ds(ROWS * snap + 8, 8), :]


def smooth_kernel(
    flags_ref, x_ref, seam_ref, south_ref, north_ref, seam_south_ref, seam_north_ref, keep_ref, send_ref
):
    half = flags_ref[0]
    row = lax.broadcasted_iota(jnp.int32, (8, LANES), 0)
    lane = lanes_of((8, LANES))
    inside = jnp.where(row < 4, 1 - flags_ref[2], 1 - flags_ref[1]) == 1
    zero = jnp.zeros((8, LANES), F32)
    wide_lane = lanes_of((ROWS, LANES))

    def along_rows(field):
        tall = jnp.concatenate(field, axis=0)
        near = pltpu.roll(tall, 1, 0) + pltpu.roll(tall, 23, 0)
        return near[0:8], near[8:16], near[16:24]

    def snapshot(snap, carry):
        edges = jnp.swapaxes(
            jnp.stack(
                [north_ref[i, pl.ds(8 * snap, 8), :] for i in range(3)]
                + [zero, zero]
                + [south_ref[i, pl.ds(8 * snap, 8), :] for i in range(3)]
            ),
            0,
            1,
        )
        fields = [
            (x_ref[snap, level, pl.ds(0, 8), :], x_ref[snap, level, pl.ds(8, 8), :], edges[level])
            for level in range(LEVELS)
        ]
        at = pl.ds(pl.multiple_of(8 * snap, 8), 8)
        seam = (
            seam_ref[pl.ds(pl.multiple_of(ROWS * snap, 8), 8), :],
            seam_ref[pl.ds(pl.multiple_of(ROWS * snap + 8, 8), 8), :],
            jnp.where(row < 4, seam_north_ref[at, :], seam_south_ref[at, :]),
        )
        for sweep in range(3):
            tiles = 3 if sweep < 2 else 2
            fresh_fields = []
            for level in range(LEVELS):
                here = fields[level]
                rows = along_rows(here)
                fresh = []
                for tile in range(tiles):
                    near = rows[tile] + pltpu.roll(here[tile], 1, 1) + pltpu.roll(here[tile], LANES - 1, 1)
                    if level > 0:
                        near = near + fields[level - 1][tile]
                    if level < LEVELS - 1:
                        near = near + fields[level + 1][tile]
                    value = here[tile] + SMOOTH_RATE * (near - 6.0 * here[tile])
                    fresh.append(jnp.where(inside, value, 0.0) if tile == 2 else value)
                fresh_fields.append(tuple(fresh))
            rows = along_rows(seam)
            fresh = []
            for tile in range(tiles):
                here = seam[tile]
                near = rows[tile] + pltpu.roll(here, 1, 1) + pltpu.roll(here, LANES - 1, 1)
                near = near + jnp.where(lane >= 16, pltpu.roll(here, 16, 1), 0.0)
                near = near + jnp.where(lane < LANES - 16, pltpu.roll(here, LANES - 16, 1), 0.0)
                value = here + SMOOTH_RATE * (near - 6.0 * here)
                fresh.append(jnp.where(inside, value, 0.0) if tile == 2 else value)
            fields, seam = fresh_fields, tuple(fresh)
        tall_seam = jnp.concatenate(seam, axis=0)
        for level in range(LEVELS):
            first = pltpu.roll(tall_seam, (LANES - 16 * level - 3) % LANES, 1)
            last = pltpu.roll(tall_seam, (117 - 16 * level) % LANES, 1)
            value = jnp.concatenate(fields[level], axis=0)
            value = value + jnp.where(wide_lane < 3, first, jnp.where(wide_lane >= LANES - 3, last, 0.0))
            to = pl.ds(ROWS * (level % 4), ROWS)
            mine = half == level // 4

            @pl.when(mine)
            def _():
                keep_ref[snap, to, :] = value

            @pl.when(jnp.logical_not(mine))
            def _():
                send_ref[snap, to, :] = value

        return carry

    lax.fori_loop(0, SNAPS, snapshot, 0)


def pieces(values, count):
    out = []
    for index in range(count):
        piece = values.astype(BF16)
        out.append(piece)
        if index < count - 1:
            values = values - piece.astype(F32)
    return out


def transposed_product(left, right):
    return lax.dot_general(left, right, (((1,), (1,)), ((), ())), preferred_element_type=F32)


def basis_gram_kernel(flags_ref, q_ref, stack_ref, gram_ref, total):
    @pl.when(pl.program_id(0) == 0)
    def _():
        total[...] = jnp.zeros_like(total)

    for part in range(q_ref.shape[1] // CHUNK):
        turned = jnp.swapaxes(q_ref[:, pl.ds(CHUNK * part, CHUNK), :], 0, 1)
        for inner in range(CHUNK):
            for index, piece in enumerate(pieces(turned[inner], 3)):
                stack_ref[pl.ds(EOFS * index, EOFS), pl.ds(LANES * (CHUNK * part + inner), LANES)] = piece
    total[...] += transposed_product(stack_ref[...], stack_ref[...])

    @pl.when(pl.program_id(0) == pl.num_programs(0) - 1)
    def _():
        down = total[pl.ds(0, 64), :] + total[pl.ds(64, 64), :] + total[pl.ds(128, 64), :]
        gram_ref[...] = down[:, 0:64] + down[:, 64:128] + down[:, 128:192]


def basis_stack_kernel(flags_ref, q_ref, stack_ref):
    for part in range(q_ref.shape[1] // CHUNK):
        turned = jnp.swapaxes(q_ref[:, pl.ds(CHUNK * part, CHUNK), :], 0, 1)
        for inner in range(CHUNK):
            for index, piece in enumerate(pieces(turned[inner], 2)):
                stack_ref[pl.ds(EOFS * index, EOFS), pl.ds(LANES * (CHUNK * part + inner), LANES)] = piece


def snapshot_columns(flags_ref, mine_ref, other_ref, start, count):
    at = pl.ds(start, CHUNK)
    mine = jnp.swapaxes(mine_ref[:, at, :], 0, 1)
    other = jnp.swapaxes(other_ref[:, at, :], 0, 1)
    first = flags_ref[0] == 0
    early, late = jnp.where(first, mine, other), jnp.where(first, other, mine)
    columns = [jnp.concatenate(pieces(jnp.concatenate([early[i], late[i]], axis=0), count), axis=0) for i in range(CHUNK)]
    return jnp.concatenate(columns, axis=1)


def snapshot_gram_kernel(flags_ref, stack_ref, gram_ref, mine_ref, other_ref, own_ref, partner_ref, cross, square, joined):
    cross[...] = jnp.zeros_like(cross)
    square[...] = jnp.zeros_like(square)

    def block(step, carry):
        columns = snapshot_columns(flags_ref, mine_ref, other_ref, pl.multiple_of(CHUNK * step, CHUNK), 3)
        width = CHUNK * LANES
        stack = stack_ref[:, pl.ds(pl.multiple_of(width * step, width), width)]
        cross[...] += transposed_product(stack, columns)
        square[...] += transposed_product(columns, columns)
        return carry

    lax.fori_loop(0, HALF_ROWS // CHUNK, block, 0)
    down = cross[pl.ds(0, 64), :] + cross[pl.ds(64, 64), :] + cross[pl.ds(128, 64), :]
    projection = down[:, 0:16] + down[:, 16:32] + down[:, 32:48]
    down = square[pl.ds(0, 16), :] + square[pl.ds(16, 16), :] + square[pl.ds(32, 16), :]
    square_sum = down[:, 0:16] + down[:, 16:32] + down[:, 32:48]
    gram = gram_ref[...]
    joined[pl.ds(0, 32), pl.ds(0, 64)] = gram[0:32, :]
    joined[pl.ds(0, 32), pl.ds(64, 64)] = gram[32:64, :]
    joined[pl.ds(32, 16), pl.ds(0, 64)] = jnp.transpose(projection)
    joined[pl.ds(32, 16), pl.ds(64, 64)] = jnp.concatenate([square_sum, jnp.zeros((16, 48), F32)], axis=1)
    side = PAYLOAD // 2
    core = flags_ref[3]
    own_ref[...] = joined[pl.ds(pl.multiple_of(side * core, 8), side), :]
    partner_ref[...] = joined[pl.ds(pl.multiple_of(side * (1 - core), 8), side), :]


def factor_kernel(cells, flags_ref, mine_ref, other_ref, maps_ref, coeffs_ref):
    mine, other = mine_ref[...], other_ref[...]
    first = flags_ref[3] == 0
    totals = jnp.concatenate([jnp.where(first, mine, other), jnp.where(first, other, mine)], axis=0)
    basis_gram = jnp.concatenate([totals[0:32, 0:64], totals[0:32, 64:128]], axis=0)
    root = math.sqrt(cells)
    coeffs_t = totals[32:48, 0:64] * (1.0 / root)
    snap_gram = totals[32:48, 64:80]
    coeffs_ref[...] = jnp.where(flags_ref[0] == 0, coeffs_t[0:8, :], coeffs_t[8:16, :])
    mixed = (2.0 * STEP_SIZE * root) * coeffs_t + (STEP_SIZE * STEP_SIZE) * jnp.dot(
        snap_gram, coeffs_t, precision=HIGHEST, preferred_element_type=F32
    )
    grown = lax.dot_general(
        coeffs_t, mixed, (((0,), (0,)), ((), ())), precision=HIGHEST, preferred_element_type=F32
    )
    gram = (basis_gram + grown) * (1.0 / cells)
    rows = lax.broadcasted_iota(jnp.int32, (EOFS, EOFS), 0)
    columns = lax.broadcasted_iota(jnp.int32, (EOFS, EOFS), 1)
    work = jnp.concatenate([gram, (rows == columns).astype(F32)], axis=1)
    row_index = lax.broadcasted_iota(jnp.int32, (EOFS, LANES), 0)
    scale = jnp.zeros((EOFS, LANES), F32)
    for step in range(EOFS):
        row = work[step : step + 1, :]
        pivot = work[step : step + 1, step : step + 1]
        column = work[:, step : step + 1]
        scaled = row * (1.0 / pivot)
        work = work - jnp.where(row_index > step, column * scaled, 0.0)
        scale = jnp.where(row_index == step, lax.rsqrt(pivot), scale)
    inverse = (work * scale)[:, EOFS:]
    update = lax.dot_general(
        inverse, coeffs_t, (((1,), (1,)), ((), ())), precision=HIGHEST, preferred_element_type=F32
    )
    rows = [
        jnp.concatenate([inverse_part, inverse_part, update_part, update_part], axis=1)
        for inverse_part, update_part in zip(pieces(inverse, 2), pieces(STEP_SIZE * update, 2))
    ]
    maps_ref[...] = jnp.concatenate(rows, axis=0)


FINAL_ROWS = 16
FINAL_STEPS = HALF_ROWS // FINAL_ROWS


def final_kernel(flags_ref, maps_ref, near_ref, far_ref, keep_ref, here_ref, send_ref, late_ref, out_ref):
    step = pl.program_id(0)

    def work(stack_ref, mine_ref, other_ref):
        for part in range(FINAL_ROWS // CHUNK):
            start = pl.multiple_of(lax.rem(step, FINAL_STEPS) * FINAL_ROWS + CHUNK * part, CHUNK)
            columns = snapshot_columns(flags_ref, mine_ref, other_ref, start, 2)
            stack = stack_ref[pl.ds(0, 2 * EOFS), pl.ds(pl.multiple_of(start * LANES, LANES), CHUNK * LANES)]
            both = jnp.dot(maps_ref[...], jnp.concatenate([stack, columns], axis=0), preferred_element_type=F32)
            result = both[0:EOFS, :] + both[EOFS:, :]
            result = jnp.stack([result[:, LANES * i : LANES * (i + 1)] for i in range(CHUNK)])
            out_ref[:, pl.ds(CHUNK * part, CHUNK), :] = jnp.swapaxes(result, 0, 1)

    @pl.when(step < FINAL_STEPS)
    def _():
        work(near_ref, keep_ref, here_ref)

    @pl.when(step >= FINAL_STEPS)
    def _():
        work(far_ref, send_ref, late_ref)


def neighbours(values_up, values_down, axis, closed):
    count = lax.axis_size(axis)
    ends = count if closed else count - 1
    from_below = lax.ppermute(values_up, axis, [(i, (i + 1) % count) for i in range(ends)])
    from_above = lax.ppermute(values_down, axis, [((i + 1) % count, i) for i in range(ends)])
    return from_below, from_above


def across(values, axis):
    return lax.ppermute(values, axis, [(0, 1), (1, 0)])


def gathered(values, axes):
    return lax.all_to_all(jnp.broadcast_to(values, (lax.axis_size(axes),) + values.shape), axes, 0, 0)


QSTEP = 16


def shards(snapshots, basis):
    lat_count = lax.axis_size("lat")
    cells = CELL_ROWS * LANES * lat_count * lax.axis_size(LON)
    lat = lax.axis_index("lat")
    flags = jnp.stack([lax.axis_index("tm"), lat == 0, lat == lat_count - 1, lax.axis_index("core")]).astype(jnp.int32)
    q = basis.reshape(EOFS, CELL_ROWS, LANES)

    packed, low, high = call(
        pack_kernel, [VMEM], (shape(CELL_ROWS, LANES), shape(3, 64, LANES), shape(3, 64, LANES))
    )(snapshots)
    west, east = neighbours(packed, packed, LON, True)
    south, north = neighbours(high, low, "lat", False)
    stack, gram = pl.pallas_call(
        basis_gram_kernel,
        grid_spec=pltpu.PrefetchScalarGridSpec(
            num_scalar_prefetch=1,
            grid=(HALF_ROWS // QSTEP,),
            in_specs=[pl.BlockSpec((EOFS, QSTEP, LANES), lambda i, flags: (0, flags[0] * (HALF_ROWS // QSTEP) + i, 0))],
            out_specs=[
                pl.BlockSpec((3 * EOFS, QSTEP * LANES), lambda i, flags: (0, i)),
                pl.BlockSpec((EOFS, EOFS), lambda i, flags: (0, 0)),
            ],
            scratch_shapes=[pltpu.VMEM((3 * EOFS, 3 * EOFS), F32)],
        ),
        out_shape=(shape(3 * EOFS, HALF_CELLS, dtype=BF16), shape(EOFS, EOFS)),
        cost_estimate=pl.CostEstimate(flops=600000000, bytes_accessed=5 << 20, transcendentals=0),
        compiler_params=pltpu.CompilerParams(vmem_limit_bytes=8 << 20),
    )(flags, q)
    seam, seam_low, seam_high = call(
        seam_kernel, [VMEM] * 3, (shape(CELL_ROWS, LANES), shape(64, LANES), shape(64, LANES))
    )(packed, west, east)
    seam_south, seam_north = neighbours(seam_high, seam_low, "lat", False)
    keep, send = call(
        smooth_kernel, [SMEM] + [VMEM] * 6, (shape(SNAPS, HALF_ROWS, LANES),) * 2
    )(flags, snapshots, seam, south, north, seam_south, seam_north)
    here = across(send, "tm")
    side = shape(PAYLOAD // 2, LANES)
    mine, theirs = call(
        snapshot_gram_kernel,
        [SMEM] + [VMEM] * 4,
        (side, side),
        [pltpu.VMEM((192, 48), F32), pltpu.VMEM((48, 48), F32), pltpu.VMEM((PAYLOAD, LANES), F32)],
    )(flags, stack, gram, keep, here)
    mine = mine + across(theirs, "core")
    mine = gathered(mine, ("pair", "tm")).sum(0)
    far = pl.pallas_call(
        basis_stack_kernel,
        grid_spec=pltpu.PrefetchScalarGridSpec(
            num_scalar_prefetch=1,
            grid=(HALF_ROWS // QSTEP,),
            in_specs=[
                pl.BlockSpec((EOFS, QSTEP, LANES), lambda i, flags: (0, (1 - flags[0]) * (HALF_ROWS // QSTEP) + i, 0))
            ],
            out_specs=pl.BlockSpec((2 * EOFS, QSTEP * LANES), lambda i, flags: (0, i)),
        ),
        out_shape=shape(2 * EOFS, HALF_CELLS, dtype=BF16),
        cost_estimate=pl.CostEstimate(flops=1000000, bytes_accessed=4 << 20, transcendentals=0),
        compiler_params=pltpu.CompilerParams(vmem_limit_bytes=8 << 20),
    )(flags, q)
    late = across(keep, "tm")
    mine = gathered(mine, "lat").sum(0)
    other = across(mine, "core")
    maps, coeffs_t = call(
        functools.partial(factor_kernel, cells),
        [SMEM, VMEM, VMEM],
        (shape(2 * EOFS, 160, dtype=BF16), shape(SNAPS, EOFS)),
    )(flags, mine, other)

    def basis_block(i, flags):
        half = jnp.where(i < FINAL_STEPS, flags[0], 1 - flags[0])
        return (0, half * FINAL_STEPS + lax.rem(i, FINAL_STEPS), 0)

    new_basis = pl.pallas_call(
        final_kernel,
        grid_spec=pltpu.PrefetchScalarGridSpec(
            num_scalar_prefetch=1,
            grid=(2 * FINAL_STEPS,),
            in_specs=[VMEM] * 7,
            out_specs=pl.BlockSpec((EOFS, FINAL_ROWS, LANES), basis_block),
        ),
        out_shape=shape(EOFS, CELL_ROWS, LANES),
        compiler_params=pltpu.CompilerParams(vmem_limit_bytes=8 << 20),
    )(flags, maps, stack, far, keep, here, send, late)
    return (new_basis.reshape(basis.shape), coeffs_t.T)


def solution(mesh):
    pairs = mesh.shape["lon"] // 2
    split = Mesh(mesh.devices.reshape(pairs, 2, *mesh.devices.shape[1:]), LON + tuple(mesh.axis_names[1:]))
    fields = P(None, None, "lat", LON)
    return jax.shard_map(
        shards,
        mesh=split,
        in_specs=(P("tm", None, "lat", LON), fields),
        out_specs=(fields, P(None, "tm")),
        check_vma=False,
    )
```

time: 1100 us -> 96.3 us (0.09); the launches traced: 1080 us -> 95.8 us
  blocking collectives: 811 us -> 16.8 us
  waiting for transfers between devices: 136 us -> 9.18 us
  matrix products: 32.8 us -> 0 us
  other arithmetic: 30.9 us -> 1.05 us
  Pallas kernels: 0 us -> 29 us
  local copies, waits for them, and re-layouts: 29 us -> 7.89 us
  between operations: 14.5 us -> 0.8 us
    psum x2 -> x0, blocking collectives: 811 us -> none  [the longest x1 541 us: shards(): lax.psum(product(grown, grown.T), ('lon', 'lat')) / total_cells]
    psum x1 -> x0, waiting for transfers between devices: 127 us -> none  [shards(): grown = columns + lax.psum(update_term, 'tm')]
    pallas_call x0 -> x8, Pallas kernels: none -> 29 us  [the longest x1 7.2 us: shards(): call(smooth_kernel, [SMEM] + [VMEM] * 6, (shape(SNAPS, HALF_ROWS, LANES),...]
    dot_general x3 -> x0, matrix products: 24.4 us -> none  [product(): jnp.dot(left, right, precision=lax.Precision.HIGHEST, preferred_element_t...]
    all_to_all x0 -> x1, blocking collectives: none -> 16.8 us  [gathered(): lax.all_to_all(jnp.broadcast_to(values, (lax.axis_size(axes),) + values.s...]
    another operation x5 -> x1, other arithmetic: 12.1 us -> 0.08 us  [shards(): jnp.stack([lax.axis_index('tm'), lat == 0, lat == lat_count - 1, lax.axis...]
    ppermute x12 -> x10, starting transfers between devices: 30.2 us -> 25.5 us  [the longest x4 12.4 us: across(): return lax.ppermute(values, axis, [(0, 1), (1, 0)])]
  transfers between devices with their start and end apart: 13 -> 11, of which waited for: 6 -> 3; matrix products, arithmetic and copies ran while one was open for 1% -> 1% of each run, Pallas kernels for 0% -> 13%
where the time goes in v2:
time: 96.3 us; the launch traced here: 95.8 us
  starting transfers between devices  31.1 us (32%)
  Pallas kernels  29 us (30%)
  blocking collectives  16.8 us (17%)
  waiting for transfers between devices  9.18 us (10%)
  local copies, waits for them, and re-layouts  7.89 us (8%)
  other arithmetic  1.05 us (1%)
    all_to_all x1, blocking collectives, gathered(): lax.all_to_all(jnp.broadcast_to(values, (lax.axis_size(axes),) + values.s...  16.8 us
    ppermute x4, starting transfers between devices, across(): return lax.ppermute(values, axis, [(0, 1), (1, 0)])  12.4 us
    ppermute x3, starting transfers between devices, neighbours(): lax.ppermute(values_up, axis, [(i, (i + 1) % count) for i in range(ends)])  7.27 us
    pallas_call x1, Pallas kernels, shards(): call(smooth_kernel, [SMEM] + [VMEM] * 6, (shape(SNAPS, HALF_ROWS, LANES),...  7.2 us
    unnamed x16, local copies, waits for them, and re-layouts  7.18 us
    pallas_call x1, Pallas kernels, shards(): call(functools.partial(factor_kernel, cells), [SMEM, VMEM, VMEM], (shape(...  7.16 us
    pallas_call x1, Pallas kernels, shards(): pl.pallas_call(final_kernel, grid_spec=pltpu.PrefetchScalarGridSpec(num_s...  6.37 us
    ppermute x3, starting transfers between devices, neighbours(): lax.ppermute(values_down, axis, [((i + 1) % count, i) for i in range(ends)])  5.86 us
  transfers between devices with their start and end apart: 11, of which 3 were waited for; matrix products, arithmetic and copies ran while one was open for 1% of the time, Pallas kernels for 13%

profile of v2, /device:TPU:1, one launch (start us, length us, event | category | flops | bytes accessed | tf_op | source)
XLA Modules:
  0.0 95.8 jit_solution(458172644704994228)
XLA Ops:
  0.6 1.0 %copy-done.2 = f32[8,8,16,128]{3,2,1,0:T(8,128)S(1)} copy-done((f32[8,8,16,128]{3,2,1,0:T(8,128)S(1)}, f32[8,8,16,128]{3,2,1,0:T(8,128)}, u32[]{:S(2)}) %copy-start.2) | copy-done | bytes 524312
  1.9 3.3 %collective-permute-start.1 = (f32[128,128]{1,0:T(8,128)S(1)}, f32[128,128]{1,0:T(8,128)S(1)}, u32[]{:S(2)}, u32[]{:S(2)}) collective-permute-start(f32[128,128]{1,0:T(8,128)S(1)} %get-tuple-element.18.packed_ref), channel_id=1, source_target_pairs={{16,0},{32,16},{48,32},{64,48},{80,64},{96,80},{112,96},{128,112},... | collective-permute-start | bytes 196616 | tf_op jit(solution)/shard_map/ppermute | solution.py:307
  5.2 3.1 %collective-permute-start.2 = (f32[3,64,128]{2,1,0:T(8,128)S(1)}, f32[3,64,128]{2,1,0:T(8,128)S(1)}, u32[]{:S(2)}, u32[]{:S(2)}) collective-permute-start(f32[3,64,128]{2,1,0:T(8,128)S(1)} %get-tuple-element.20), channel_id=1, source_target_pairs={{0,2},{2,4},{4,6},{6,8},{8,10},{10,12},{12,14},{1,3},{3,5},{5,7},{... | collective-permute-start | bytes 294920 | tf_op jit(solution)/shard_map/ppermute | solution.py:306
  8.3 1.3 %collective-permute-start.3 = (f32[3,64,128]{2,1,0:T(8,128)S(1)}, f32[3,64,128]{2,1,0:T(8,128)S(1)}, u32[]{:S(2)}, u32[]{:S(2)}) collective-permute-start(f32[3,64,128]{2,1,0:T(8,128)S(1)} %get-tuple-element.21), channel_id=1, source_target_pairs={{2,0},{4,2},{6,4},{8,6},{10,8},{12,10},{14,12},{3,1},{5,3},{7,5},{... | collective-permute-start | bytes 294920 | tf_op jit(solution)/shard_map/ppermute | solution.py:307
  9.7 4.2 %collective-permute-start.4 = (f32[64,128]{1,0:T(8,128)S(1)}, f32[64,128]{1,0:T(8,128)S(1)}, u32[]{:S(2)}, u32[]{:S(2)}) collective-permute-start(f32[64,128]{1,0:T(8,128)S(1)} %get-tuple-element.22), channel_id=1, source_target_pairs={{0,2},{2,4},{4,6},{6,8},{8,10},{10,12},{12,14},{1,3},{3,5},{5,7},{... | collective-permute-start | bytes 98312 | tf_op jit(solution)/shard_map/ppermute | solution.py:306
  13.9 1.3 %collective-permute-start.5 = (f32[64,128]{1,0:T(8,128)S(1)}, f32[64,128]{1,0:T(8,128)S(1)}, u32[]{:S(2)}, u32[]{:S(2)}) collective-permute-start(f32[64,128]{1,0:T(8,128)S(1)} %get-tuple-element.23), channel_id=1, source_target_pairs={{2,0},{4,2},{6,4},{8,6},{10,8},{12,10},{14,12},{3,1},{5,3},{7,5},{... | collective-permute-start | bytes 98312 | tf_op jit(solution)/shard_map/ppermute | solution.py:307
  15.3 3.5 %collective-permute-done.5.seam_north_ref = f32[64,128]{1,0:T(8,128)S(1)} collective-permute-done((f32[64,128]{1,0:T(8,128)S(1)}, f32[64,128]{1,0:T(8,128)S(1)}, u32[]{:S(2)}, u32[]{:S(2)}) %collective-permute-start.5) | collective-permute-done | bytes 32800 | tf_op jit(solution)/shard_map/ppermute | solution.py:307
  18.7 1.0 %copy-done.3 = f32[8,8,16,128]{3,2,1,0:T(8,128)S(1)} copy-done((f32[8,8,16,128]{3,2,1,0:T(8,128)S(1)}, f32[8,8,16,128]{3,2,1,0:T(8,128)}, u32[]{:S(2)}) %copy-start.3) | copy-done | bytes 524312
  19.8 7.2 %shard_map.44 = (f32[8,64,128]{2,1,0:T(8,128)S(1)}, f32[8,64,128]{2,1,0:T(8,128)S(1)}) custom-call(s32[4]{0:T(128)S(1)} %pad_add_fusion.flags_ref, f32[8,8,16,128]{3,2,1,0:T(8,128)S(1)} %copy-done.3, f32[128,128]{1,0:T(8,128)S(1)} %get-tuple-element.19.seam_ref, f32[3,64,128]{2,1,0:T(8,128)S(1)} %collective-permute-done.2.south_ref, ...), custom_call_target="tpu_custom_call" | custom-call | flops 1000000 | bytes 1000000 | tf_op jit(solution)/shard_map/pallas_call | solution.py:354
  27.0 2.8 %collective-permute-start.6 = (f32[8,64,128]{2,1,0:T(8,128)S(1)}, f32[8,64,128]{2,1,0:T(8,128)S(1)}, u32[]{:S(2)}, u32[]{:S(2)}) collective-permute-start(f32[8,64,128]{2,1,0:T(8,128)S(1)} %get-tuple-element.25.send_ref), channel_id=1, source_target_pairs={{0,1},{1,0},{2,3},{3,2},{4,5},{5,4},{6,7},{7,6},{8,9},{9,8},{10,11... | collective-permute-start | bytes 786440 | tf_op jit(solution)/shard_map/ppermute | solution.py:312
  29.7 2.2 %copy-done = f32[64,8,16,128]{3,2,1,0:T(8,128)S(1)} copy-done((f32[64,8,16,128]{3,2,1,0:T(8,128)S(1)}, f32[64,8,16,128]{3,2,1,0:T(8,128)}, u32[]{:S(2)}) %copy-start) | copy-done | bytes 4194328
  31.9 3.3 %shard_map.41 = (bf16[192,8192]{1,0:T(8,128)(2,1)S(1)}, f32[64,64]{1,0:T(8,128)S(1)}) custom-call(s32[4]{0:T(128)S(1)} %pad_add_fusion.flags_ref, f32[64,128,128]{2,1,0:T(8,128)S(1)} %bitcast.7), custom_call_target="tpu_custom_call" | custom-call | flops 600000000 | bytes 5242880 | tf_op jit(solution)/shard_map/pallas_call | solution.py:334
  35.3 2.9 %shard_map.45 = (f32[24,128]{1,0:T(8,128)S(1)}, f32[24,128]{1,0:T(8,128)S(1)}) custom-call(s32[4]{0:T(128)S(1)} %pad_add_fusion.flags_ref, bf16[192,8192]{1,0:T(8,128)(2,1)S(1)} %get-tuple-element.16.stack_ref.near_ref, f32[64,64]{1,0:T(8,128)S(1)} %get-tuple-element.17.gram_ref, f32[8,64,128]{2,1,0:T(8,128)S(1)} %get-tuple-element.24.mine_ref.keep_ref, ...), custom_call_target="tpu_custom_call" | custom-call | flops 1000000 | bytes 1000000 | tf_op jit(solution)/shard_map/pallas_call | solution.py:359
  39.0 3.8 %collective-permute-start.7 = (f32[24,128]{1,0:T(8,128)S(1)}, f32[24,128]{1,0:T(8,128)S(1)}, u32[]{:S(2)}, u32[]{:S(2)}) collective-permute-start(f32[24,128]{1,0:T(8,128)S(1)} %get-tuple-element.27), channel_id=1, source_target_pairs={{0,16},{16,0},{1,17},{17,1},{2,18},{18,2},{3,19},{19,3},{4,20},{20... | collective-permute-start | bytes 36872 | tf_op jit(solution)/shard_map/ppermute | solution.py:312
  44.3 5.5 %all-to-all-start = ((f32[16,24,128]{2,1,0:T(8,128)}), f32[16,24,128]{2,1,0:T(8,128)}, u32[]{:S(2)}, u32[]{:S(2)}) async-start(f32[16,24,128]{2,1,0:T(8,128)} %broadcast_in_dim.6), calls=%async_computation | async-start | bytes 393216 | tf_op jit(solution)/shard_map/all_to_all | solution.py:316
  49.8 2.8 %collective-permute-start.9 = (f32[8,64,128]{2,1,0:T(8,128)S(1)}, f32[8,64,128]{2,1,0:T(8,128)}, u32[]{:S(2)}, u32[]{:S(2)}) collective-permute-start(f32[8,64,128]{2,1,0:T(8,128)S(1)} %get-tuple-element.24.mine_ref.keep_ref), channel_id=1, source_target_pairs={{0,1},{1,0},{2,3},{3,2},{4,5},{5,4},{6,7},{7,6},{8,9},{9,8},{10,11... | collective-permute-start | bytes 786440 | tf_op jit(solution)/shard_map/ppermute | solution.py:312
  52.6 4.9 %all-to-all-done = f32[16,24,128]{2,1,0:T(8,128)} async-done(((f32[16,24,128]{2,1,0:T(8,128)}), f32[16,24,128]{2,1,0:T(8,128)}, u32[]{:S(2)}, u32[]{:S(2)}) %all-to-all-start) | async-done | bytes 196640 | tf_op jit(solution)/shard_map/all_to_all | solution.py:316
  57.5 0.9 reduce_sum.18
  58.5 16.8 %all_to_all.10 = f32[8,24,128]{2,1,0:T(8,128)S(1)} all-to-all(f32[8,24,128]{2,1,0:T(8,128)S(1)} %broadcast_in_dim.7), channel_id=1, replica_groups=mesh['pair'=8,'core'=2,'lat'=8,'tm'=2] {'lat'}, dimensions={0} | all-to-all | bytes 196608 | tf_op jit(solution)/shard_map/all_to_all | solution.py:316
  75.3 3.1 %collective-permute-start.8 = (f32[24,128]{1,0:T(8,128)S(1)}, f32[24,128]{1,0:T(8,128)S(1)}, u32[]{:S(2)}, u32[]{:S(2)}) collective-permute-start(f32[24,128]{1,0:T(8,128)S(1)} %reduce_sum.19.mine_ref), channel_id=1, source_target_pairs={{0,16},{16,0},{1,17},{17,1},{2,18},{18,2},{3,19},{19,3},{4,20},{20... | collective-permute-start | bytes 36872 | tf_op jit(solution)/shard_map/ppermute | solution.py:312
  78.3 2.2 %copy-done.1 = f32[64,8,16,128]{3,2,1,0:T(8,128)S(1)} copy-done((f32[64,8,16,128]{3,2,1,0:T(8,128)S(1)}, f32[64,8,16,128]{3,2,1,0:T(8,128)}, u32[]{:S(2)}) %copy-start.1) | copy-done | bytes 4194328
  80.5 1.7 %shard_map.47.far_ref = bf16[128,8192]{1,0:T(8,128)(2,1)S(1)} custom-call(s32[4]{0:T(128)S(1)} %pad_add_fusion.flags_ref, f32[64,128,128]{2,1,0:T(8,128)S(1)} %bitcast.8), custom_call_target="tpu_custom_call" | custom-call | flops 1000000 | bytes 4194304 | tf_op jit(solution)/shard_map/pallas_call | solution.py:367
  82.2 7.2 %shard_map.46 = (bf16[128,160]{1,0:T(8,128)(2,1)S(1)}, f32[8,64]{1,0:T(8,128)}) custom-call(s32[4]{0:T(128)S(1)} %pad_add_fusion.flags_ref, f32[24,128]{1,0:T(8,128)S(1)} %reduce_sum.19.mine_ref, f32[24,128]{1,0:T(8,128)S(1)} %collective-permute-done.8.other_ref), custom_call_target="tpu_custom_call" | custom-call | flops 1000000 | bytes 1000000 | tf_op jit(solution)/shard_map/pallas_call | solution.py:384
  89.4 6.4 %shard_map.48 = f32[64,128,128]{2,1,0:T(8,128)} custom-call(s32[4]{0:T(128)S(1)} %pad_add_fusion.flags_ref, bf16[128,160]{1,0:T(8,128)(2,1)S(1)} %get-tuple-element.28.maps_ref, bf16[192,8192]{1,0:T(8,128)(2,1)S(1)} %get-tuple-element.16.stack_ref.near_ref, bf16[128,8192]{1,0:T(8,128)(2,1)S(1)} %shard_map.47.far_ref, ...), custom_call_target="tpu_custom_call" | custom-call | tf_op jit(solution)/shard_map/pallas_call | solution.py:394
  (29 shorter events, 2.7 us)
Async XLA Ops:
  0.6 1.0 %copy-start.2 = (f32[8,8,16,128]{3,2,1,0:T(8,128)S(1)}, f32[8,8,16,128]{3,2,1,0:T(8,128)}, u32[]{:S(2)}) copy-start(f32[8,8,16,128]{3,2,1,0:T(8,128)} %x_ref.3) | copy-start | bytes 1572868
  1.9 7.7 %collective-permute-start.1 = (f32[128,128]{1,0:T(8,128)S(1)}, f32[128,128]{1,0:T(8,128)S(1)}, u32[]{:S(2)}, u32[]{:S(2)}) collective-permute-start(f32[128,128]{1,0:T(8,128)S(1)} %get-tuple-element.18.packed_ref), channel_id=1, source_target_pairs={{16,0},{32,16},{48,32},{64,48},{80,64},{96,80},{112,96},{128,112},... | collective-permute-start | bytes 196616 | tf_op jit(solution)/shard_map/ppermute | solution.py:307
  5.2 4.4 %collective-permute-start = (f32[128,128]{1,0:T(8,128)S(1)}, f32[128,128]{1,0:T(8,128)S(1)}, u32[]{:S(2)}, u32[]{:S(2)}) collective-permute-start(f32[128,128]{1,0:T(8,128)S(1)} %get-tuple-element.18.packed_ref), channel_id=1, source_target_pairs={{0,16},{16,32},{32,48},{48,64},{64,80},{80,96},{96,112},{112,128},... | collective-permute-start | bytes 196616 | tf_op jit(solution)/shard_map/ppermute | solution.py:306
  5.2 13.6 %collective-permute-start.2 = (f32[3,64,128]{2,1,0:T(8,128)S(1)}, f32[3,64,128]{2,1,0:T(8,128)S(1)}, u32[]{:S(2)}, u32[]{:S(2)}) collective-permute-start(f32[3,64,128]{2,1,0:T(8,128)S(1)} %get-tuple-element.20), channel_id=1, source_target_pairs={{0,2},{2,4},{4,6},{6,8},{8,10},{10,12},{12,14},{1,3},{3,5},{5,7},{... | collective-permute-start | bytes 294920 | tf_op jit(solution)/shard_map/ppermute | solution.py:306
  8.3 10.5 %collective-permute-start.3 = (f32[3,64,128]{2,1,0:T(8,128)S(1)}, f32[3,64,128]{2,1,0:T(8,128)S(1)}, u32[]{:S(2)}, u32[]{:S(2)}) collective-permute-start(f32[3,64,128]{2,1,0:T(8,128)S(1)} %get-tuple-element.21), channel_id=1, source_target_pairs={{2,0},{4,2},{6,4},{8,6},{10,8},{12,10},{14,12},{3,1},{5,3},{7,5},{... | collective-permute-start | bytes 294920 | tf_op jit(solution)/shard_map/ppermute | solution.py:307
  9.7 5.6 %collective-permute-start.4 = (f32[64,128]{1,0:T(8,128)S(1)}, f32[64,128]{1,0:T(8,128)S(1)}, u32[]{:S(2)}, u32[]{:S(2)}) collective-permute-start(f32[64,128]{1,0:T(8,128)S(1)} %get-tuple-element.22), channel_id=1, source_target_pairs={{0,2},{2,4},{4,6},{6,8},{8,10},{10,12},{12,14},{1,3},{3,5},{5,7},{... | collective-permute-start | bytes 98312 | tf_op jit(solution)/shard_map/ppermute | solution.py:306
  13.9 4.8 %collective-permute-start.5 = (f32[64,128]{1,0:T(8,128)S(1)}, f32[64,128]{1,0:T(8,128)S(1)}, u32[]{:S(2)}, u32[]{:S(2)}) collective-permute-start(f32[64,128]{1,0:T(8,128)S(1)} %get-tuple-element.23), channel_id=1, source_target_pairs={{2,0},{4,2},{6,4},{8,6},{10,8},{12,10},{14,12},{3,1},{5,3},{7,5},{... | collective-permute-start | bytes 98312 | tf_op jit(solution)/shard_map/ppermute | solution.py:307
  18.7 1.0 %copy-start.3 = (f32[8,8,16,128]{3,2,1,0:T(8,128)S(1)}, f32[8,8,16,128]{3,2,1,0:T(8,128)}, u32[]{:S(2)}) copy-start(f32[8,8,16,128]{3,2,1,0:T(8,128)} %x_ref.3) | copy-start | bytes 1572868
  27.0 11.3 %copy-start.6 = (f32[8,64,128]{2,1,0:T(8,128)}, f32[8,64,128]{2,1,0:T(8,128)S(1)}, u32[]{:S(2)}) copy-start(f32[8,64,128]{2,1,0:T(8,128)S(1)} %get-tuple-element.25.send_ref) | copy-start | bytes 786436
  27.0 8.3 %collective-permute-start.6 = (f32[8,64,128]{2,1,0:T(8,128)S(1)}, f32[8,64,128]{2,1,0:T(8,128)S(1)}, u32[]{:S(2)}, u32[]{:S(2)}) collective-permute-start(f32[8,64,128]{2,1,0:T(8,128)S(1)} %get-tuple-element.25.send_ref), channel_id=1, source_target_pairs={{0,1},{1,0},{2,3},{3,2},{4,5},{5,4},{6,7},{7,6},{8,9},{9,8},{10,11... | collective-permute-start | bytes 786440 | tf_op jit(solution)/shard_map/ppermute | solution.py:312
  29.7 2.2 %copy-start = (f32[64,8,16,128]{3,2,1,0:T(8,128)S(1)}, f32[64,8,16,128]{3,2,1,0:T(8,128)}, u32[]{:S(2)}) copy-start(f32[64,8,16,128]{3,2,1,0:T(8,128)} %param.3) | copy-start | bytes 12582916
  38.2 0.7 copy-start.4
  39.0 4.6 %collective-permute-start.7 = (f32[24,128]{1,0:T(8,128)S(1)}, f32[24,128]{1,0:T(8,128)S(1)}, u32[]{:S(2)}, u32[]{:S(2)}) collective-permute-start(f32[24,128]{1,0:T(8,128)S(1)} %get-tuple-element.27), channel_id=1, source_target_pairs={{0,16},{16,0},{1,17},{17,1},{2,18},{18,2},{3,19},{19,3},{4,20},{20... | collective-permute-start | bytes 36872 | tf_op jit(solution)/shard_map/ppermute | solution.py:312
  44.3 13.2 %all-to-all-start = ((f32[16,24,128]{2,1,0:T(8,128)}), f32[16,24,128]{2,1,0:T(8,128)}, u32[]{:S(2)}, u32[]{:S(2)}) async-start(f32[16,24,128]{2,1,0:T(8,128)} %broadcast_in_dim.6), calls=%async_computation | async-start | bytes 393216 | tf_op jit(solution)/shard_map/all_to_all | solution.py:316
  49.8 39.6 %collective-permute-start.9 = (f32[8,64,128]{2,1,0:T(8,128)S(1)}, f32[8,64,128]{2,1,0:T(8,128)}, u32[]{:S(2)}, u32[]{:S(2)}) collective-permute-start(f32[8,64,128]{2,1,0:T(8,128)S(1)} %get-tuple-element.24.mine_ref.keep_ref), channel_id=1, source_target_pairs={{0,1},{1,0},{2,3},{3,2},{4,5},{5,4},{6,7},{7,6},{8,9},{9,8},{10,11... | collective-permute-start | bytes 786440 | tf_op jit(solution)/shard_map/ppermute | solution.py:312
  75.3 7.0 %collective-permute-start.8 = (f32[24,128]{1,0:T(8,128)S(1)}, f32[24,128]{1,0:T(8,128)S(1)}, u32[]{:S(2)}, u32[]{:S(2)}) collective-permute-start(f32[24,128]{1,0:T(8,128)S(1)} %reduce_sum.19.mine_ref), channel_id=1, source_target_pairs={{0,16},{16,0},{1,17},{17,1},{2,18},{18,2},{3,19},{19,3},{4,20},{20... | collective-permute-start | bytes 36872 | tf_op jit(solution)/shard_map/ppermute | solution.py:312
  78.3 2.2 %copy-start.1 = (f32[64,8,16,128]{3,2,1,0:T(8,128)S(1)}, f32[64,8,16,128]{3,2,1,0:T(8,128)}, u32[]{:S(2)}) copy-start(f32[64,8,16,128]{3,2,1,0:T(8,128)} %param.3) | copy-start | bytes 12582916
  80.5 8.9 %copy-start.5 = (f32[8,64,128]{2,1,0:T(8,128)S(1)}, f32[8,64,128]{2,1,0:T(8,128)}, u32[]{:S(2)}) copy-start(f32[8,64,128]{2,1,0:T(8,128)} %copy-done.4) | copy-start | bytes 786436
  80.5 8.9 %copy-start.7 = (f32[8,64,128]{2,1,0:T(8,128)S(1)}, f32[8,64,128]{2,1,0:T(8,128)}, u32[]{:S(2)}) copy-start(f32[8,64,128]{2,1,0:T(8,128)} %copy-done.6) | copy-start | bytes 786436

commit v3 on v2

v3 whole, which is shorter than its diff:
```python
import functools
import math

import jax
import jax.numpy as jnp
from jax import lax
from jax.experimental import pallas as pl
from jax.experimental.pallas import tpu as pltpu
from jax.sharding import Mesh, PartitionSpec as P

SMOOTH_RATE = 0.1
STEP_SIZE = 0.25
SNAPS = 8
LEVELS = 8
ROWS = 16
LANES = 128
EOFS = 64
CELL_ROWS = LEVELS * ROWS
HALF_ROWS = CELL_ROWS // 2
HALF_CELLS = HALF_ROWS * LANES
CHUNK = 8
PAYLOAD = 48
SIDE = PAYLOAD // 2
QROWS = 16
FINAL_ROWS = 16
LON = ("pair", "core")
F32 = jnp.float32
BF16 = jnp.bfloat16
HIGHEST = lax.Precision.HIGHEST
VMEM = pl.BlockSpec(memory_space=pltpu.VMEM)
ANY = pl.BlockSpec(memory_space=pl.ANY)


def lanes_of(shape):
    return lax.broadcasted_iota(jnp.int32, shape, len(shape) - 1)


def shape(*dims, dtype=F32):
    return jax.ShapeDtypeStruct(dims, dtype)


def call(kernel, inputs, outputs, scratch=(), flops=1000000, traffic=1000000, megabytes=8):
    return pl.pallas_call(
        kernel,
        out_shape=outputs,
        in_specs=inputs,
        out_specs=jax.tree.map(lambda _: VMEM, outputs),
        scratch_shapes=scratch,
        cost_estimate=pl.CostEstimate(flops=flops, bytes_accessed=traffic, transcendentals=0),
        compiler_params=pltpu.CompilerParams(vmem_limit_bytes=megabytes << 20),
    )


def pack_kernel(x_ref, packed_ref):
    lane = lanes_of((ROWS, LANES))
    for snap in range(SNAPS):
        packed = jnp.zeros((ROWS, LANES), F32)
        for level in range(LEVELS):
            turned = pltpu.roll(x_ref[snap, level], 16 * level + 3, 1)
            packed = jnp.where((lane >= 16 * level) & (lane < 16 * level + 6), turned, packed)
        packed_ref[pl.ds(ROWS * snap, ROWS), :] = packed


def seam_kernel(x_ref, packed_ref, west_ref, east_ref, seam_ref, low_ref, high_ref):
    packed = packed_ref[...]
    lane = lanes_of(packed.shape) % 16
    west = jnp.where(lane < 3, west_ref[...] - packed, 0.0)
    east = pltpu.roll(jnp.where((lane >= 3) & (lane < 6), east_ref[...] - packed, 0.0), 8, 1)
    seam_ref[...] = west + east
    for snap in range(SNAPS):
        at = pl.ds(8 * snap, 8)
        low = jnp.swapaxes(x_ref[snap, :, pl.ds(0, 8), :], 0, 1)
        high = jnp.swapaxes(x_ref[snap, :, pl.ds(8, 8), :], 0, 1)
        for row in range(3):
            low_ref[row, at, :] = low[row]
            high_ref[row, at, :] = high[5 + row]
        low_ref[3, at, :] = seam_ref[pl.ds(ROWS * snap, 8), :]
        high_ref[3, at, :] = seam_ref[pl.ds(ROWS * snap + 8, 8), :]


def smooth_kernel(x_ref, seam_ref, south_ref, north_ref, order_ref, keep_ref, send_ref, done):
    lat = lax.axis_index("lat")
    not_first = jnp.where(lat == 0, 0, 1)
    not_last = jnp.where(lat == lax.axis_size("lat") - 1, 0, 1)
    row = lax.broadcasted_iota(jnp.int32, (8, LANES), 0)
    lane = lanes_of((8, LANES))
    inside = jnp.where(row < 4, not_last, not_first) == 1
    zero = jnp.zeros((8, LANES), F32)
    wide_lane = lanes_of((ROWS, LANES))

    def along_rows(field):
        tall = jnp.concatenate(field, axis=0)
        near = pltpu.roll(tall, 1, 0) + pltpu.roll(tall, 23, 0)
        return near[0:8], near[8:16], near[16:24]

    def snapshot(snap, carry):
        edges = jnp.swapaxes(
            jnp.stack(
                [north_ref[i, pl.ds(8 * snap, 8), :] for i in range(3)]
                + [zero, zero]
                + [south_ref[i, pl.ds(8 * snap, 8), :] for i in range(3)]
            ),
            0,
            1,
        )
        fields = [
            (x_ref[snap, level, pl.ds(0, 8), :], x_ref[snap, level, pl.ds(8, 8), :], edges[level])
            for level in range(LEVELS)
        ]
        at = pl.ds(pl.multiple_of(8 * snap, 8), 8)
        seam = (
            seam_ref[pl.ds(pl.multiple_of(ROWS * snap, 8), 8), :],
            seam_ref[pl.ds(pl.multiple_of(ROWS * snap + 8, 8), 8), :],
            jnp.where(row < 4, north_ref[3, at, :], south_ref[3, at, :]),
        )
        for sweep in range(3):
            tiles = 3 if sweep < 2 else 2
            fresh_fields = []
            for level in range(LEVELS):
                here = fields[level]
                rows = along_rows(here)
                fresh = []
                for tile in range(tiles):
                    near = rows[tile] + pltpu.roll(here[tile], 1, 1) + pltpu.roll(here[tile], LANES - 1, 1)
                    if level > 0:
                        near = near + fields[level - 1][tile]
                    if level < LEVELS - 1:
                        near = near + fields[level + 1][tile]
                    value = here[tile] + SMOOTH_RATE * (near - 6.0 * here[tile])
                    fresh.append(jnp.where(inside, value, 0.0) if tile == 2 else value)
                fresh_fields.append(tuple(fresh))
            rows = along_rows(seam)
            fresh = []
            for tile in range(tiles):
                here = seam[tile]
                near = rows[tile] + pltpu.roll(here, 1, 1) + pltpu.roll(here, LANES - 1, 1)
                near = near + jnp.where(lane >= 16, pltpu.roll(here, 16, 1), 0.0)
                near = near + jnp.where(lane < LANES - 16, pltpu.roll(here, LANES - 16, 1), 0.0)
                value = here + SMOOTH_RATE * (near - 6.0 * here)
                fresh.append(jnp.where(inside, value, 0.0) if tile == 2 else value)
            fields, seam = fresh_fields, tuple(fresh)
        tall_seam = jnp.concatenate(seam, axis=0)
        for level in range(LEVELS):
            first = pltpu.roll(tall_seam, (LANES - 16 * level - 3) % LANES, 1)
            last = pltpu.roll(tall_seam, (117 - 16 * level) % LANES, 1)
            value = jnp.concatenate(fields[level], axis=0)
            value = value + jnp.where(wide_lane < 3, first, jnp.where(wide_lane >= LANES - 3, last, 0.0))
            done[snap, pl.ds(ROWS * level, ROWS), :] = value
        return carry

    lax.fori_loop(0, SNAPS, snapshot, 0)
    group = lax.axis_index("tm")
    for snap in range(SNAPS):
        keep_ref[snap] = done[snap, pl.ds(pl.multiple_of(HALF_ROWS * group, 8), HALF_ROWS), :]
        send_ref[snap] = done[snap, pl.ds(pl.multiple_of(HALF_ROWS * (1 - group), 8), HALF_ROWS), :]


def pieces(values, count):
    out = []
    for index in range(count):
        piece = values.astype(BF16)
        out.append(piece)
        if index < count - 1:
            values = values - piece.astype(F32)
    return out


def transposed_product(left, right):
    return lax.dot_general(left, right, (((1,), (1,)), ((), ())), preferred_element_type=F32)


def basis_copies(half, q_ref, blocks, sems):
    copies = [
        pltpu.make_async_copy(
            q_ref.at[:, pl.ds(pl.multiple_of(HALF_ROWS * half + QROWS * part, QROWS), QROWS), :],
            blocks.at[part],
            sems.at[part],
        )
        for part in range(HALF_ROWS // QROWS)
    ]
    for copy in copies:
        copy.start()
    return copies


def split_block(block, part, count, stack_ref):
    for sub in range(QROWS // CHUNK):
        turned = jnp.swapaxes(block[:, pl.ds(CHUNK * sub, CHUNK), :], 0, 1)
        for inner in range(CHUNK):
            at = pl.ds(LANES * (QROWS * part + CHUNK * sub + inner), LANES)
            for index, piece in enumerate(pieces(turned[inner], count)):
                stack_ref[pl.ds(EOFS * index, EOFS), at] = piece


def basis_gram_kernel(order_ref, q_ref, stack_ref, gram_ref, blocks, total, sems):
    copies = basis_copies(lax.axis_index("tm"), q_ref, blocks, sems)
    for part, copy in enumerate(copies):
        copy.wait()
        split_block(blocks.at[part], part, 3, stack_ref)
        stack = stack_ref[:, pl.ds(QROWS * LANES * part, QROWS * LANES)]
        product = transposed_product(stack, stack)
        total[...] = product if part == 0 else total[...] + product
    down = total[pl.ds(0, 64), :] + total[pl.ds(64, 64), :] + total[pl.ds(128, 64), :]
    gram_ref[...] = down[:, 0:64] + down[:, 64:128] + down[:, 128:192]


def basis_stack_kernel(order_ref, q_ref, stack_ref, blocks, sems):
    copies = basis_copies(1 - lax.axis_index("tm"), q_ref, blocks, sems)
    for part, copy in enumerate(copies):
        copy.wait()
        split_block(blocks.at[part], part, 2, stack_ref)


def snapshot_columns(ref, start, count):
    turned = jnp.swapaxes(ref[:, pl.ds(start, CHUNK), :], 0, 1)
    return [pieces(turned[i], count) for i in range(CHUNK)]


def side_by_side(early, late):
    columns = [
        jnp.concatenate([jnp.concatenate(pair, axis=0) for pair in zip(one, two)], axis=0) for one, two in zip(early, late)
    ]
    return jnp.concatenate(columns, axis=1)


def in_order(mine, other):
    first = lax.axis_index("tm") == 0
    return jnp.where(first, mine, other), jnp.where(first, other, mine)


def own_gram_kernel(stack_ref, mine_ref, cross_ref, square_ref):
    def block(step, carry):
        cross, square = carry
        columns = snapshot_columns(mine_ref, pl.multiple_of(CHUNK * step, CHUNK), 3)
        columns = jnp.concatenate([jnp.concatenate(c, axis=0) for c in columns], axis=1)
        width = CHUNK * LANES
        stack = stack_ref[:, pl.ds(pl.multiple_of(width * step, width), width)]
        return cross + transposed_product(stack, columns), square + transposed_product(columns, columns)

    zeros = (jnp.zeros((192, 24), F32), jnp.zeros((24, 24), F32))
    cross_ref[...], square_ref[...] = lax.fori_loop(0, HALF_ROWS // CHUNK, block, zeros)


def folded(sums, rows):
    down = sums[0:rows] + sums[rows : 2 * rows] + sums[2 * rows : 3 * rows]
    return down[:, 0:8] + down[:, 8:16] + down[:, 16:24]


def snapshot_gram_kernel(
    stack_ref, gram_ref, mine_ref, other_ref, cross_ref, square_ref, order_ref, own_ref, partner_ref, joined
):
    def block(step, carry):
        cross, square, mixed = carry
        start = pl.multiple_of(CHUNK * step, CHUNK)
        other = snapshot_columns(other_ref, start, 3)
        other = jnp.concatenate([jnp.concatenate(c, axis=0) for c in other], axis=1)
        mine = snapshot_columns(mine_ref, start, 3)
        mine = jnp.concatenate([jnp.concatenate(c, axis=0) for c in mine], axis=1)
        width = CHUNK * LANES
        stack = stack_ref[:, pl.ds(pl.multiple_of(width * step, width), width)]
        return (
            cross + transposed_product(stack, other),
            square + transposed_product(other, other),
            mixed + transposed_product(mine, other),
        )

    zeros = (jnp.zeros((192, 24), F32), jnp.zeros((24, 24), F32), jnp.zeros((24, 24), F32))
    cross, square, mixed = lax.fori_loop(0, HALF_ROWS // CHUNK, block, zeros)
    mixed = folded(mixed, 8)
    projection = jnp.concatenate(in_order(folded(cross_ref[...], 64), folded(cross, 64)), axis=1)
    early, late = in_order(folded(square_ref[...], 8), folded(square, 8))
    upper, _ = in_order(mixed, jnp.transpose(mixed))
    square = jnp.concatenate(
        [jnp.concatenate([early, upper], axis=1), jnp.concatenate([jnp.transpose(upper), late], axis=1)], axis=0
    )
    gram = gram_ref[...]
    joined[pl.ds(0, 32), pl.ds(0, 64)] = gram[0:32, :]
    joined[pl.ds(0, 32), pl.ds(64, 64)] = gram[32:64, :]
    joined[pl.ds(32, 16), pl.ds(0, 64)] = jnp.transpose(projection)
    joined[pl.ds(32, 16), pl.ds(64, 64)] = jnp.concatenate([square, jnp.zeros((16, 48), F32)], axis=1)
    core = lax.axis_index("core")
    own_ref[...] = joined[pl.ds(pl.multiple_of(SIDE * core, 8), SIDE), :]
    partner_ref[...] = joined[pl.ds(pl.multiple_of(SIDE * (1 - core), 8), SIDE), :]


def pair_kernel(one_ref, two_ref, out_ref):
    out_ref[...] = jnp.broadcast_to((one_ref[...] + two_ref[...])[None], out_ref.shape)


def group_kernel(parts_ref, out_ref):
    out_ref[...] = jnp.broadcast_to(jnp.sum(parts_ref[...], axis=0)[None], out_ref.shape)


def factor_kernel(cells, parts_ref, maps_ref, coeffs_ref):
    count = parts_ref.shape[0] // 2
    totals = jnp.concatenate(
        [jnp.sum(parts_ref[pl.ds(count * core, count)], axis=0) for core in range(2)], axis=0
    )
    basis_gram = jnp.concatenate([totals[0:32, 0:64], totals[0:32, 64:128]], axis=0)
    root = math.sqrt(cells)
    coeffs_t = totals[32:48, 0:64] * (1.0 / root)
    snap_gram = totals[32:48, 64:80]
    coeffs_ref[...] = jnp.where(lax.axis_index("tm") == 0, coeffs_t[0:8, :], coeffs_t[8:16, :])
    mixed = (2.0 * STEP_SIZE * root) * coeffs_t + (STEP_SIZE * STEP_SIZE) * jnp.dot(
        snap_gram, coeffs_t, precision=HIGHEST, preferred_element_type=F32
    )
    grown = lax.dot_general(
        coeffs_t, mixed, (((0,), (0,)), ((), ())), precision=HIGHEST, preferred_element_type=F32
    )
    gram = (basis_gram + grown) * (1.0 / cells)
    rows = lax.broadcasted_iota(jnp.int32, (EOFS, EOFS), 0)
    columns = lax.broadcasted_iota(jnp.int32, (EOFS, EOFS), 1)
    work = jnp.concatenate([gram, (rows == columns).astype(F32)], axis=1)
    blocks = [work[8 * i : 8 * i + 8, :] for i in range(8)]
    results = []
    for panel in range(8):
        lower = blocks[panel:]
        columns = [
            [jnp.broadcast_to(b[:, 8 * panel + k : 8 * panel + k + 1], (8, LANES)) for b in lower] for k in range(8)
        ]
        rows = [lower[0][k : k + 1, :] for k in range(8)]
        for k in range(8):
            pivot = columns[k][0][k : k + 1, :]
            inverse = 1.0 / pivot
            factors = [c * inverse for c in columns[k]]
            for m in range(k + 1, 8):
                entry = columns[m][0][k : k + 1, :]
                columns[m] = [c - f * entry for c, f in zip(columns[m], factors)]
                rows[m] = rows[m] - factors[0][m : m + 1, :] * rows[k]
            for i in range(panel + 1, 8):
                blocks[i] = blocks[i] - factors[i - panel] * rows[k]
            results.append(rows[k] * lax.rsqrt(pivot))
    inverse = jnp.concatenate(results, axis=0)[:, EOFS:]
    update = lax.dot_general(
        inverse, coeffs_t, (((1,), (1,)), ((), ())), precision=HIGHEST, preferred_element_type=F32
    )
    rows = [
        jnp.concatenate([inverse_part, inverse_part, update_part, update_part], axis=1)
        for inverse_part, update_part in zip(pieces(inverse, 2), pieces(STEP_SIZE * update, 2))
    ]
    maps_ref[...] = jnp.concatenate(rows, axis=0)


def final_kernel(maps_ref, near_ref, far_ref, keep_ref, here_ref, send_ref, late_ref, out_ref, blocks, sems):
    group = lax.axis_index("tm")
    steps = HALF_ROWS // FINAL_ROWS
    copies = []
    for step in range(2 * steps):
        near = step < steps
        half = group if near else 1 - group
        local = step % steps
        stack_ref, mine_ref, other_ref = (near_ref, keep_ref, here_ref) if near else (far_ref, send_ref, late_ref)
        for sub in range(FINAL_ROWS // CHUNK):
            start = local * FINAL_ROWS + CHUNK * sub
            at = pl.ds(start, CHUNK)
            early, late = in_order(
                jnp.swapaxes(mine_ref[:, at, :], 0, 1), jnp.swapaxes(other_ref[:, at, :], 0, 1)
            )
            columns = jnp.concatenate(
                [
                    jnp.concatenate(pieces(jnp.concatenate([early[i], late[i]], axis=0), 2), axis=0)
                    for i in range(CHUNK)
                ],
                axis=1,
            )
            stack = stack_ref[pl.ds(0, 2 * EOFS), pl.ds(start * LANES, CHUNK * LANES)]
            both = jnp.dot(maps_ref[...], jnp.concatenate([stack, columns], axis=0), preferred_element_type=F32)
            result = both[0:EOFS, :] + both[EOFS:, :]
            result = jnp.stack([result[:, LANES * i : LANES * (i + 1)] for i in range(CHUNK)])
            blocks[step, :, pl.ds(CHUNK * sub, CHUNK), :] = jnp.swapaxes(result, 0, 1)
        to = pl.ds(pl.multiple_of(HALF_ROWS * half + FINAL_ROWS * local, FINAL_ROWS), FINAL_ROWS)
        copy = pltpu.make_async_copy(blocks.at[step], out_ref.at[:, to, :], sems.at[step])
        copy.start()
        copies.append(copy)
    for copy in copies:
        copy.wait()


def neighbours(values_up, values_down, axis, closed):
    count = lax.axis_size(axis)
    ends = count if closed else count - 1
    from_below = lax.ppermute(values_up, axis, [(i, (i + 1) % count) for i in range(ends)])
    from_above = lax.ppermute(values_down, axis, [((i + 1) % count, i) for i in range(ends)])
    return from_below, from_above


def across(values, axis):
    return lax.ppermute(values, axis, [(0, 1), (1, 0)])


def gathered(values, axes):
    return lax.all_to_all(values, axes, 0, 0)


def shards(snapshots, basis):
    lat_count = lax.axis_size("lat")
    cells = CELL_ROWS * LANES * lat_count * lax.axis_size(LON)
    q = pltpu.with_memory_space_constraint(basis.reshape(EOFS, CELL_ROWS, LANES), pltpu.HBM)

    packed = call(pack_kernel, [VMEM], shape(CELL_ROWS, LANES))(snapshots)
    west, east = neighbours(packed, packed, LON, True)
    seam, low, high = call(
        seam_kernel, [VMEM] * 4, (shape(CELL_ROWS, LANES), shape(4, 64, LANES), shape(4, 64, LANES))
    )(snapshots, packed, west, east)
    south, north = neighbours(high, low, "lat", False)
    parts = HALF_ROWS // QROWS
    stack, gram = call(
        basis_gram_kernel,
        [VMEM, ANY],
        (shape(3 * EOFS, HALF_CELLS, dtype=BF16), shape(EOFS, EOFS)),
        [pltpu.VMEM((parts, EOFS, QROWS, LANES), F32), pltpu.VMEM((192, 192), F32), pltpu.SemaphoreType.DMA((parts,))],
        traffic=8 << 20,
    )(seam, q)
    keep, send = call(
        smooth_kernel,
        [VMEM] * 5,
        (shape(SNAPS, HALF_ROWS, LANES),) * 2,
        [pltpu.VMEM((SNAPS, CELL_ROWS, LANES), F32)],
    )(snapshots, seam, south, north, gram)
    here = across(send, "tm")
    far = call(
        basis_stack_kernel,
        [VMEM, ANY],
        shape(2 * EOFS, HALF_CELLS, dtype=BF16),
        [pltpu.VMEM((parts, EOFS, QROWS, LANES), F32), pltpu.SemaphoreType.DMA((parts,))],
        traffic=6 << 20,
    )(keep, q)
    cross, square = call(own_gram_kernel, [VMEM] * 2, (shape(192, 24), shape(24, 24)), traffic=4 << 20)(stack, keep)
    side = shape(SIDE, LANES)
    mine, theirs = call(
        snapshot_gram_kernel, [VMEM] * 7, (side, side), [pltpu.VMEM((PAYLOAD, LANES), F32)]
    )(stack, gram, keep, here, cross, square, far)
    group = lax.axis_size(("pair", "tm"))
    spread = call(pair_kernel, [VMEM] * 2, shape(group, SIDE, LANES))(mine, across(theirs, "core"))
    spread = gathered(spread, ("pair", "tm"))
    late = across(keep, "tm")
    spread = call(group_kernel, [VMEM], shape(2 * lat_count, SIDE, LANES))(spread)
    spread = gathered(spread, ("core", "lat"))
    maps, coeffs_t = call(
        functools.partial(factor_kernel, cells), [VMEM], (shape(2 * EOFS, 160, dtype=BF16), shape(SNAPS, EOFS))
    )(spread)
    final_steps = CELL_ROWS // FINAL_ROWS
    new_basis = pl.pallas_call(
        final_kernel,
        out_shape=shape(EOFS, CELL_ROWS, LANES),
        in_specs=[VMEM] * 7,
        out_specs=ANY,
        scratch_shapes=[
            pltpu.VMEM((final_steps, EOFS, FINAL_ROWS, LANES), F32),
            pltpu.SemaphoreType.DMA((final_steps,)),
        ],
        compiler_params=pltpu.CompilerParams(vmem_limit_bytes=8 << 20),
    )(maps, stack, far, keep, here, send, late)
    return (new_basis.reshape(basis.shape), coeffs_t.T)


def solution(mesh):
    pairs = mesh.shape["lon"] // 2
    split = Mesh(mesh.devices.reshape(pairs, 2, *mesh.devices.shape[1:]), LON + tuple(mesh.axis_names[1:]))
    fields = P(None, None, "lat", LON)
    return jax.shard_map(
        shards,
        mesh=split,
        in_specs=(P("tm", None, "lat", LON), fields),
        out_specs=(fields, P(None, "tm")),
        check_vma=False,
    )
```

time: 96.3 us -> 79.6 us (0.83)
  Pallas kernels: 29 us -> 20.8 us
  blocking collectives: 16.8 us -> 11.5 us
  waiting for transfers between devices: 9.18 us -> 11.9 us
  local copies, waits for them, and re-layouts: 7.89 us -> 5.27 us
  starting transfers between devices: 31.1 us -> 29 us
  other arithmetic: 1.05 us -> 0 us
    pallas_call x8 -> x11, Pallas kernels: 29 us -> 20.8 us  [the longest x1 3.69 us: shards(): call(functools.partial(factor_kernel, cells), [VMEM], (shape(2 * EOFS, 16...]
    all_to_all x1, blocking collectives: 16.8 us -> 11.5 us  [gathered(): return lax.all_to_all(values, axes, 0, 0)]
    all_to_all x1, starting transfers between devices: 5.53 us -> 10 us  [gathered(): return lax.all_to_all(values, axes, 0, 0)]
    ppermute x3 -> x2, starting transfers between devices: 7.27 us -> 3.55 us  [neighbours(): lax.ppermute(values_up, axis, [(i, (i + 1) % count) for i in range(ends)])]
    all_to_all x1, waiting for transfers between devices: 4.87 us -> 7.78 us  [gathered(): return lax.all_to_all(values, axes, 0, 0)]
    unnamed x16 -> x18, local copies, waits for them, and re-layouts: 7.18 us -> 5.27 us
    ppermute x4 -> x3, starting transfers between devices: 12.4 us -> 10.8 us  [across(): return lax.ppermute(values, axis, [(0, 1), (1, 0)])]
    ppermute x3 -> x2, starting transfers between devices: 5.86 us -> 4.57 us  [neighbours(): lax.ppermute(values_down, axis, [((i + 1) % count, i) for i in range(ends)])]
  transfers between devices with their start and end apart: 11 -> 8, of which waited for: 3 -> 5; matrix products, arithmetic and copies ran while one was open for 1% -> 0% of each run, Pallas kernels for 13% -> 14%
where the time goes in v3:
time: 79.6 us; the launch traced here: 79.1 us
  starting transfers between devices  29 us (36%)
  Pallas kernels  20.8 us (26%)
  waiting for transfers between devices  11.9 us (15%)
  blocking collectives  11.5 us (14%)
  local copies, waits for them, and re-layouts  5.27 us (7%)
    all_to_all x1, blocking collectives, gathered(): return lax.all_to_all(values, axes, 0, 0)  11.5 us
    ppermute x3, starting transfers between devices, across(): return lax.ppermute(values, axis, [(0, 1), (1, 0)])  10.8 us
    all_to_all x1, starting transfers between devices, gathered(): return lax.all_to_all(values, axes, 0, 0)  10 us
    all_to_all x1, waiting for transfers between devices, gathered(): return lax.all_to_all(values, axes, 0, 0)  7.78 us
    unnamed x18, local copies, waits for them, and re-layouts  5.27 us
    ppermute x2, starting transfers between devices, neighbours(): lax.ppermute(values_down, axis, [((i + 1) % count, i) for i in range(ends)])  4.57 us
    pallas_call x1, Pallas kernels, shards(): call(functools.partial(factor_kernel, cells), [VMEM], (shape(2 * EOFS, 16...  3.69 us
    pallas_call x1, Pallas kernels, shards(): call(basis_gram_kernel, [VMEM, ANY], (shape(3 * EOFS, HALF_CELLS, dtype=B...  3.56 us
  transfers between devices with their start and end apart: 8, of which 5 were waited for; matrix products, arithmetic and copies ran while one was open for 0% of the time, Pallas kernels for 14%

profile of v3, /device:TPU:1, one launch (start us, length us, event | category | flops | bytes accessed | tf_op | source)
XLA Modules:
  0.0 79.1 jit_solution(17170527703043930365)
XLA Ops:
  0.6 1.0 %copy-done.2 = f32[8,8,16,128]{3,2,1,0:T(8,128)S(1)} copy-done((f32[8,8,16,128]{3,2,1,0:T(8,128)S(1)}, f32[8,8,16,128]{3,2,1,0:T(8,128)}, u32[]{:S(2)}) %copy-start.2) | copy-done | bytes 524312
  1.9 3.3 %collective-permute-start.1 = (f32[128,128]{1,0:T(8,128)S(1)}, f32[128,128]{1,0:T(8,128)S(1)}, u32[]{:S(2)}, u32[]{:S(2)}) collective-permute-start(f32[128,128]{1,0:T(8,128)S(1)} %shard_map.41.packed_ref), channel_id=1, source_target_pairs={{16,0},{32,16},{48,32},{64,48},{80,64},{96,80},{112,96},{128,112},... | collective-permute-start | bytes 196616 | tf_op jit(solution)/shard_map/ppermute | solution.py:383
  5.2 1.4 %collective-permute-done.1.east_ref = f32[128,128]{1,0:T(8,128)S(1)} collective-permute-done((f32[128,128]{1,0:T(8,128)S(1)}, f32[128,128]{1,0:T(8,128)S(1)}, u32[]{:S(2)}, u32[]{:S(2)}) %collective-permute-start.1) | collective-permute-done | bytes 65568 | tf_op jit(solution)/shard_map/ppermute | solution.py:383
  6.6 0.8 %collective-permute-done.west_ref = f32[128,128]{1,0:T(8,128)S(1)} collective-permute-done((f32[128,128]{1,0:T(8,128)S(1)}, f32[128,128]{1,0:T(8,128)S(1)}, u32[]{:S(2)}, u32[]{:S(2)}) %collective-permute-start) | collective-permute-done | bytes 65568 | tf_op jit(solution)/shard_map/ppermute | solution.py:382
  7.5 3.5 %collective-permute-start.2 = (f32[4,64,128]{2,1,0:T(8,128)S(1)}, f32[4,64,128]{2,1,0:T(8,128)S(1)}, u32[]{:S(2)}, u32[]{:S(2)}) collective-permute-start(f32[4,64,128]{2,1,0:T(8,128)S(1)} %get-tuple-element.18), channel_id=1, source_target_pairs={{0,2},{2,4},{4,6},{6,8},{8,10},{10,12},{12,14},{1,3},{3,5},{5,7},{... | collective-permute-start | bytes 393224 | tf_op jit(solution)/shard_map/ppermute | solution.py:382
  11.1 1.3 %collective-permute-start.3 = (f32[4,64,128]{2,1,0:T(8,128)S(1)}, f32[4,64,128]{2,1,0:T(8,128)S(1)}, u32[]{:S(2)}, u32[]{:S(2)}) collective-permute-start(f32[4,64,128]{2,1,0:T(8,128)S(1)} %get-tuple-element.19), channel_id=1, source_target_pairs={{2,0},{4,2},{6,4},{8,6},{10,8},{12,10},{14,12},{3,1},{5,3},{7,5},{... | collective-permute-start | bytes 393224 | tf_op jit(solution)/shard_map/ppermute | solution.py:383
  12.4 3.6 %shard_map.43 = (bf16[192,8192]{1,0:T(8,128)(2,1)S(1)}, f32[64,64]{1,0:T(8,128)S(1)}) custom-call(f32[128,128]{1,0:T(8,128)S(1)} %get-tuple-element.15.order_ref.seam_ref, f32[64,128,128]{2,1,0:T(8,128)} %bitcast.3), custom_call_target="tpu_custom_call" | custom-call | flops 1000000 | bytes 8388608 | tf_op jit(solution)/shard_map/pallas_call | solution.py:407
  15.9 1.0 %collective-permute-done.3.north_ref = f32[4,64,128]{2,1,0:T(8,128)S(1)} collective-permute-done((f32[4,64,128]{2,1,0:T(8,128)S(1)}, f32[4,64,128]{2,1,0:T(8,128)S(1)}, u32[]{:S(2)}, u32[]{:S(2)}) %collective-permute-start.3) | collective-permute-done | bytes 131104 | tf_op jit(solution)/shard_map/ppermute | solution.py:383
  16.9 3.1 %shard_map.44 = (f32[8,64,128]{2,1,0:T(8,128)S(1)}, f32[8,64,128]{2,1,0:T(8,128)S(1)}) custom-call(f32[8,8,16,128]{3,2,1,0:T(8,128)S(1)} %copy-done.3, f32[128,128]{1,0:T(8,128)S(1)} %get-tuple-element.15.order_ref.seam_ref, f32[4,64,128]{2,1,0:T(8,128)S(1)} %collective-permute-done.2.south_ref, f32[4,64,128]{2,1,0:T(8,128)S(1)} %collective-permute-done.3.north_ref, ...), custom_call_target="tpu_custom_call" | custom-call | flops 1000000 | bytes 1000000 | tf_op jit(solution)/shard_map/pallas_call | solution.py:414
  20.1 2.7 %collective-permute-start.4 = (f32[8,64,128]{2,1,0:T(8,128)S(1)}, f32[8,64,128]{2,1,0:T(8,128)S(1)}, u32[]{:S(2)}, u32[]{:S(2)}) collective-permute-start(f32[8,64,128]{2,1,0:T(8,128)S(1)} %get-tuple-element.21.send_ref), channel_id=1, source_target_pairs={{0,1},{1,0},{2,3},{3,2},{4,5},{5,4},{6,7},{7,6},{8,9},{9,8},{10,11... | collective-permute-start | bytes 786440 | tf_op jit(solution)/shard_map/ppermute | solution.py:388
  22.8 1.9 %shard_map.46.order_ref.far_ref = bf16[128,8192]{1,0:T(8,128)(2,1)S(1)} custom-call(f32[8,64,128]{2,1,0:T(8,128)S(1)} %get-tuple-element.20.mine_ref.order_ref.keep_ref, f32[64,128,128]{2,1,0:T(8,128)} %bitcast.4), custom_call_target="tpu_custom_call" | custom-call | flops 1000000 | bytes 6291456 | tf_op jit(solution)/shard_map/pallas_call | solution.py:421
  24.7 2.2 %shard_map.45 = (f32[192,24]{1,0:T(8,128)S(1)}, f32[24,24]{1,0:T(8,128)S(1)}) custom-call(bf16[192,8192]{1,0:T(8,128)(2,1)S(1)} %get-tuple-element.16.stack_ref.near_ref, f32[8,64,128]{2,1,0:T(8,128)S(1)} %get-tuple-element.20.mine_ref.order_ref.keep_ref), custom_call_target="tpu_custom_call" | custom-call | flops 1000000 | bytes 4194304 | tf_op jit(solution)/shard_map/pallas_call | solution.py:428
  26.9 2.6 %shard_map.47 = (f32[24,128]{1,0:T(8,128)S(1)}, f32[24,128]{1,0:T(8,128)S(1)}) custom-call(bf16[192,8192]{1,0:T(8,128)(2,1)S(1)} %get-tuple-element.16.stack_ref.near_ref, f32[64,64]{1,0:T(8,128)S(1)} %get-tuple-element.17.order_ref.gram_ref, f32[8,64,128]{2,1,0:T(8,128)S(1)} %get-tuple-element.20.mine_ref.order_ref.keep_ref, ...), custom_call_target="tpu_custom_call" | custom-call | flops 1000000 | bytes 1000000 | tf_op jit(solution)/shard_map/pallas_call | solution.py:430
  29.6 7.5 %collective-permute-start.5 = (f32[24,128]{1,0:T(8,128)S(1)}, f32[24,128]{1,0:T(8,128)S(1)}, u32[]{:S(2)}, u32[]{:S(2)}) collective-permute-start(f32[24,128]{1,0:T(8,128)S(1)} %get-tuple-element.25), channel_id=1, source_target_pairs={{0,16},{16,0},{1,17},{17,1},{2,18},{18,2},{3,19},{19,3},{4,20},{20... | collective-permute-start | bytes 36872 | tf_op jit(solution)/shard_map/ppermute | solution.py:388
  37.1 0.8 %collective-permute-done.5.two_ref = f32[24,128]{1,0:T(8,128)S(1)} collective-permute-done((f32[24,128]{1,0:T(8,128)S(1)}, f32[24,128]{1,0:T(8,128)S(1)}, u32[]{:S(2)}, u32[]{:S(2)}) %collective-permute-start.5) | collective-permute-done | bytes 12320 | tf_op jit(solution)/shard_map/ppermute | solution.py:388
  38.0 11.5 %all_to_all.10.parts_ref = f32[16,24,128]{2,1,0:T(8,128)S(1)} all-to-all(f32[16,24,128]{2,1,0:T(8,128)S(1)} %shard_map.48), channel_id=1, replica_groups=mesh['pair'=8,'core'=2,'lat'=8,'tm'=2] {'pair','tm'}, dimensions={0} | all-to-all | bytes 393216 | tf_op jit(solution)/shard_map/all_to_all | solution.py:392
  49.5 0.7 copy-done.6
  50.2 10.0 %all-to-all-start.1 = ((f32[16,24,128]{2,1,0:T(8,128)}), f32[16,24,128]{2,1,0:T(8,128)}, u32[]{:S(2)}, u32[]{:S(2)}) async-start(f32[16,24,128]{2,1,0:T(8,128)} %copy-done.6), calls=%async_computation.1 | async-start | bytes 393216 | tf_op jit(solution)/shard_map/all_to_all | solution.py:392
  60.8 7.8 %all-to-all-done.1.parts_ref = f32[16,24,128]{2,1,0:T(8,128)} async-done(((f32[16,24,128]{2,1,0:T(8,128)}), f32[16,24,128]{2,1,0:T(8,128)}, u32[]{:S(2)}, u32[]{:S(2)}) %all-to-all-start.1) | async-done | bytes 196640 | tf_op jit(solution)/shard_map/all_to_all | solution.py:392
  68.6 3.7 %shard_map.50 = (bf16[128,160]{1,0:T(8,128)(2,1)S(1)}, f32[8,64]{1,0:T(8,128)}) custom-call(f32[16,24,128]{2,1,0:T(8,128)} %all-to-all-done.1.parts_ref), custom_call_target="tpu_custom_call" | custom-call | flops 1000000 | bytes 1000000 | tf_op jit(solution)/shard_map/pallas_call | solution.py:439
  72.3 1.6 %copy-done.1 = bf16[128,8192]{1,0:T(8,128)(2,1)S(1)} copy-done((bf16[128,8192]{1,0:T(8,128)(2,1)S(1)}, bf16[128,8192]{1,0:T(8,128)(2,1)}, u32[]{:S(2)}) %copy-start.1) | copy-done | bytes 2097176
  73.9 0.9 %copy-done.5 = f32[8,64,128]{2,1,0:T(8,128)S(1)} copy-done((f32[8,64,128]{2,1,0:T(8,128)S(1)}, f32[8,64,128]{2,1,0:T(8,128)}, u32[]{:S(2)}) %copy-start.5) | copy-done | bytes 262168
  74.8 0.9 %copy-done.8 = f32[8,64,128]{2,1,0:T(8,128)S(1)} copy-done((f32[8,64,128]{2,1,0:T(8,128)S(1)}, f32[8,64,128]{2,1,0:T(8,128)}, u32[]{:S(2)}) %copy-start.8) | copy-done | bytes 262168
  75.8 3.4 %shard_map.51 = f32[64,128,128]{2,1,0:T(8,128)} custom-call(bf16[128,160]{1,0:T(8,128)(2,1)S(1)} %get-tuple-element.26.maps_ref, bf16[192,8192]{1,0:T(8,128)(2,1)S(1)} %get-tuple-element.16.stack_ref.near_ref, bf16[128,8192]{1,0:T(8,128)(2,1)S(1)} %copy-done.1, f32[8,64,128]{2,1,0:T(8,128)S(1)} %get-tuple-element.20.mine_ref.order_ref.keep_ref, ...), custom_call_target="tpu_custom_call" | custom-call | tf_op jit(solution)/shard_map/pallas_call | solution.py:443
  (22 shorter events, 1.0 us)
Async XLA Ops:
  0.6 1.0 %copy-start.2 = (f32[8,8,16,128]{3,2,1,0:T(8,128)S(1)}, f32[8,8,16,128]{3,2,1,0:T(8,128)}, u32[]{:S(2)}) copy-start(f32[8,8,16,128]{3,2,1,0:T(8,128)} %x_ref.5) | copy-start | bytes 1572868
  1.7 15.3 %copy-start.3 = (f32[8,8,16,128]{3,2,1,0:T(8,128)S(1)}, f32[8,8,16,128]{3,2,1,0:T(8,128)}, u32[]{:S(2)}) copy-start(f32[8,8,16,128]{3,2,1,0:T(8,128)} %x_ref.5) | copy-start | bytes 1572868
  1.9 4.7 %collective-permute-start.1 = (f32[128,128]{1,0:T(8,128)S(1)}, f32[128,128]{1,0:T(8,128)S(1)}, u32[]{:S(2)}, u32[]{:S(2)}) collective-permute-start(f32[128,128]{1,0:T(8,128)S(1)} %shard_map.41.packed_ref), channel_id=1, source_target_pairs={{16,0},{32,16},{48,32},{64,48},{80,64},{96,80},{112,96},{128,112},... | collective-permute-start | bytes 196616 | tf_op jit(solution)/shard_map/ppermute | solution.py:383
  5.2 2.3 %collective-permute-start = (f32[128,128]{1,0:T(8,128)S(1)}, f32[128,128]{1,0:T(8,128)S(1)}, u32[]{:S(2)}, u32[]{:S(2)}) collective-permute-start(f32[128,128]{1,0:T(8,128)S(1)} %shard_map.41.packed_ref), channel_id=1, source_target_pairs={{0,16},{16,32},{32,48},{48,64},{64,80},{80,96},{96,112},{112,128},... | collective-permute-start | bytes 196616 | tf_op jit(solution)/shard_map/ppermute | solution.py:382
  7.5 8.4 %collective-permute-start.2 = (f32[4,64,128]{2,1,0:T(8,128)S(1)}, f32[4,64,128]{2,1,0:T(8,128)S(1)}, u32[]{:S(2)}, u32[]{:S(2)}) collective-permute-start(f32[4,64,128]{2,1,0:T(8,128)S(1)} %get-tuple-element.18), channel_id=1, source_target_pairs={{0,2},{2,4},{4,6},{6,8},{8,10},{10,12},{12,14},{1,3},{3,5},{5,7},{... | collective-permute-start | bytes 393224 | tf_op jit(solution)/shard_map/ppermute | solution.py:382
  11.1 5.9 %collective-permute-start.3 = (f32[4,64,128]{2,1,0:T(8,128)S(1)}, f32[4,64,128]{2,1,0:T(8,128)S(1)}, u32[]{:S(2)}, u32[]{:S(2)}) collective-permute-start(f32[4,64,128]{2,1,0:T(8,128)S(1)} %get-tuple-element.19), channel_id=1, source_target_pairs={{2,0},{4,2},{6,4},{8,6},{10,8},{12,10},{14,12},{3,1},{5,3},{7,5},{... | collective-permute-start | bytes 393224 | tf_op jit(solution)/shard_map/ppermute | solution.py:383
  20.1 6.8 %copy-start.7 = (f32[8,64,128]{2,1,0:T(8,128)}, f32[8,64,128]{2,1,0:T(8,128)S(1)}, u32[]{:S(2)}) copy-start(f32[8,64,128]{2,1,0:T(8,128)S(1)} %get-tuple-element.21.send_ref) | copy-start | bytes 786436
  20.1 6.8 %collective-permute-start.4 = (f32[8,64,128]{2,1,0:T(8,128)S(1)}, f32[8,64,128]{2,1,0:T(8,128)S(1)}, u32[]{:S(2)}, u32[]{:S(2)}) collective-permute-start(f32[8,64,128]{2,1,0:T(8,128)S(1)} %get-tuple-element.21.send_ref), channel_id=1, source_target_pairs={{0,1},{1,0},{2,3},{3,2},{4,5},{5,4},{6,7},{7,6},{8,9},{9,8},{10,11... | collective-permute-start | bytes 786440 | tf_op jit(solution)/shard_map/ppermute | solution.py:388
  24.7 4.9 %copy-start = (bf16[128,8192]{1,0:T(8,128)(2,1)}, bf16[128,8192]{1,0:T(8,128)(2,1)S(1)}, u32[]{:S(2)}) copy-start(bf16[128,8192]{1,0:T(8,128)(2,1)S(1)} %shard_map.46.order_ref.far_ref) | copy-start | bytes 6291460
  26.9 2.7 %copy-start.4 = (f32[8,64,128]{2,1,0:T(8,128)}, f32[8,64,128]{2,1,0:T(8,128)S(1)}, u32[]{:S(2)}) copy-start(f32[8,64,128]{2,1,0:T(8,128)S(1)} %collective-permute-done.4.other_ref.here_ref) | copy-start | bytes 786436
  29.6 8.3 %collective-permute-start.5 = (f32[24,128]{1,0:T(8,128)S(1)}, f32[24,128]{1,0:T(8,128)S(1)}, u32[]{:S(2)}, u32[]{:S(2)}) collective-permute-start(f32[24,128]{1,0:T(8,128)S(1)} %get-tuple-element.25), channel_id=1, source_target_pairs={{0,16},{16,0},{1,17},{17,1},{2,18},{18,2},{3,19},{19,3},{4,20},{20... | collective-permute-start | bytes 36872 | tf_op jit(solution)/shard_map/ppermute | solution.py:388
  49.5 0.7 copy-start.6
  50.2 18.4 %all-to-all-start.1 = ((f32[16,24,128]{2,1,0:T(8,128)}), f32[16,24,128]{2,1,0:T(8,128)}, u32[]{:S(2)}, u32[]{:S(2)}) async-start(f32[16,24,128]{2,1,0:T(8,128)} %copy-done.6), calls=%async_computation.1 | async-start | bytes 393216 | tf_op jit(solution)/shard_map/all_to_all | solution.py:392
  60.2 12.1 %collective-permute-start.6 = (f32[8,64,128]{2,1,0:T(8,128)S(1)}, f32[8,64,128]{2,1,0:T(8,128)}, u32[]{:S(2)}, u32[]{:S(2)}) collective-permute-start(f32[8,64,128]{2,1,0:T(8,128)S(1)} %get-tuple-element.20.mine_ref.order_ref.keep_ref), channel_id=1, source_target_pairs={{0,1},{1,0},{2,3},{3,2},{4,5},{5,4},{6,7},{7,6},{8,9},{9,8},{10,11... | collective-permute-start | bytes 786440 | tf_op jit(solution)/shard_map/ppermute | solution.py:388
  72.3 1.6 %copy-start.1 = (bf16[128,8192]{1,0:T(8,128)(2,1)S(1)}, bf16[128,8192]{1,0:T(8,128)(2,1)}, u32[]{:S(2)}) copy-start(bf16[128,8192]{1,0:T(8,128)(2,1)} %copy-done) | copy-start | bytes 6291460
  73.9 0.9 %copy-start.5 = (f32[8,64,128]{2,1,0:T(8,128)S(1)}, f32[8,64,128]{2,1,0:T(8,128)}, u32[]{:S(2)}) copy-start(f32[8,64,128]{2,1,0:T(8,128)} %copy-done.4) | copy-start | bytes 786436
  74.8 0.9 %copy-start.8 = (f32[8,64,128]{2,1,0:T(8,128)S(1)}, f32[8,64,128]{2,1,0:T(8,128)}, u32[]{:S(2)}) copy-start(f32[8,64,128]{2,1,0:T(8,128)} %copy-done.7) | copy-start | bytes 786436

commit v4 on v3

--- a/solution.py
+++ b/solution.py
@@ -7,6 +7,7 @@
 from jax.experimental import pallas as pl
 from jax.experimental.pallas import tpu as pltpu
 from jax.sharding import Mesh, PartitionSpec as P
+
 
 SMOOTH_RATE = 0.1
 STEP_SIZE = 0.25
@@ -19,7 +20,7 @@
 HALF_ROWS = CELL_ROWS // 2
 HALF_CELLS = HALF_ROWS * LANES
 CHUNK = 8
-PAYLOAD = 48
+PAYLOAD = 32
 SIDE = PAYLOAD // 2
 QROWS = 16
 FINAL_ROWS = 16
@@ -216,26 +217,20 @@
     return [pieces(turned[i], count) for i in range(CHUNK)]
 
 
-def side_by_side(early, late):
-    columns = [
-        jnp.concatenate([jnp.concatenate(pair, axis=0) for pair in zip(one, two)], axis=0) for one, two in zip(early, late)
-    ]
-    return jnp.concatenate(columns, axis=1)
-
-
 def in_order(mine, other):
     first = lax.axis_index("tm") == 0
     return jnp.where(first, mine, other), jnp.where(first, other, mine)
 
 
-def own_gram_kernel(stack_ref, mine_ref, cross_ref, square_ref):
+def own_gram_kernel(stack_ref, mine_ref, cross_ref, square_ref, pieces_ref):
     def block(step, carry):
         cross, square = carry
         columns = snapshot_columns(mine_ref, pl.multiple_of(CHUNK * step, CHUNK), 3)
         columns = jnp.concatenate([jnp.concatenate(c, axis=0) for c in columns], axis=1)
         width = CHUNK * LANES
-        stack = stack_ref[:, pl.ds(pl.multiple_of(width * step, width), width)]
-        return cross + transposed_product(stack, columns), square + transposed_product(columns, columns)
+        at = pl.ds(pl.multiple_of(width * step, width), width)
+        pieces_ref[:, at] = columns
+        return cross + transposed_product(stack_ref[:, at], columns), square + transposed_product(columns, columns)
 
     zeros = (jnp.zeros((192, 24), F32), jnp.zeros((24, 24), F32))
     cross_ref[...], square_ref[...] = lax.fori_loop(0, HALF_ROWS // CHUNK, block, zeros)
@@ -247,21 +242,19 @@
 
 
 def snapshot_gram_kernel(
-    stack_ref, gram_ref, mine_ref, other_ref, cross_ref, square_ref, order_ref, own_ref, partner_ref, joined
+    stack_ref, gram_ref, pieces_ref, other_ref, cross_ref, square_ref, order_ref, own_ref, partner_ref, joined
 ):
     def block(step, carry):
         cross, square, mixed = carry
         start = pl.multiple_of(CHUNK * step, CHUNK)
         other = snapshot_columns(other_ref, start, 3)
         other = jnp.concatenate([jnp.concatenate(c, axis=0) for c in other], axis=1)
-        mine = snapshot_columns(mine_ref, start, 3)
-        mine = jnp.concatenate([jnp.concatenate(c, axis=0) for c in mine], axis=1)
         width = CHUNK * LANES
-        stack = stack_ref[:, pl.ds(pl.multiple_of(width * step, width), width)]
+        at = pl.ds(pl.multiple_of(width * step, width), width)
         return (
-            cross + transposed_product(stack, other),
+            cross + transposed_product(stack_ref[:, at], other),
             square + transposed_product(other, other),
-            mixed + transposed_product(mine, other),
+            mixed + transposed_product(pieces_ref[:, at], other),
         )
 
     zeros = (jnp.zeros((192, 24), F32), jnp.zeros((24, 24), F32), jnp.zeros((24, 24), F32))
@@ -274,10 +267,16 @@
         [jnp.concatenate([early, upper], axis=1), jnp.concatenate([jnp.transpose(upper), late], axis=1)], axis=0
     )
     gram = gram_ref[...]
-    joined[pl.ds(0, 32), pl.ds(0, 64)] = gram[0:32, :]
-    joined[pl.ds(0, 32), pl.ds(64, 64)] = gram[32:64, :]
-    joined[pl.ds(32, 16), pl.ds(0, 64)] = jnp.transpose(projection)
-    joined[pl.ds(32, 16), pl.ds(64, 64)] = jnp.concatenate([square, jnp.zeros((16, 48), F32)], axis=1)
+    low, high = gram[0:32, 0:32], gram[32:64, 32:64]
+    row = lax.broadcasted_iota(jnp.int32, (32, 32), 0)
+    column = lax.broadcasted_iota(jnp.int32, (32, 32), 1)
+    diagonal = jnp.sum(jnp.where(row == column, high, 0.0), axis=0, keepdims=True)
+    both = jnp.where(row >= column, low, high)
+    below = jnp.concatenate(
+        [square, jnp.zeros((16, 16), F32), jnp.broadcast_to(diagonal, (16, 32))], axis=1
+    )
+    right = jnp.concatenate([jnp.transpose(projection), below], axis=0)
+    joined[...] = jnp.concatenate([both, gram[32:64, 0:32], right], axis=1)
     core = lax.axis_index("core")
     own_ref[...] = joined[pl.ds(pl.multiple_of(SIDE * core, 8), SIDE), :]
     partner_ref[...] = joined[pl.ds(pl.multiple_of(SIDE * (1 - core), 8), SIDE), :]
@@ -296,10 +295,19 @@
     totals = jnp.concatenate(
         [jnp.sum(parts_ref[pl.ds(count * core, count)], axis=0) for core in range(2)], axis=0
     )
-    basis_gram = jnp.concatenate([totals[0:32, 0:64], totals[0:32, 64:128]], axis=0)
+    row = lax.broadcasted_iota(jnp.int32, (EOFS, EOFS), 0)
+    column = lax.broadcasted_iota(jnp.int32, (EOFS, EOFS), 1)
+    both = totals[:, 0:32]
+    once = jnp.concatenate(
+        [jnp.concatenate([both, jnp.zeros((32, 32), F32)], axis=1), jnp.concatenate([totals[:, 32:64], both], axis=1)], axis=0
+    )
+    once = jnp.where(((row < 32) & (row > column)) | ((row >= 32) & ((column < 32) | (row < column))), once, 0.0)
+    corner = jnp.concatenate([both, jnp.zeros((32, 32), F32)], axis=1)
+    diagonal = jnp.concatenate([corner, jnp.broadcast_to(totals[16:17, 64:128], (32, EOFS))], axis=0)
+    basis_gram = once + jnp.transpose(once) + jnp.where(row == column, diagonal, 0.0)
     root = math.sqrt(cells)
-    coeffs_t = totals[32:48, 0:64] * (1.0 / root)
-    snap_gram = totals[32:48, 64:80]
+    coeffs_t = totals[0:16, 64:128] * (1.0 / root)
+    snap_gram = totals[16:32, 64:80]
     coeffs_ref[...] = jnp.where(lax.axis_index("tm") == 0, coeffs_t[0:8, :], coeffs_t[8:16, :])
     mixed = (2.0 * STEP_SIZE * root) * coeffs_t + (STEP_SIZE * STEP_SIZE) * jnp.dot(
         snap_gram, coeffs_t, precision=HIGHEST, preferred_element_type=F32
@@ -392,7 +400,7 @@
     return lax.all_to_all(values, axes, 0, 0)
 
 
-def shards(snapshots, basis):
+def update(snapshots, basis):
     lat_count = lax.axis_size("lat")
     cells = CELL_ROWS * LANES * lat_count * lax.axis_size(LON)
     q = pltpu.with_memory_space_constraint(basis.reshape(EOFS, CELL_ROWS, LANES), pltpu.HBM)
@@ -425,15 +433,20 @@
         [pltpu.VMEM((parts, EOFS, QROWS, LANES), F32), pltpu.SemaphoreType.DMA((parts,))],
         traffic=6 << 20,
     )(keep, q)
-    cross, square = call(own_gram_kernel, [VMEM] * 2, (shape(192, 24), shape(24, 24)), traffic=4 << 20)(stack, keep)
+    cross, square, split = call(
+        own_gram_kernel,
+        [VMEM] * 2,
+        (shape(192, 24), shape(24, 24), shape(24, HALF_CELLS, dtype=BF16)),
+        traffic=4 << 20,
+    )(stack, keep)
     side = shape(SIDE, LANES)
+    late = across(keep, "tm")
     mine, theirs = call(
         snapshot_gram_kernel, [VMEM] * 7, (side, side), [pltpu.VMEM((PAYLOAD, LANES), F32)]
-    )(stack, gram, keep, here, cross, square, far)
+    )(stack, gram, split, here, cross, square, far)
     group = lax.axis_size(("pair", "tm"))
     spread = call(pair_kernel, [VMEM] * 2, shape(group, SIDE, LANES))(mine, across(theirs, "core"))
     spread = gathered(spread, ("pair", "tm"))
-    late = across(keep, "tm")
     spread = call(group_kernel, [VMEM], shape(2 * lat_count, SIDE, LANES))(spread)
     spread = gathered(spread, ("core", "lat"))
     maps, coeffs_t = call(
@@ -459,7 +472,7 @@
     split = Mesh(mesh.devices.reshape(pairs, 2, *mesh.devices.shape[1:]), LON + tuple(mesh.axis_names[1:]))
     fields = P(None, None, "lat", LON)
     return jax.shard_map(
-        shards,
+        update,
         mesh=split,
         in_specs=(P("tm", None, "lat", LON), fields),
         out_specs=(fields, P(None, "tm")),

time: 79.6 us -> 77.7 us (0.976)
  blocking collectives: 11.5 us -> 17.3 us
  waiting for transfers between devices: 11.9 us -> 8.33 us
  starting transfers between devices: 29 us -> 25.5 us
    all_to_all x1, starting transfers between devices: 10 us -> 4.23 us  [gathered(): return lax.all_to_all(values, axes, 0, 0)]
    all_to_all x1, blocking collectives: 11.5 us -> 17.3 us  [gathered(): return lax.all_to_all(values, axes, 0, 0)]
    all_to_all x1, waiting for transfers between devices: 7.78 us -> 4.2 us  [gathered(): return lax.all_to_all(values, axes, 0, 0)]
    ppermute x3, starting transfers between devices: 10.8 us -> 13.1 us  [across(): return lax.ppermute(values, axis, [(0, 1), (1, 0)])]
where the time goes in v4:
time: 77.7 us; the launch traced here: 77.3 us
  starting transfers between devices  25.5 us (33%)
  Pallas kernels  20.2 us (26%)
  blocking collectives  17.3 us (22%)
  waiting for transfers between devices  8.33 us (11%)
  local copies, waits for them, and re-layouts  5.2 us (7%)
  between operations  0.78 us (1%)
    all_to_all x1, blocking collectives, gathered(): return lax.all_to_all(values, axes, 0, 0)  17.3 us
    ppermute x3, starting transfers between devices, across(): return lax.ppermute(values, axis, [(0, 1), (1, 0)])  13.1 us
    unnamed x18, local copies, waits for them, and re-layouts  5.2 us
    ppermute x2, starting transfers between devices, neighbours(): lax.ppermute(values_down, axis, [((i + 1) % count, i) for i in range(ends)])  4.57 us
    all_to_all x1, starting transfers between devices, gathered(): return lax.all_to_all(values, axes, 0, 0)  4.23 us
    all_to_all x1, waiting for transfers between devices, gathered(): return lax.all_to_all(values, axes, 0, 0)  4.2 us
    pallas_call x1, Pallas kernels, update(): call(basis_gram_kernel, [VMEM, ANY], (shape(3 * EOFS, HALF_CELLS, dtype=B...  3.56 us
    ppermute x2, starting transfers between devices, neighbours(): lax.ppermute(values_up, axis, [(i, (i + 1) % count) for i in range(ends)])  3.55 us
  transfers between devices with their start and end apart: 8, of which 5 were waited for; matrix products, arithmetic and copies ran while one was open for 0% of the time, Pallas kernels for 14%

profile of v4, /device:TPU:1, one launch (start us, length us, event | category | flops | bytes accessed | tf_op | source)
XLA Modules:
  0.0 77.3 jit_solution(18193818996694760392)
XLA Ops:
  0.6 1.0 %copy-done.2 = f32[8,8,16,128]{3,2,1,0:T(8,128)S(1)} copy-done((f32[8,8,16,128]{3,2,1,0:T(8,128)S(1)}, f32[8,8,16,128]{3,2,1,0:T(8,128)}, u32[]{:S(2)}) %copy-start.2) | copy-done | bytes 524312
  1.9 3.3 %collective-permute-start.1 = (f32[128,128]{1,0:T(8,128)S(1)}, f32[128,128]{1,0:T(8,128)S(1)}, u32[]{:S(2)}, u32[]{:S(2)}) collective-permute-start(f32[128,128]{1,0:T(8,128)S(1)} %shard_map.41.packed_ref), channel_id=1, source_target_pairs={{16,0},{32,16},{48,32},{64,48},{80,64},{96,80},{112,96},{128,112},... | collective-permute-start | bytes 196616 | tf_op jit(solution)/shard_map/ppermute | solution.py:391
  5.2 1.4 %collective-permute-done.1.east_ref = f32[128,128]{1,0:T(8,128)S(1)} collective-permute-done((f32[128,128]{1,0:T(8,128)S(1)}, f32[128,128]{1,0:T(8,128)S(1)}, u32[]{:S(2)}, u32[]{:S(2)}) %collective-permute-start.1) | collective-permute-done | bytes 65568 | tf_op jit(solution)/shard_map/ppermute | solution.py:391
  6.6 0.8 %collective-permute-done.west_ref = f32[128,128]{1,0:T(8,128)S(1)} collective-permute-done((f32[128,128]{1,0:T(8,128)S(1)}, f32[128,128]{1,0:T(8,128)S(1)}, u32[]{:S(2)}, u32[]{:S(2)}) %collective-permute-start) | collective-permute-done | bytes 65568 | tf_op jit(solution)/shard_map/ppermute | solution.py:390
  7.5 3.5 %collective-permute-start.2 = (f32[4,64,128]{2,1,0:T(8,128)S(1)}, f32[4,64,128]{2,1,0:T(8,128)S(1)}, u32[]{:S(2)}, u32[]{:S(2)}) collective-permute-start(f32[4,64,128]{2,1,0:T(8,128)S(1)} %get-tuple-element.19), channel_id=1, source_target_pairs={{0,2},{2,4},{4,6},{6,8},{8,10},{10,12},{12,14},{1,3},{3,5},{5,7},{... | collective-permute-start | bytes 393224 | tf_op jit(solution)/shard_map/ppermute | solution.py:390
  11.1 1.3 %collective-permute-start.3 = (f32[4,64,128]{2,1,0:T(8,128)S(1)}, f32[4,64,128]{2,1,0:T(8,128)S(1)}, u32[]{:S(2)}, u32[]{:S(2)}) collective-permute-start(f32[4,64,128]{2,1,0:T(8,128)S(1)} %get-tuple-element.20), channel_id=1, source_target_pairs={{2,0},{4,2},{6,4},{8,6},{10,8},{12,10},{14,12},{3,1},{5,3},{7,5},{... | collective-permute-start | bytes 393224 | tf_op jit(solution)/shard_map/ppermute | solution.py:391
  12.4 3.6 %shard_map.43 = (bf16[192,8192]{1,0:T(8,128)(2,1)S(1)}, f32[64,64]{1,0:T(8,128)S(1)}) custom-call(f32[128,128]{1,0:T(8,128)S(1)} %get-tuple-element.16.order_ref.seam_ref, f32[64,128,128]{2,1,0:T(8,128)} %bitcast.3), custom_call_target="tpu_custom_call" | custom-call | flops 1000000 | bytes 8388608 | tf_op jit(solution)/shard_map/pallas_call | solution.py:415
  15.9 1.0 %collective-permute-done.3.north_ref = f32[4,64,128]{2,1,0:T(8,128)S(1)} collective-permute-done((f32[4,64,128]{2,1,0:T(8,128)S(1)}, f32[4,64,128]{2,1,0:T(8,128)S(1)}, u32[]{:S(2)}, u32[]{:S(2)}) %collective-permute-start.3) | collective-permute-done | bytes 131104 | tf_op jit(solution)/shard_map/ppermute | solution.py:391
  16.9 3.1 %shard_map.44 = (f32[8,64,128]{2,1,0:T(8,128)S(1)}, f32[8,64,128]{2,1,0:T(8,128)S(1)}) custom-call(f32[8,8,16,128]{3,2,1,0:T(8,128)S(1)} %copy-done.3, f32[128,128]{1,0:T(8,128)S(1)} %get-tuple-element.16.order_ref.seam_ref, f32[4,64,128]{2,1,0:T(8,128)S(1)} %collective-permute-done.2.south_ref, f32[4,64,128]{2,1,0:T(8,128)S(1)} %collective-permute-done.3.north_ref, ...), custom_call_target="tpu_custom_call" | custom-call | flops 1000000 | bytes 1000000 | tf_op jit(solution)/shard_map/pallas_call | solution.py:422
  20.1 2.7 %collective-permute-start.4 = (f32[8,64,128]{2,1,0:T(8,128)S(1)}, f32[8,64,128]{2,1,0:T(8,128)S(1)}, u32[]{:S(2)}, u32[]{:S(2)}) collective-permute-start(f32[8,64,128]{2,1,0:T(8,128)S(1)} %get-tuple-element.23.send_ref), channel_id=1, source_target_pairs={{0,1},{1,0},{2,3},{3,2},{4,5},{5,4},{6,7},{7,6},{8,9},{9,8},{10,11... | collective-permute-start | bytes 786440 | tf_op jit(solution)/shard_map/ppermute | solution.py:396
  22.8 1.9 %shard_map.46.order_ref.far_ref = bf16[128,8192]{1,0:T(8,128)(2,1)S(1)} custom-call(f32[8,64,128]{2,1,0:T(8,128)S(1)} %get-tuple-element.21.mine_ref.order_ref.keep_ref, f32[64,128,128]{2,1,0:T(8,128)} %bitcast.4), custom_call_target="tpu_custom_call" | custom-call | flops 1000000 | bytes 6291456 | tf_op jit(solution)/shard_map/pallas_call | solution.py:429
  24.7 2.2 %shard_map.45 = (f32[192,24]{1,0:T(8,128)S(1)}, f32[24,24]{1,0:T(8,128)S(1)}, bf16[24,8192]{1,0:T(8,128)(2,1)S(1)}) custom-call(bf16[192,8192]{1,0:T(8,128)(2,1)S(1)} %get-tuple-element.17.stack_ref.near_ref, f32[8,64,128]{2,1,0:T(8,128)S(1)} %get-tuple-element.21.mine_ref.order_ref.keep_ref), custom_call_target="tpu_custom_call" | custom-call | flops 1000000 | bytes 4194304 | tf_op jit(solution)/shard_map/pallas_call | solution.py:436
  26.9 2.6 %shard_map.47 = (f32[16,128]{1,0:T(8,128)S(1)}, f32[16,128]{1,0:T(8,128)S(1)}) custom-call(bf16[192,8192]{1,0:T(8,128)(2,1)S(1)} %get-tuple-element.17.stack_ref.near_ref, f32[64,64]{1,0:T(8,128)S(1)} %get-tuple-element.18.order_ref.gram_ref, bf16[24,8192]{1,0:T(8,128)(2,1)S(1)} %get-tuple-element.22.pieces_ref, ...), custom_call_target="tpu_custom_call" | custom-call | flops 1000000 | bytes 1000000 | tf_op jit(solution)/shard_map/pallas_call | solution.py:444
  29.6 7.5 %collective-permute-start.5 = (f32[16,128]{1,0:T(8,128)S(1)}, f32[16,128]{1,0:T(8,128)S(1)}, u32[]{:S(2)}, u32[]{:S(2)}) collective-permute-start(f32[16,128]{1,0:T(8,128)S(1)} %get-tuple-element.27), channel_id=1, source_target_pairs={{0,16},{16,0},{1,17},{17,1},{2,18},{18,2},{3,19},{19,3},{4,20},{20... | collective-permute-start | bytes 24584 | tf_op jit(solution)/shard_map/ppermute | solution.py:396
  37.1 0.8 %collective-permute-done.5.two_ref = f32[16,128]{1,0:T(8,128)S(1)} collective-permute-done((f32[16,128]{1,0:T(8,128)S(1)}, f32[16,128]{1,0:T(8,128)S(1)}, u32[]{:S(2)}, u32[]{:S(2)}) %collective-permute-start.5) | collective-permute-done | bytes 8224 | tf_op jit(solution)/shard_map/ppermute | solution.py:396
  38.6 4.2 %all-to-all-start = ((f32[16,16,128]{2,1,0:T(8,128)}), f32[16,16,128]{2,1,0:T(8,128)S(1)}, u32[]{:S(2)}, u32[]{:S(2)}) async-start(f32[16,16,128]{2,1,0:T(8,128)} %copy-done.6), calls=%async_computation | async-start | bytes 262144 | tf_op jit(solution)/shard_map/all_to_all | solution.py:400
  42.9 2.9 %collective-permute-start.6 = (f32[8,64,128]{2,1,0:T(8,128)S(1)}, f32[8,64,128]{2,1,0:T(8,128)}, u32[]{:S(2)}, u32[]{:S(2)}) collective-permute-start(f32[8,64,128]{2,1,0:T(8,128)S(1)} %get-tuple-element.21.mine_ref.order_ref.keep_ref), channel_id=1, source_target_pairs={{0,1},{1,0},{2,3},{3,2},{4,5},{5,4},{6,7},{7,6},{8,9},{9,8},{10,11... | collective-permute-start | bytes 786440 | tf_op jit(solution)/shard_map/ppermute | solution.py:396
  45.7 4.2 %all-to-all-done.parts_ref = f32[16,16,128]{2,1,0:T(8,128)S(1)} async-done(((f32[16,16,128]{2,1,0:T(8,128)}), f32[16,16,128]{2,1,0:T(8,128)S(1)}, u32[]{:S(2)}, u32[]{:S(2)}) %all-to-all-start) | async-done | bytes 131104 | tf_op jit(solution)/shard_map/all_to_all | solution.py:400
  50.0 17.3 %all_to_all.10.parts_ref = f32[16,16,128]{2,1,0:T(8,128)S(1)} all-to-all(f32[16,16,128]{2,1,0:T(8,128)S(1)} %shard_map.49), channel_id=1, replica_groups=mesh['pair'=8,'core'=2,'lat'=8,'tm'=2] {'core','lat'}, dimensions={0} | all-to-all | bytes 262144 | tf_op jit(solution)/shard_map/all_to_all | solution.py:400
  67.2 3.1 %shard_map.50 = (bf16[128,160]{1,0:T(8,128)(2,1)S(1)}, f32[8,64]{1,0:T(8,128)}) custom-call(f32[16,16,128]{2,1,0:T(8,128)S(1)} %all_to_all.10.parts_ref), custom_call_target="tpu_custom_call" | custom-call | flops 1000000 | bytes 1000000 | tf_op jit(solution)/shard_map/pallas_call | solution.py:452
  70.4 1.6 %copy-done.1 = bf16[128,8192]{1,0:T(8,128)(2,1)S(1)} copy-done((bf16[128,8192]{1,0:T(8,128)(2,1)S(1)}, bf16[128,8192]{1,0:T(8,128)(2,1)}, u32[]{:S(2)}) %copy-start.1) | copy-done | bytes 2097176
  72.0 0.9 %copy-done.5 = f32[8,64,128]{2,1,0:T(8,128)S(1)} copy-done((f32[8,64,128]{2,1,0:T(8,128)S(1)}, f32[8,64,128]{2,1,0:T(8,128)}, u32[]{:S(2)}) %copy-start.5) | copy-done | bytes 262168
  72.9 0.9 %copy-done.8 = f32[8,64,128]{2,1,0:T(8,128)S(1)} copy-done((f32[8,64,128]{2,1,0:T(8,128)S(1)}, f32[8,64,128]{2,1,0:T(8,128)}, u32[]{:S(2)}) %copy-start.8) | copy-done | bytes 262168
  73.9 3.4 %shard_map.51 = f32[64,128,128]{2,1,0:T(8,128)} custom-call(bf16[128,160]{1,0:T(8,128)(2,1)S(1)} %get-tuple-element.28.maps_ref, bf16[192,8192]{1,0:T(8,128)(2,1)S(1)} %get-tuple-element.17.stack_ref.near_ref, bf16[128,8192]{1,0:T(8,128)(2,1)S(1)} %copy-done.1, f32[8,64,128]{2,1,0:T(8,128)S(1)} %get-tuple-element.21.mine_ref.order_ref.keep_ref, ...), custom_call_target="tpu_custom_call" | custom-call | tf_op jit(solution)/shard_map/pallas_call | solution.py:456
  (22 shorter events, 1.0 us)
Async XLA Ops:
  0.6 1.0 %copy-start.2 = (f32[8,8,16,128]{3,2,1,0:T(8,128)S(1)}, f32[8,8,16,128]{3,2,1,0:T(8,128)}, u32[]{:S(2)}) copy-start(f32[8,8,16,128]{3,2,1,0:T(8,128)} %x_ref.5) | copy-start | bytes 1572868
  1.7 15.3 %copy-start.3 = (f32[8,8,16,128]{3,2,1,0:T(8,128)S(1)}, f32[8,8,16,128]{3,2,1,0:T(8,128)}, u32[]{:S(2)}) copy-start(f32[8,8,16,128]{3,2,1,0:T(8,128)} %x_ref.5) | copy-start | bytes 1572868
  1.9 4.7 %collective-permute-start.1 = (f32[128,128]{1,0:T(8,128)S(1)}, f32[128,128]{1,0:T(8,128)S(1)}, u32[]{:S(2)}, u32[]{:S(2)}) collective-permute-start(f32[128,128]{1,0:T(8,128)S(1)} %shard_map.41.packed_ref), channel_id=1, source_target_pairs={{16,0},{32,16},{48,32},{64,48},{80,64},{96,80},{112,96},{128,112},... | collective-permute-start | bytes 196616 | tf_op jit(solution)/shard_map/ppermute | solution.py:391
  5.2 2.3 %collective-permute-start = (f32[128,128]{1,0:T(8,128)S(1)}, f32[128,128]{1,0:T(8,128)S(1)}, u32[]{:S(2)}, u32[]{:S(2)}) collective-permute-start(f32[128,128]{1,0:T(8,128)S(1)} %shard_map.41.packed_ref), channel_id=1, source_target_pairs={{0,16},{16,32},{32,48},{48,64},{64,80},{80,96},{96,112},{112,128},... | collective-permute-start | bytes 196616 | tf_op jit(solution)/shard_map/ppermute | solution.py:390
  7.5 8.4 %collective-permute-start.2 = (f32[4,64,128]{2,1,0:T(8,128)S(1)}, f32[4,64,128]{2,1,0:T(8,128)S(1)}, u32[]{:S(2)}, u32[]{:S(2)}) collective-permute-start(f32[4,64,128]{2,1,0:T(8,128)S(1)} %get-tuple-element.19), channel_id=1, source_target_pairs={{0,2},{2,4},{4,6},{6,8},{8,10},{10,12},{12,14},{1,3},{3,5},{5,7},{... | collective-permute-start | bytes 393224 | tf_op jit(solution)/shard_map/ppermute | solution.py:390
  11.1 5.9 %collective-permute-start.3 = (f32[4,64,128]{2,1,0:T(8,128)S(1)}, f32[4,64,128]{2,1,0:T(8,128)S(1)}, u32[]{:S(2)}, u32[]{:S(2)}) collective-permute-start(f32[4,64,128]{2,1,0:T(8,128)S(1)} %get-tuple-element.20), channel_id=1, source_target_pairs={{2,0},{4,2},{6,4},{8,6},{10,8},{12,10},{14,12},{3,1},{5,3},{7,5},{... | collective-permute-start | bytes 393224 | tf_op jit(solution)/shard_map/ppermute | solution.py:391
  20.1 6.8 %copy-start.7 = (f32[8,64,128]{2,1,0:T(8,128)}, f32[8,64,128]{2,1,0:T(8,128)S(1)}, u32[]{:S(2)}) copy-start(f32[8,64,128]{2,1,0:T(8,128)S(1)} %get-tuple-element.23.send_ref) | copy-start | bytes 786436
  20.1 6.8 %collective-permute-start.4 = (f32[8,64,128]{2,1,0:T(8,128)S(1)}, f32[8,64,128]{2,1,0:T(8,128)S(1)}, u32[]{:S(2)}, u32[]{:S(2)}) collective-permute-start(f32[8,64,128]{2,1,0:T(8,128)S(1)} %get-tuple-element.23.send_ref), channel_id=1, source_target_pairs={{0,1},{1,0},{2,3},{3,2},{4,5},{5,4},{6,7},{7,6},{8,9},{9,8},{10,11... | collective-permute-start | bytes 786440 | tf_op jit(solution)/shard_map/ppermute | solution.py:396
  24.7 4.9 %copy-start = (bf16[128,8192]{1,0:T(8,128)(2,1)}, bf16[128,8192]{1,0:T(8,128)(2,1)S(1)}, u32[]{:S(2)}) copy-start(bf16[128,8192]{1,0:T(8,128)(2,1)S(1)} %shard_map.46.order_ref.far_ref) | copy-start | bytes 6291460
  26.9 2.7 %copy-start.4 = (f32[8,64,128]{2,1,0:T(8,128)}, f32[8,64,128]{2,1,0:T(8,128)S(1)}, u32[]{:S(2)}) copy-start(f32[8,64,128]{2,1,0:T(8,128)S(1)} %collective-permute-done.4.other_ref.here_ref) | copy-start | bytes 786436
  29.6 8.4 %collective-permute-start.5 = (f32[16,128]{1,0:T(8,128)S(1)}, f32[16,128]{1,0:T(8,128)S(1)}, u32[]{:S(2)}, u32[]{:S(2)}) collective-permute-start(f32[16,128]{1,0:T(8,128)S(1)} %get-tuple-element.27), channel_id=1, source_target_pairs={{0,16},{16,0},{1,17},{17,1},{2,18},{18,2},{3,19},{19,3},{4,20},{20... | collective-permute-start | bytes 24584 | tf_op jit(solution)/shard_map/ppermute | solution.py:396
  38.0 0.7 copy-start.6
  38.6 11.3 %all-to-all-start = ((f32[16,16,128]{2,1,0:T(8,128)}), f32[16,16,128]{2,1,0:T(8,128)S(1)}, u32[]{:S(2)}, u32[]{:S(2)}) async-start(f32[16,16,128]{2,1,0:T(8,128)} %copy-done.6), calls=%async_computation | async-start | bytes 262144 | tf_op jit(solution)/shard_map/all_to_all | solution.py:400
  42.9 27.5 %collective-permute-start.6 = (f32[8,64,128]{2,1,0:T(8,128)S(1)}, f32[8,64,128]{2,1,0:T(8,128)}, u32[]{:S(2)}, u32[]{:S(2)}) collective-permute-start(f32[8,64,128]{2,1,0:T(8,128)S(1)} %get-tuple-element.21.mine_ref.order_ref.keep_ref), channel_id=1, source_target_pairs={{0,1},{1,0},{2,3},{3,2},{4,5},{5,4},{6,7},{7,6},{8,9},{9,8},{10,11... | collective-permute-start | bytes 786440 | tf_op jit(solution)/shard_map/ppermute | solution.py:396
  70.4 1.6 %copy-start.1 = (bf16[128,8192]{1,0:T(8,128)(2,1)S(1)}, bf16[128,8192]{1,0:T(8,128)(2,1)}, u32[]{:S(2)}) copy-start(bf16[128,8192]{1,0:T(8,128)(2,1)} %copy-done) | copy-start | bytes 6291460
  72.0 0.9 %copy-start.5 = (f32[8,64,128]{2,1,0:T(8,128)S(1)}, f32[8,64,128]{2,1,0:T(8,128)}, u32[]{:S(2)}) copy-start(f32[8,64,128]{2,1,0:T(8,128)} %copy-done.4) | copy-start | bytes 786436
  72.9 0.9 %copy-start.8 = (f32[8,64,128]{2,1,0:T(8,128)S(1)}, f32[8,64,128]{2,1,0:T(8,128)}, u32[]{:S(2)}) copy-start(f32[8,64,128]{2,1,0:T(8,128)} %copy-done.7) | copy-start | bytes 786436

commit v5 on v4

--- a/solution.py
+++ b/solution.py
@@ -62,25 +62,29 @@
         packed_ref[pl.ds(ROWS * snap, ROWS), :] = packed
 
 
-def seam_kernel(x_ref, packed_ref, west_ref, east_ref, seam_ref, low_ref, high_ref):
+def seam_kernel(x_ref, packed_ref, across_ref, beside_ref, seam_ref, one_ref, two_ref):
     packed = packed_ref[...]
     lane = lanes_of(packed.shape) % 16
-    west = jnp.where(lane < 3, west_ref[...] - packed, 0.0)
-    east = pltpu.roll(jnp.where((lane >= 3) & (lane < 6), east_ref[...] - packed, 0.0), 8, 1)
+    eastern = lax.axis_index("core") == 1
+    far, near = across_ref[...] - packed, beside_ref[...] - packed
+    west = jnp.where(lane < 3, jnp.where(eastern, near, far), 0.0)
+    east = pltpu.roll(jnp.where((lane >= 3) & (lane < 6), jnp.where(eastern, far, near), 0.0), 8, 1)
     seam_ref[...] = west + east
+    even = lax.axis_index("lat") % 2 == 0
     for snap in range(SNAPS):
         at = pl.ds(8 * snap, 8)
         low = jnp.swapaxes(x_ref[snap, :, pl.ds(0, 8), :], 0, 1)
         high = jnp.swapaxes(x_ref[snap, :, pl.ds(8, 8), :], 0, 1)
-        for row in range(3):
-            low_ref[row, at, :] = low[row]
-            high_ref[row, at, :] = high[5 + row]
-        low_ref[3, at, :] = seam_ref[pl.ds(ROWS * snap, 8), :]
-        high_ref[3, at, :] = seam_ref[pl.ds(ROWS * snap + 8, 8), :]
-
-
-def smooth_kernel(x_ref, seam_ref, south_ref, north_ref, order_ref, keep_ref, send_ref, done):
+        rows = [(low[row], high[5 + row]) for row in range(3)]
+        rows.append((seam_ref[pl.ds(ROWS * snap, 8), :], seam_ref[pl.ds(ROWS * snap + 8, 8), :]))
+        for row, (low, high) in enumerate(rows):
+            one_ref[row, at, :] = jnp.where(even, high, low)
+            two_ref[row, at, :] = jnp.where(even, low, high)
+
+
+def smooth_kernel(x_ref, seam_ref, one_ref, two_ref, order_ref, keep_ref, send_ref, done):
     lat = lax.axis_index("lat")
+    even = lat % 2 == 0
     not_first = jnp.where(lat == 0, 0, 1)
     not_last = jnp.where(lat == lax.axis_size("lat") - 1, 0, 1)
     row = lax.broadcasted_iota(jnp.int32, (8, LANES), 0)
@@ -95,11 +99,12 @@
         return near[0:8], near[8:16], near[16:24]
 
     def snapshot(snap, carry):
+        at = pl.ds(pl.multiple_of(8 * snap, 8), 8)
         edges = jnp.swapaxes(
             jnp.stack(
-                [north_ref[i, pl.ds(8 * snap, 8), :] for i in range(3)]
+                [jnp.where(even, one_ref[i, at, :], two_ref[i, at, :]) for i in range(3)]
                 + [zero, zero]
-                + [south_ref[i, pl.ds(8 * snap, 8), :] for i in range(3)]
+                + [jnp.where(even, two_ref[i, at, :], one_ref[i, at, :]) for i in range(3)]
             ),
             0,
             1,
@@ -108,11 +113,10 @@
             (x_ref[snap, level, pl.ds(0, 8), :], x_ref[snap, level, pl.ds(8, 8), :], edges[level])
             for level in range(LEVELS)
         ]
-        at = pl.ds(pl.multiple_of(8 * snap, 8), 8)
         seam = (
             seam_ref[pl.ds(pl.multiple_of(ROWS * snap, 8), 8), :],
             seam_ref[pl.ds(pl.multiple_of(ROWS * snap + 8, 8), 8), :],
-            jnp.where(row < 4, north_ref[3, at, :], south_ref[3, at, :]),
+            jnp.where((row < 4) == even, one_ref[3, at, :], two_ref[3, at, :]),
         )
         for sweep in range(3):
             tiles = 3 if sweep < 2 else 2
@@ -242,23 +246,16 @@
 
 
 def snapshot_gram_kernel(
-    stack_ref, gram_ref, pieces_ref, other_ref, cross_ref, square_ref, order_ref, own_ref, partner_ref, joined
+    stack_ref, gram_ref, pieces_ref, other_ref, cross_ref, square_ref, order_ref, own_ref, partner_ref, columns, joined
 ):
-    def block(step, carry):
-        cross, square, mixed = carry
-        start = pl.multiple_of(CHUNK * step, CHUNK)
-        other = snapshot_columns(other_ref, start, 3)
-        other = jnp.concatenate([jnp.concatenate(c, axis=0) for c in other], axis=1)
-        width = CHUNK * LANES
-        at = pl.ds(pl.multiple_of(width * step, width), width)
-        return (
-            cross + transposed_product(stack_ref[:, at], other),
-            square + transposed_product(other, other),
-            mixed + transposed_product(pieces_ref[:, at], other),
+    for step in range(HALF_ROWS // CHUNK):
+        other = snapshot_columns(other_ref, CHUNK * step, 3)
+        columns[:, pl.ds(CHUNK * LANES * step, CHUNK * LANES)] = jnp.concatenate(
+            [jnp.concatenate(c, axis=0) for c in other], axis=1
         )
-
-    zeros = (jnp.zeros((192, 24), F32), jnp.zeros((24, 24), F32), jnp.zeros((24, 24), F32))
-    cross, square, mixed = lax.fori_loop(0, HALF_ROWS // CHUNK, block, zeros)
+    cross = transposed_product(stack_ref[...], columns[...])
+    square = transposed_product(columns[...], columns[...])
+    mixed = transposed_product(pieces_ref[...], columns[...])
     mixed = folded(mixed, 8)
     projection = jnp.concatenate(in_order(folded(cross_ref[...], 64), folded(cross, 64)), axis=1)
     early, late = in_order(folded(square_ref[...], 8), folded(square, 8))
@@ -329,7 +326,12 @@
         rows = [lower[0][k : k + 1, :] for k in range(8)]
         for k in range(8):
             pivot = columns[k][0][k : k + 1, :]
-            inverse = 1.0 / pivot
+            if k % 2 == 0:
+                corner, upper, side = columns[k + 1][0][k + 1 : k + 2, :], columns[k + 1][0][k : k + 1, :], columns[k][0][k + 1 : k + 2, :]
+                inverse = 1.0 / pivot
+                following = pivot * (1.0 / (pivot * corner - upper * side))
+            else:
+                inverse = following
             factors = [c * inverse for c in columns[k]]
             for m in range(k + 1, 8):
                 entry = columns[m][0][k : k + 1, :]
@@ -384,12 +386,10 @@
         copy.wait()
 
 
-def neighbours(values_up, values_down, axis, closed):
+def swapped(values, axis, first):
     count = lax.axis_size(axis)
-    ends = count if closed else count - 1
-    from_below = lax.ppermute(values_up, axis, [(i, (i + 1) % count) for i in range(ends)])
-    from_above = lax.ppermute(values_down, axis, [((i + 1) % count, i) for i in range(ends)])
-    return from_below, from_above
+    pairs = [(i, (i + 1) % count) for i in range(first, count - first % 2 * (axis == "lat"), 2)]
+    return lax.ppermute(values, axis, [p for one, two in pairs for p in ((one, two), (two, one))])
 
 
 def across(values, axis):
@@ -406,11 +406,12 @@
     q = pltpu.with_memory_space_constraint(basis.reshape(EOFS, CELL_ROWS, LANES), pltpu.HBM)
 
     packed = call(pack_kernel, [VMEM], shape(CELL_ROWS, LANES))(snapshots)
-    west, east = neighbours(packed, packed, LON, True)
-    seam, low, high = call(
+    chip = swapped(packed, LON, 1)
+    beside = across(packed, "core")
+    seam, one, two = call(
         seam_kernel, [VMEM] * 4, (shape(CELL_ROWS, LANES), shape(4, 64, LANES), shape(4, 64, LANES))
-    )(snapshots, packed, west, east)
-    south, north = neighbours(high, low, "lat", False)
+    )(snapshots, packed, chip, beside)
+    one, two = swapped(one, "lat", 0), swapped(two, "lat", 1)
     parts = HALF_ROWS // QROWS
     stack, gram = call(
         basis_gram_kernel,
@@ -424,7 +425,7 @@
         [VMEM] * 5,
         (shape(SNAPS, HALF_ROWS, LANES),) * 2,
         [pltpu.VMEM((SNAPS, CELL_ROWS, LANES), F32)],
-    )(snapshots, seam, south, north, gram)
+    )(snapshots, seam, one, two, gram)
     here = across(send, "tm")
     far = call(
         basis_stack_kernel,
@@ -442,7 +443,7 @@
     side = shape(SIDE, LANES)
     late = across(keep, "tm")
     mine, theirs = call(
-        snapshot_gram_kernel, [VMEM] * 7, (side, side), [pltpu.VMEM((PAYLOAD, LANES), F32)]
+        snapshot_gram_kernel, [VMEM] * 7, (side, side), [pltpu.VMEM((24, HALF_CELLS), BF16), pltpu.VMEM((PAYLOAD, LANES), F32)]
     )(stack, gram, split, here, cross, square, far)
     group = lax.axis_size(("pair", "tm"))
     spread = call(pair_kernel, [VMEM] * 2, shape(group, SIDE, LANES))(mine, across(theirs, "core"))

time: 77.7 us -> 75.4 us (0.970)
  starting transfers between devices: 25.5 us -> 20.6 us
  blocking collectives: 17.3 us -> 20.7 us
  Pallas kernels: 20.2 us -> 18.9 us
    ppermute x4 -> x3, starting transfers between devices: 8.12 us -> 0.76 us  [swapped(): lax.ppermute(values, axis, [p for one, two in pairs for p in ((one, two),...]
    all_to_all x1, blocking collectives: 17.3 us -> 20.7 us  [gathered(): return lax.all_to_all(values, axes, 0, 0)]
    all_to_all x1, starting transfers between devices: 4.23 us -> 6.82 us  [gathered(): return lax.all_to_all(values, axes, 0, 0)]
    pallas_call x1, Pallas kernels: 2.65 us -> 1.52 us  [update(): call(snapshot_gram_kernel, [VMEM] * 7, (side, side), [pltpu.VMEM((24, HAL...]
    ppermute x3 -> x4, waiting for transfers between devices: 0.86 us -> 1.73 us  [across(): return lax.ppermute(values, axis, [(0, 1), (1, 0)])]
    ppermute x4 -> x3, waiting for transfers between devices: 3.27 us -> 2.79 us  [swapped(): lax.ppermute(values, axis, [p for one, two in pairs for p in ((one, two),...]
    ppermute x3 -> x4, starting transfers between devices: 13.1 us -> 13 us  [across(): return lax.ppermute(values, axis, [(0, 1), (1, 0)])]
  transfers between devices with their start and end apart: 8 -> 8, of which waited for: 5 -> 4; matrix products, arithmetic and copies ran while one was open for 0% -> 0% of each run, Pallas kernels for 14% -> 14%
where the time goes in v5:
time: 75.4 us; the launch traced here: 74.9 us
  blocking collectives  20.7 us (27%)
  starting transfers between devices  20.6 us (27%)
  Pallas kernels  18.9 us (25%)
  waiting for transfers between devices  8.73 us (12%)
  local copies, waits for them, and re-layouts  5.2 us (7%)
  between operations  0.81 us (1%)
    all_to_all x1, blocking collectives, gathered(): return lax.all_to_all(values, axes, 0, 0)  20.7 us
    ppermute x4, starting transfers between devices, across(): return lax.ppermute(values, axis, [(0, 1), (1, 0)])  13 us
    all_to_all x1, starting transfers between devices, gathered(): return lax.all_to_all(values, axes, 0, 0)  6.82 us
    unnamed x18, local copies, waits for them, and re-layouts  5.2 us
    all_to_all x1, waiting for transfers between devices, gathered(): return lax.all_to_all(values, axes, 0, 0)  4.2 us
    pallas_call x1, Pallas kernels, update(): call(basis_gram_kernel, [VMEM, ANY], (shape(3 * EOFS, HALF_CELLS, dtype=B...  3.56 us
    pallas_call x1, Pallas kernels, update(): pl.pallas_call(final_kernel, out_shape=shape(EOFS, CELL_ROWS, LANES), in_...  3.37 us
    pallas_call x1, Pallas kernels, update(): call(smooth_kernel, [VMEM] * 5, (shape(SNAPS, HALF_ROWS, LANES),) * 2, [p...  3.13 us
  transfers between devices with their start and end apart: 8, of which 4 were waited for; matrix products, arithmetic and copies ran while one was open for 0% of the time, Pallas kernels for 14%

profile of v5, /device:TPU:1, one launch (start us, length us, event | category | flops | bytes accessed | tf_op | source)
XLA Modules:
  0.0 74.9 jit_solution(16430916221288360894)
XLA Ops:
  0.6 1.0 %copy-done.2 = f32[8,8,16,128]{3,2,1,0:T(8,128)S(1)} copy-done((f32[8,8,16,128]{3,2,1,0:T(8,128)S(1)}, f32[8,8,16,128]{3,2,1,0:T(8,128)}, u32[]{:S(2)}) %copy-start.2) | copy-done | bytes 524312
  1.7 0.2 shard_map.41.packed_ref
  1.9 3.3 %collective-permute-start.1 = (f32[128,128]{1,0:T(8,128)S(1)}, f32[128,128]{1,0:T(8,128)S(1)}, u32[]{:S(2)}, u32[]{:S(2)}) collective-permute-start(f32[128,128]{1,0:T(8,128)S(1)} %shard_map.41.packed_ref), channel_id=1, source_target_pairs={{0,16},{16,0},{1,17},{17,1},{2,18},{18,2},{3,19},{19,3},{4,20},{20... | collective-permute-start | bytes 196616 | tf_op jit(solution)/shard_map/ppermute | solution.py:396
  5.2 0.9 %collective-permute-done.1.beside_ref = f32[128,128]{1,0:T(8,128)S(1)} collective-permute-done((f32[128,128]{1,0:T(8,128)S(1)}, f32[128,128]{1,0:T(8,128)S(1)}, u32[]{:S(2)}, u32[]{:S(2)}) %collective-permute-start.1) | collective-permute-done | bytes 65568 | tf_op jit(solution)/shard_map/ppermute | solution.py:396
  6.1 2.8 %collective-permute-done.across_ref = f32[128,128]{1,0:T(8,128)S(1)} collective-permute-done((f32[128,128]{1,0:T(8,128)S(1)}, f32[128,128]{1,0:T(8,128)S(1)}, u32[]{:S(2)}, u32[]{:S(2)}) %collective-permute-start) | collective-permute-done | bytes 65568 | tf_op jit(solution)/shard_map/ppermute | solution.py:392
  9.1 0.7 collective-permute-start.3
  9.7 3.6 %shard_map.43 = (bf16[192,8192]{1,0:T(8,128)(2,1)S(1)}, f32[64,64]{1,0:T(8,128)S(1)}) custom-call(f32[128,128]{1,0:T(8,128)S(1)} %get-tuple-element.16.order_ref.seam_ref, f32[64,128,128]{2,1,0:T(8,128)} %bitcast.3), custom_call_target="tpu_custom_call" | custom-call | flops 1000000 | bytes 8388608 | tf_op jit(solution)/shard_map/pallas_call | solution.py:416
  13.3 3.1 %shard_map.44 = (f32[8,64,128]{2,1,0:T(8,128)S(1)}, f32[8,64,128]{2,1,0:T(8,128)S(1)}) custom-call(f32[8,8,16,128]{3,2,1,0:T(8,128)S(1)} %copy-done.3, f32[128,128]{1,0:T(8,128)S(1)} %get-tuple-element.16.order_ref.seam_ref, f32[4,64,128]{2,1,0:T(8,128)S(1)} %collective-permute-done.2.one_ref, f32[4,64,128]{2,1,0:T(8,128)S(1)} %collective-permute-done.3.two_ref, ...), custom_call_target="tpu_custom_call" | custom-call | flops 1000000 | bytes 1000000 | tf_op jit(solution)/shard_map/pallas_call | solution.py:423
  16.5 2.9 %collective-permute-start.4 = (f32[8,64,128]{2,1,0:T(8,128)S(1)}, f32[8,64,128]{2,1,0:T(8,128)S(1)}, u32[]{:S(2)}, u32[]{:S(2)}) collective-permute-start(f32[8,64,128]{2,1,0:T(8,128)S(1)} %get-tuple-element.23.send_ref), channel_id=1, source_target_pairs={{0,1},{1,0},{2,3},{3,2},{4,5},{5,4},{6,7},{7,6},{8,9},{9,8},{10,11... | collective-permute-start | bytes 786440 | tf_op jit(solution)/shard_map/ppermute | solution.py:396
  19.4 1.9 %shard_map.46.order_ref.far_ref = bf16[128,8192]{1,0:T(8,128)(2,1)S(1)} custom-call(f32[8,64,128]{2,1,0:T(8,128)S(1)} %get-tuple-element.21.mine_ref.order_ref.keep_ref, f32[64,128,128]{2,1,0:T(8,128)} %bitcast.4), custom_call_target="tpu_custom_call" | custom-call | flops 1000000 | bytes 6291456 | tf_op jit(solution)/shard_map/pallas_call | solution.py:430
  21.3 2.2 %shard_map.45 = (f32[192,24]{1,0:T(8,128)S(1)}, f32[24,24]{1,0:T(8,128)S(1)}, bf16[24,8192]{1,0:T(8,128)(2,1)S(1)}) custom-call(bf16[192,8192]{1,0:T(8,128)(2,1)S(1)} %get-tuple-element.17.stack_ref.near_ref, f32[8,64,128]{2,1,0:T(8,128)S(1)} %get-tuple-element.21.mine_ref.order_ref.keep_ref), custom_call_target="tpu_custom_call" | custom-call | flops 1000000 | bytes 4194304 | tf_op jit(solution)/shard_map/pallas_call | solution.py:437
  23.5 1.5 %shard_map.47 = (f32[16,128]{1,0:T(8,128)S(1)}, f32[16,128]{1,0:T(8,128)S(1)}) custom-call(bf16[192,8192]{1,0:T(8,128)(2,1)S(1)} %get-tuple-element.17.stack_ref.near_ref, f32[64,64]{1,0:T(8,128)S(1)} %get-tuple-element.18.order_ref.gram_ref, bf16[24,8192]{1,0:T(8,128)(2,1)S(1)} %get-tuple-element.22.pieces_ref, ...), custom_call_target="tpu_custom_call" | custom-call | flops 1000000 | bytes 1000000 | tf_op jit(solution)/shard_map/pallas_call | solution.py:445
  25.1 3.9 %collective-permute-start.5 = (f32[16,128]{1,0:T(8,128)S(1)}, f32[16,128]{1,0:T(8,128)S(1)}, u32[]{:S(2)}, u32[]{:S(2)}) collective-permute-start(f32[16,128]{1,0:T(8,128)S(1)} %get-tuple-element.27), channel_id=1, source_target_pairs={{0,16},{16,0},{1,17},{17,1},{2,18},{18,2},{3,19},{19,3},{4,20},{20... | collective-permute-start | bytes 24584 | tf_op jit(solution)/shard_map/ppermute | solution.py:396
  29.0 0.8 %collective-permute-done.5.two_ref = f32[16,128]{1,0:T(8,128)S(1)} collective-permute-done((f32[16,128]{1,0:T(8,128)S(1)}, f32[16,128]{1,0:T(8,128)S(1)}, u32[]{:S(2)}, u32[]{:S(2)}) %collective-permute-start.5) | collective-permute-done | bytes 8224 | tf_op jit(solution)/shard_map/ppermute | solution.py:396
  29.8 0.6 copy-done.6
  30.5 6.8 %all-to-all-start = ((f32[16,16,128]{2,1,0:T(8,128)}), f32[16,16,128]{2,1,0:T(8,128)S(1)}, u32[]{:S(2)}, u32[]{:S(2)}) async-start(f32[16,16,128]{2,1,0:T(8,128)} %copy-done.6), calls=%async_computation | async-start | bytes 262144 | tf_op jit(solution)/shard_map/all_to_all | solution.py:400
  37.3 2.9 %collective-permute-start.6 = (f32[8,64,128]{2,1,0:T(8,128)S(1)}, f32[8,64,128]{2,1,0:T(8,128)}, u32[]{:S(2)}, u32[]{:S(2)}) collective-permute-start(f32[8,64,128]{2,1,0:T(8,128)S(1)} %get-tuple-element.21.mine_ref.order_ref.keep_ref), channel_id=1, source_target_pairs={{0,1},{1,0},{2,3},{3,2},{4,5},{5,4},{6,7},{7,6},{8,9},{9,8},{10,11... | collective-permute-start | bytes 786440 | tf_op jit(solution)/shard_map/ppermute | solution.py:396
  40.2 4.2 %all-to-all-done.parts_ref = f32[16,16,128]{2,1,0:T(8,128)S(1)} async-done(((f32[16,16,128]{2,1,0:T(8,128)}), f32[16,16,128]{2,1,0:T(8,128)S(1)}, u32[]{:S(2)}, u32[]{:S(2)}) %all-to-all-start) | async-done | bytes 131104 | tf_op jit(solution)/shard_map/all_to_all | solution.py:400
  44.4 20.7 %all_to_all.10.parts_ref = f32[16,16,128]{2,1,0:T(8,128)S(1)} all-to-all(f32[16,16,128]{2,1,0:T(8,128)S(1)} %shard_map.49), channel_id=1, replica_groups=mesh['pair'=8,'core'=2,'lat'=8,'tm'=2] {'core','lat'}, dimensions={0} | all-to-all | bytes 262144 | tf_op jit(solution)/shard_map/all_to_all | solution.py:400
  65.1 2.9 %shard_map.50 = (bf16[128,160]{1,0:T(8,128)(2,1)S(1)}, f32[8,64]{1,0:T(8,128)}) custom-call(f32[16,16,128]{2,1,0:T(8,128)S(1)} %all_to_all.10.parts_ref), custom_call_target="tpu_custom_call" | custom-call | flops 1000000 | bytes 1000000 | tf_op jit(solution)/shard_map/pallas_call | solution.py:453
  68.1 1.6 %copy-done.1 = bf16[128,8192]{1,0:T(8,128)(2,1)S(1)} copy-done((bf16[128,8192]{1,0:T(8,128)(2,1)S(1)}, bf16[128,8192]{1,0:T(8,128)(2,1)}, u32[]{:S(2)}) %copy-start.1) | copy-done | bytes 2097176
  69.7 0.9 %copy-done.5 = f32[8,64,128]{2,1,0:T(8,128)S(1)} copy-done((f32[8,64,128]{2,1,0:T(8,128)S(1)}, f32[8,64,128]{2,1,0:T(8,128)}, u32[]{:S(2)}) %copy-start.5) | copy-done | bytes 262168
  70.6 0.9 %copy-done.8 = f32[8,64,128]{2,1,0:T(8,128)S(1)} copy-done((f32[8,64,128]{2,1,0:T(8,128)S(1)}, f32[8,64,128]{2,1,0:T(8,128)}, u32[]{:S(2)}) %copy-start.8) | copy-done | bytes 262168
  71.6 3.4 %shard_map.51 = f32[64,128,128]{2,1,0:T(8,128)} custom-call(bf16[128,160]{1,0:T(8,128)(2,1)S(1)} %get-tuple-element.28.maps_ref, bf16[192,8192]{1,0:T(8,128)(2,1)S(1)} %get-tuple-element.17.stack_ref.near_ref, bf16[128,8192]{1,0:T(8,128)(2,1)S(1)} %copy-done.1, f32[8,64,128]{2,1,0:T(8,128)S(1)} %get-tuple-element.21.mine_ref.order_ref.keep_ref, ...), custom_call_target="tpu_custom_call" | custom-call | tf_op jit(solution)/shard_map/pallas_call | solution.py:457
  (22 shorter events, 0.3 us)
Async XLA Ops:
  0.6 1.0 %copy-start.2 = (f32[8,8,16,128]{3,2,1,0:T(8,128)S(1)}, f32[8,8,16,128]{3,2,1,0:T(8,128)}, u32[]{:S(2)}) copy-start(f32[8,8,16,128]{3,2,1,0:T(8,128)} %x_ref.5) | copy-start | bytes 1572868
  1.7 11.6 %copy-start.3 = (f32[8,8,16,128]{3,2,1,0:T(8,128)S(1)}, f32[8,8,16,128]{3,2,1,0:T(8,128)}, u32[]{:S(2)}) copy-start(f32[8,8,16,128]{3,2,1,0:T(8,128)} %x_ref.5) | copy-start | bytes 1572868
  1.9 4.2 %collective-permute-start.1 = (f32[128,128]{1,0:T(8,128)S(1)}, f32[128,128]{1,0:T(8,128)S(1)}, u32[]{:S(2)}, u32[]{:S(2)}) collective-permute-start(f32[128,128]{1,0:T(8,128)S(1)} %shard_map.41.packed_ref), channel_id=1, source_target_pairs={{0,16},{16,0},{1,17},{17,1},{2,18},{18,2},{3,19},{19,3},{4,20},{20... | collective-permute-start | bytes 196616 | tf_op jit(solution)/shard_map/ppermute | solution.py:396
  5.2 3.7 %collective-permute-start = (f32[128,128]{1,0:T(8,128)S(1)}, f32[128,128]{1,0:T(8,128)S(1)}, u32[]{:S(2)}, u32[]{:S(2)}) collective-permute-start(f32[128,128]{1,0:T(8,128)S(1)} %shard_map.41.packed_ref), channel_id=1, source_target_pairs={{16,32},{32,16},{48,64},{64,48},{80,96},{96,80},{112,128},{128,112... | collective-permute-start | bytes 196616 | tf_op jit(solution)/shard_map/ppermute | solution.py:392
  9.0 4.3 %collective-permute-start.2 = (f32[4,64,128]{2,1,0:T(8,128)S(1)}, f32[4,64,128]{2,1,0:T(8,128)S(1)}, u32[]{:S(2)}, u32[]{:S(2)}) collective-permute-start(f32[4,64,128]{2,1,0:T(8,128)S(1)} %get-tuple-element.19), channel_id=1, source_target_pairs={{0,2},{2,0},{4,6},{6,4},{8,10},{10,8},{12,14},{14,12},{1,3},{3,1},... | collective-permute-start | bytes 393224 | tf_op jit(solution)/shard_map/ppermute | solution.py:392
  9.1 4.3 %collective-permute-start.3 = (f32[4,64,128]{2,1,0:T(8,128)S(1)}, f32[4,64,128]{2,1,0:T(8,128)S(1)}, u32[]{:S(2)}, u32[]{:S(2)}) collective-permute-start(f32[4,64,128]{2,1,0:T(8,128)S(1)} %get-tuple-element.20), channel_id=1, source_target_pairs={{2,4},{4,2},{6,8},{8,6},{10,12},{12,10},{3,5},{5,3},{7,9},{9,7},{1... | collective-permute-start | bytes 393224 | tf_op jit(solution)/shard_map/ppermute | solution.py:392
  16.5 7.0 %copy-start.7 = (f32[8,64,128]{2,1,0:T(8,128)}, f32[8,64,128]{2,1,0:T(8,128)S(1)}, u32[]{:S(2)}) copy-start(f32[8,64,128]{2,1,0:T(8,128)S(1)} %get-tuple-element.23.send_ref) | copy-start | bytes 786436
  16.5 7.0 %collective-permute-start.4 = (f32[8,64,128]{2,1,0:T(8,128)S(1)}, f32[8,64,128]{2,1,0:T(8,128)S(1)}, u32[]{:S(2)}, u32[]{:S(2)}) collective-permute-start(f32[8,64,128]{2,1,0:T(8,128)S(1)} %get-tuple-element.23.send_ref), channel_id=1, source_target_pairs={{0,1},{1,0},{2,3},{3,2},{4,5},{5,4},{6,7},{7,6},{8,9},{9,8},{10,11... | collective-permute-start | bytes 786440 | tf_op jit(solution)/shard_map/ppermute | solution.py:396
  21.3 3.8 %copy-start = (bf16[128,8192]{1,0:T(8,128)(2,1)}, bf16[128,8192]{1,0:T(8,128)(2,1)S(1)}, u32[]{:S(2)}) copy-start(bf16[128,8192]{1,0:T(8,128)(2,1)S(1)} %shard_map.46.order_ref.far_ref) | copy-start | bytes 6291460
  23.5 1.6 %copy-start.4 = (f32[8,64,128]{2,1,0:T(8,128)}, f32[8,64,128]{2,1,0:T(8,128)S(1)}, u32[]{:S(2)}) copy-start(f32[8,64,128]{2,1,0:T(8,128)S(1)} %collective-permute-done.4.other_ref.here_ref) | copy-start | bytes 786436
  25.1 4.7 %collective-permute-start.5 = (f32[16,128]{1,0:T(8,128)S(1)}, f32[16,128]{1,0:T(8,128)S(1)}, u32[]{:S(2)}, u32[]{:S(2)}) collective-permute-start(f32[16,128]{1,0:T(8,128)S(1)} %get-tuple-element.27), channel_id=1, source_target_pairs={{0,16},{16,0},{1,17},{17,1},{2,18},{18,2},{3,19},{19,3},{4,20},{20... | collective-permute-start | bytes 24584 | tf_op jit(solution)/shard_map/ppermute | solution.py:396
  29.8 0.7 copy-start.6
  30.5 13.9 %all-to-all-start = ((f32[16,16,128]{2,1,0:T(8,128)}), f32[16,16,128]{2,1,0:T(8,128)S(1)}, u32[]{:S(2)}, u32[]{:S(2)}) async-start(f32[16,16,128]{2,1,0:T(8,128)} %copy-done.6), calls=%async_computation | async-start | bytes 262144 | tf_op jit(solution)/shard_map/all_to_all | solution.py:400
  37.3 30.8 %collective-permute-start.6 = (f32[8,64,128]{2,1,0:T(8,128)S(1)}, f32[8,64,128]{2,1,0:T(8,128)}, u32[]{:S(2)}, u32[]{:S(2)}) collective-permute-start(f32[8,64,128]{2,1,0:T(8,128)S(1)} %get-tuple-element.21.mine_ref.order_ref.keep_ref), channel_id=1, source_target_pairs={{0,1},{1,0},{2,3},{3,2},{4,5},{5,4},{6,7},{7,6},{8,9},{9,8},{10,11... | collective-permute-start | bytes 786440 | tf_op jit(solution)/shard_map/ppermute | solution.py:396
  68.1 1.6 %copy-start.1 = (bf16[128,8192]{1,0:T(8,128)(2,1)S(1)}, bf16[128,8192]{1,0:T(8,128)(2,1)}, u32[]{:S(2)}) copy-start(bf16[128,8192]{1,0:T(8,128)(2,1)} %copy-done) | copy-start | bytes 6291460
  69.7 0.9 %copy-start.5 = (f32[8,64,128]{2,1,0:T(8,128)S(1)}, f32[8,64,128]{2,1,0:T(8,128)}, u32[]{:S(2)}) copy-start(f32[8,64,128]{2,1,0:T(8,128)} %copy-done.4) | copy-start | bytes 786436
  70.6 0.9 %copy-start.8 = (f32[8,64,128]{2,1,0:T(8,128)S(1)}, f32[8,64,128]{2,1,0:T(8,128)}, u32[]{:S(2)}) copy-start(f32[8,64,128]{2,1,0:T(8,128)} %copy-done.7) | copy-start | bytes 786436

commit v6 on v5

--- a/solution.py
+++ b/solution.py
@@ -52,9 +52,13 @@
     )
 
 
-def pack_kernel(x_ref, packed_ref):
+def pack_kernel(fields_ref, packed_ref, x_ref, sems):
+    copies = [pltpu.make_async_copy(fields_ref.at[snap], x_ref.at[snap], sems.at[snap]) for snap in range(SNAPS)]
+    for copy in copies:
+        copy.start()
     lane = lanes_of((ROWS, LANES))
-    for snap in range(SNAPS):
+    for snap, copy in enumerate(copies):
+        copy.wait()
         packed = jnp.zeros((ROWS, LANES), F32)
         for level in range(LEVELS):
             turned = pltpu.roll(x_ref[snap, level], 16 * level + 3, 1)
@@ -75,14 +79,17 @@
         at = pl.ds(8 * snap, 8)
         low = jnp.swapaxes(x_ref[snap, :, pl.ds(0, 8), :], 0, 1)
         high = jnp.swapaxes(x_ref[snap, :, pl.ds(8, 8), :], 0, 1)
-        rows = [(low[row], high[5 + row]) for row in range(3)]
-        rows.append((seam_ref[pl.ds(ROWS * snap, 8), :], seam_ref[pl.ds(ROWS * snap + 8, 8), :]))
-        for row, (low, high) in enumerate(rows):
-            one_ref[row, at, :] = jnp.where(even, high, low)
-            two_ref[row, at, :] = jnp.where(even, low, high)
-
-
-def smooth_kernel(x_ref, seam_ref, one_ref, two_ref, order_ref, keep_ref, send_ref, done):
+        for row in range(3):
+            one_ref[8 * row + snap] = jnp.where(even, high[5 + row], low[row])
+            two_ref[8 * row + snap] = jnp.where(even, low[row], high[5 + row])
+    low = jnp.swapaxes(jnp.stack([seam_ref[pl.ds(ROWS * snap, 8), :] for snap in range(SNAPS)]), 0, 1)
+    high = jnp.swapaxes(jnp.stack([seam_ref[pl.ds(ROWS * snap + 8, 8), :] for snap in range(SNAPS)]), 0, 1)
+    for row in range(3):
+        one_ref[24 + row] = jnp.where(even, high[5 + row], low[row])
+        two_ref[24 + row] = jnp.where(even, low[row], high[5 + row])
+
+
+def smooth_kernel(x_ref, seam_ref, one_ref, two_ref, order_ref, keep_ref, send_ref, done, seam_edges):
     lat = lax.axis_index("lat")
     even = lat % 2 == 0
     not_first = jnp.where(lat == 0, 0, 1)
@@ -98,13 +105,16 @@
         near = pltpu.roll(tall, 1, 0) + pltpu.roll(tall, 23, 0)
         return near[0:8], near[8:16], near[16:24]
 
+    norths = [jnp.where(even, one_ref[24 + i], two_ref[24 + i]) for i in range(3)]
+    souths = [jnp.where(even, two_ref[24 + i], one_ref[24 + i]) for i in range(3)]
+    seam_edges[...] = jnp.swapaxes(jnp.stack(norths + [zero, zero] + souths), 0, 1)
+
     def snapshot(snap, carry):
-        at = pl.ds(pl.multiple_of(8 * snap, 8), 8)
         edges = jnp.swapaxes(
             jnp.stack(
-                [jnp.where(even, one_ref[i, at, :], two_ref[i, at, :]) for i in range(3)]
+                [jnp.where(even, one_ref[8 * i + snap], two_ref[8 * i + snap]) for i in range(3)]
                 + [zero, zero]
-                + [jnp.where(even, two_ref[i, at, :], one_ref[i, at, :]) for i in range(3)]
+                + [jnp.where(even, two_ref[8 * i + snap], one_ref[8 * i + snap]) for i in range(3)]
             ),
             0,
             1,
@@ -116,7 +126,7 @@
         seam = (
             seam_ref[pl.ds(pl.multiple_of(ROWS * snap, 8), 8), :],
             seam_ref[pl.ds(pl.multiple_of(ROWS * snap + 8, 8), 8), :],
-            jnp.where((row < 4) == even, one_ref[3, at, :], two_ref[3, at, :]),
+            seam_edges[snap],
         )
         for sweep in range(3):
             tiles = 3 if sweep < 2 else 2
@@ -153,7 +163,7 @@
             done[snap, pl.ds(ROWS * level, ROWS), :] = value
         return carry
 
-    lax.fori_loop(0, SNAPS, snapshot, 0)
+    lax.fori_loop(0, SNAPS, snapshot, 0, unroll=2)
     group = lax.axis_index("tm")
     for snap in range(SNAPS):
         keep_ref[snap] = done[snap, pl.ds(pl.multiple_of(HALF_ROWS * group, 8), HALF_ROWS), :]
@@ -405,12 +415,17 @@
     cells = CELL_ROWS * LANES * lat_count * lax.axis_size(LON)
     q = pltpu.with_memory_space_constraint(basis.reshape(EOFS, CELL_ROWS, LANES), pltpu.HBM)
 
-    packed = call(pack_kernel, [VMEM], shape(CELL_ROWS, LANES))(snapshots)
+    packed, x = call(
+        pack_kernel,
+        [ANY],
+        (shape(CELL_ROWS, LANES), shape(*snapshots.shape)),
+        [pltpu.SemaphoreType.DMA((SNAPS,))],
+    )(pltpu.with_memory_space_constraint(snapshots, pltpu.HBM))
     chip = swapped(packed, LON, 1)
     beside = across(packed, "core")
     seam, one, two = call(
-        seam_kernel, [VMEM] * 4, (shape(CELL_ROWS, LANES), shape(4, 64, LANES), shape(4, 64, LANES))
-    )(snapshots, packed, chip, beside)
+        seam_kernel, [VMEM] * 4, (shape(CELL_ROWS, LANES), shape(27, 8, LANES), shape(27, 8, LANES))
+    )(x, packed, chip, beside)
     one, two = swapped(one, "lat", 0), swapped(two, "lat", 1)
     parts = HALF_ROWS // QROWS
     stack, gram = call(
@@ -424,8 +439,8 @@
         smooth_kernel,
         [VMEM] * 5,
         (shape(SNAPS, HALF_ROWS, LANES),) * 2,
-        [pltpu.VMEM((SNAPS, CELL_ROWS, LANES), F32)],
-    )(snapshots, seam, one, two, gram)
+        [pltpu.VMEM((SNAPS, CELL_ROWS, LANES), F32), pltpu.VMEM((SNAPS, 8, LANES), F32)],
+    )(x, seam, one, two, gram)
     here = across(send, "tm")
     far = call(
         basis_stack_kernel,

time: 75.4 us -> 74.9 us (level)
  local copies, waits for them, and re-layouts: 5.2 us -> 4.16 us
  Pallas kernels: 18.9 us -> 19.9 us
    pallas_call x2, Pallas kernels: 0.29 us -> 1.7 us  [the longest x1 1.59 us: update(): call(pack_kernel, [ANY], (shape(CELL_ROWS, LANES), shape(*snapshots.shape...]
    unnamed x18 -> x14, local copies, waits for them, and re-layouts: 5.2 us -> 4.16 us
where the time goes in v6:
time: 74.9 us; the launch traced here: 74.5 us
  starting transfers between devices  20.6 us (28%)
  blocking collectives  20.3 us (27%)
  Pallas kernels  19.9 us (27%)
  waiting for transfers between devices  8.73 us (12%)
  local copies, waits for them, and re-layouts  4.16 us (6%)
  between operations  0.79 us (1%)
    all_to_all x1, blocking collectives, gathered(): return lax.all_to_all(values, axes, 0, 0)  20.3 us
    ppermute x4, starting transfers between devices, across(): return lax.ppermute(values, axis, [(0, 1), (1, 0)])  12.8 us
    all_to_all x1, starting transfers between devices, gathered(): return lax.all_to_all(values, axes, 0, 0)  7.04 us
    all_to_all x1, waiting for transfers between devices, gathered(): return lax.all_to_all(values, axes, 0, 0)  4.2 us
    unnamed x14, local copies, waits for them, and re-layouts  4.16 us
    pallas_call x1, Pallas kernels, update(): call(basis_gram_kernel, [VMEM, ANY], (shape(3 * EOFS, HALF_CELLS, dtype=B...  3.56 us
    pallas_call x1, Pallas kernels, update(): pl.pallas_call(final_kernel, out_shape=shape(EOFS, CELL_ROWS, LANES), in_...  3.37 us
    pallas_call x1, Pallas kernels, update(): call(functools.partial(factor_kernel, cells), [VMEM], (shape(2 * EOFS, 16...  2.94 us
  transfers between devices with their start and end apart: 8, of which 4 were waited for; matrix products, arithmetic and copies ran while one was open for 0% of the time, Pallas kernels for 14%

profile of v6, /device:TPU:1, one launch (start us, length us, event | category | flops | bytes accessed | tf_op | source)
XLA Modules:
  0.0 74.5 jit_solution(2035042647752681356)
XLA Ops:
  0.6 1.6 %shard_map.41 = (f32[128,128]{1,0:T(8,128)S(1)}, f32[8,8,16,128]{3,2,1,0:T(8,128)S(1)}) custom-call(f32[8,8,16,128]{3,2,1,0:T(8,128)} %fields_ref.1), custom_call_target="tpu_custom_call" | custom-call | flops 1000000 | bytes 1000000 | tf_op jit(solution)/shard_map/pallas_call | solution.py:418
  2.2 3.3 %collective-permute-start.1 = (f32[128,128]{1,0:T(8,128)S(1)}, f32[128,128]{1,0:T(8,128)S(1)}, u32[]{:S(2)}, u32[]{:S(2)}) collective-permute-start(f32[128,128]{1,0:T(8,128)S(1)} %get-tuple-element.19.packed_ref), channel_id=1, source_target_pairs={{0,16},{16,0},{1,17},{17,1},{2,18},{18,2},{3,19},{19,3},{4,20},{20... | collective-permute-start | bytes 196616 | tf_op jit(solution)/shard_map/ppermute | solution.py:406
  5.5 0.9 %collective-permute-done.1.beside_ref = f32[128,128]{1,0:T(8,128)S(1)} collective-permute-done((f32[128,128]{1,0:T(8,128)S(1)}, f32[128,128]{1,0:T(8,128)S(1)}, u32[]{:S(2)}, u32[]{:S(2)}) %collective-permute-start.1) | collective-permute-done | bytes 65568 | tf_op jit(solution)/shard_map/ppermute | solution.py:406
  6.4 2.8 %collective-permute-done.across_ref = f32[128,128]{1,0:T(8,128)S(1)} collective-permute-done((f32[128,128]{1,0:T(8,128)S(1)}, f32[128,128]{1,0:T(8,128)S(1)}, u32[]{:S(2)}, u32[]{:S(2)}) %collective-permute-start) | collective-permute-done | bytes 65568 | tf_op jit(solution)/shard_map/ppermute | solution.py:402
  9.2 0.1 shard_map.42
  9.4 0.7 collective-permute-start.3
  10.1 3.6 %shard_map.43 = (bf16[192,8192]{1,0:T(8,128)(2,1)S(1)}, f32[64,64]{1,0:T(8,128)S(1)}) custom-call(f32[128,128]{1,0:T(8,128)S(1)} %get-tuple-element.20.order_ref.seam_ref, f32[64,128,128]{2,1,0:T(8,128)} %bitcast.3), custom_call_target="tpu_custom_call" | custom-call | flops 1000000 | bytes 8388608 | tf_op jit(solution)/shard_map/pallas_call | solution.py:431
  13.7 2.8 %shard_map.44 = (f32[8,64,128]{2,1,0:T(8,128)S(1)}, f32[8,64,128]{2,1,0:T(8,128)S(1)}) custom-call(f32[8,8,16,128]{3,2,1,0:T(8,128)S(1)} %get-tuple-element.18.x_ref, f32[128,128]{1,0:T(8,128)S(1)} %get-tuple-element.20.order_ref.seam_ref, f32[27,8,128]{2,1,0:T(8,128)S(1)} %collective-permute-done.2.one_ref, ...), custom_call_target="tpu_custom_call" | custom-call | flops 1000000 | bytes 1000000 | tf_op jit(solution)/shard_map/pallas_call | solution.py:438
  16.4 2.9 %collective-permute-start.4 = (f32[8,64,128]{2,1,0:T(8,128)S(1)}, f32[8,64,128]{2,1,0:T(8,128)S(1)}, u32[]{:S(2)}, u32[]{:S(2)}) collective-permute-start(f32[8,64,128]{2,1,0:T(8,128)S(1)} %get-tuple-element.27.send_ref), channel_id=1, source_target_pairs={{0,1},{1,0},{2,3},{3,2},{4,5},{5,4},{6,7},{7,6},{8,9},{9,8},{10,11... | collective-permute-start | bytes 786440 | tf_op jit(solution)/shard_map/ppermute | solution.py:406
  19.3 1.9 %shard_map.46.order_ref.far_ref = bf16[128,8192]{1,0:T(8,128)(2,1)S(1)} custom-call(f32[8,64,128]{2,1,0:T(8,128)S(1)} %get-tuple-element.25.mine_ref.order_ref.keep_ref, f32[64,128,128]{2,1,0:T(8,128)} %bitcast.4), custom_call_target="tpu_custom_call" | custom-call | flops 1000000 | bytes 6291456 | tf_op jit(solution)/shard_map/pallas_call | solution.py:445
  21.2 2.2 %shard_map.45 = (f32[192,24]{1,0:T(8,128)S(1)}, f32[24,24]{1,0:T(8,128)S(1)}, bf16[24,8192]{1,0:T(8,128)(2,1)S(1)}) custom-call(bf16[192,8192]{1,0:T(8,128)(2,1)S(1)} %get-tuple-element.21.stack_ref.near_ref, f32[8,64,128]{2,1,0:T(8,128)S(1)} %get-tuple-element.25.mine_ref.order_ref.keep_ref), custom_call_target="tpu_custom_call" | custom-call | flops 1000000 | bytes 4194304 | tf_op jit(solution)/shard_map/pallas_call | solution.py:452
  23.5 1.5 %shard_map.47 = (f32[16,128]{1,0:T(8,128)S(1)}, f32[16,128]{1,0:T(8,128)S(1)}) custom-call(bf16[192,8192]{1,0:T(8,128)(2,1)S(1)} %get-tuple-element.21.stack_ref.near_ref, f32[64,64]{1,0:T(8,128)S(1)} %get-tuple-element.22.order_ref.gram_ref, bf16[24,8192]{1,0:T(8,128)(2,1)S(1)} %get-tuple-element.26.pieces_ref, ...), custom_call_target="tpu_custom_call" | custom-call | flops 1000000 | bytes 1000000 | tf_op jit(solution)/shard_map/pallas_call | solution.py:460
  25.0 3.7 %collective-permute-start.5 = (f32[16,128]{1,0:T(8,128)S(1)}, f32[16,128]{1,0:T(8,128)S(1)}, u32[]{:S(2)}, u32[]{:S(2)}) collective-permute-start(f32[16,128]{1,0:T(8,128)S(1)} %get-tuple-element.31), channel_id=1, source_target_pairs={{0,16},{16,0},{1,17},{17,1},{2,18},{18,2},{3,19},{19,3},{4,20},{20... | collective-permute-start | bytes 24584 | tf_op jit(solution)/shard_map/ppermute | solution.py:406
  28.7 0.8 %collective-permute-done.5.two_ref = f32[16,128]{1,0:T(8,128)S(1)} collective-permute-done((f32[16,128]{1,0:T(8,128)S(1)}, f32[16,128]{1,0:T(8,128)S(1)}, u32[]{:S(2)}, u32[]{:S(2)}) %collective-permute-start.5) | collective-permute-done | bytes 8224 | tf_op jit(solution)/shard_map/ppermute | solution.py:406
  29.6 0.6 copy-done.4
  30.2 7.0 %all-to-all-start = ((f32[16,16,128]{2,1,0:T(8,128)}), f32[16,16,128]{2,1,0:T(8,128)S(1)}, u32[]{:S(2)}, u32[]{:S(2)}) async-start(f32[16,16,128]{2,1,0:T(8,128)} %copy-done.4), calls=%async_computation | async-start | bytes 262144 | tf_op jit(solution)/shard_map/all_to_all | solution.py:410
  37.3 2.9 %collective-permute-start.6 = (f32[8,64,128]{2,1,0:T(8,128)S(1)}, f32[8,64,128]{2,1,0:T(8,128)}, u32[]{:S(2)}, u32[]{:S(2)}) collective-permute-start(f32[8,64,128]{2,1,0:T(8,128)S(1)} %get-tuple-element.25.mine_ref.order_ref.keep_ref), channel_id=1, source_target_pairs={{0,1},{1,0},{2,3},{3,2},{4,5},{5,4},{6,7},{7,6},{8,9},{9,8},{10,11... | collective-permute-start | bytes 786440 | tf_op jit(solution)/shard_map/ppermute | solution.py:406
  40.1 4.2 %all-to-all-done.parts_ref = f32[16,16,128]{2,1,0:T(8,128)S(1)} async-done(((f32[16,16,128]{2,1,0:T(8,128)}), f32[16,16,128]{2,1,0:T(8,128)S(1)}, u32[]{:S(2)}, u32[]{:S(2)}) %all-to-all-start) | async-done | bytes 131104 | tf_op jit(solution)/shard_map/all_to_all | solution.py:410
  44.4 20.3 %all_to_all.10.parts_ref = f32[16,16,128]{2,1,0:T(8,128)S(1)} all-to-all(f32[16,16,128]{2,1,0:T(8,128)S(1)} %shard_map.49), channel_id=1, replica_groups=mesh['pair'=8,'core'=2,'lat'=8,'tm'=2] {'core','lat'}, dimensions={0} | all-to-all | bytes 262144 | tf_op jit(solution)/shard_map/all_to_all | solution.py:410
  64.7 2.9 %shard_map.50 = (bf16[128,160]{1,0:T(8,128)(2,1)S(1)}, f32[8,64]{1,0:T(8,128)}) custom-call(f32[16,16,128]{2,1,0:T(8,128)S(1)} %all_to_all.10.parts_ref), custom_call_target="tpu_custom_call" | custom-call | flops 1000000 | bytes 1000000 | tf_op jit(solution)/shard_map/pallas_call | solution.py:468
  67.6 1.6 %copy-done.1 = bf16[128,8192]{1,0:T(8,128)(2,1)S(1)} copy-done((bf16[128,8192]{1,0:T(8,128)(2,1)S(1)}, bf16[128,8192]{1,0:T(8,128)(2,1)}, u32[]{:S(2)}) %copy-start.1) | copy-done | bytes 2097176
  69.2 0.9 %copy-done.3 = f32[8,64,128]{2,1,0:T(8,128)S(1)} copy-done((f32[8,64,128]{2,1,0:T(8,128)S(1)}, f32[8,64,128]{2,1,0:T(8,128)}, u32[]{:S(2)}) %copy-start.3) | copy-done | bytes 262168
  70.2 0.9 %copy-done.6 = f32[8,64,128]{2,1,0:T(8,128)S(1)} copy-done((f32[8,64,128]{2,1,0:T(8,128)S(1)}, f32[8,64,128]{2,1,0:T(8,128)}, u32[]{:S(2)}) %copy-start.6) | copy-done | bytes 262168
  71.1 3.4 %shard_map.51 = f32[64,128,128]{2,1,0:T(8,128)} custom-call(bf16[128,160]{1,0:T(8,128)(2,1)S(1)} %get-tuple-element.32.maps_ref, bf16[192,8192]{1,0:T(8,128)(2,1)S(1)} %get-tuple-element.21.stack_ref.near_ref, bf16[128,8192]{1,0:T(8,128)(2,1)S(1)} %copy-done.1, f32[8,64,128]{2,1,0:T(8,128)S(1)} %get-tuple-element.25.mine_ref.order_ref.keep_ref, ...), custom_call_target="tpu_custom_call" | custom-call | tf_op jit(solution)/shard_map/pallas_call | solution.py:472
  (18 shorter events, 0.2 us)
Async XLA Ops:
  2.2 4.2 %collective-permute-start.1 = (f32[128,128]{1,0:T(8,128)S(1)}, f32[128,128]{1,0:T(8,128)S(1)}, u32[]{:S(2)}, u32[]{:S(2)}) collective-permute-start(f32[128,128]{1,0:T(8,128)S(1)} %get-tuple-element.19.packed_ref), channel_id=1, source_target_pairs={{0,16},{16,0},{1,17},{17,1},{2,18},{18,2},{3,19},{19,3},{4,20},{20... | collective-permute-start | bytes 196616 | tf_op jit(solution)/shard_map/ppermute | solution.py:406
  5.5 3.7 %collective-permute-start = (f32[128,128]{1,0:T(8,128)S(1)}, f32[128,128]{1,0:T(8,128)S(1)}, u32[]{:S(2)}, u32[]{:S(2)}) collective-permute-start(f32[128,128]{1,0:T(8,128)S(1)} %get-tuple-element.19.packed_ref), channel_id=1, source_target_pairs={{16,32},{32,16},{48,64},{64,48},{80,96},{96,80},{112,128},{128,112... | collective-permute-start | bytes 196616 | tf_op jit(solution)/shard_map/ppermute | solution.py:402
  9.3 4.3 %collective-permute-start.2 = (f32[27,8,128]{2,1,0:T(8,128)S(1)}, f32[27,8,128]{2,1,0:T(8,128)S(1)}, u32[]{:S(2)}, u32[]{:S(2)}) collective-permute-start(f32[27,8,128]{2,1,0:T(8,128)S(1)} %get-tuple-element.23), channel_id=1, source_target_pairs={{0,2},{2,0},{4,6},{6,4},{8,10},{10,8},{12,14},{14,12},{1,3},{3,1},... | collective-permute-start | bytes 331784 | tf_op jit(solution)/shard_map/ppermute | solution.py:402
  9.4 4.3 %collective-permute-start.3 = (f32[27,8,128]{2,1,0:T(8,128)S(1)}, f32[27,8,128]{2,1,0:T(8,128)S(1)}, u32[]{:S(2)}, u32[]{:S(2)}) collective-permute-start(f32[27,8,128]{2,1,0:T(8,128)S(1)} %get-tuple-element.24), channel_id=1, source_target_pairs={{2,4},{4,2},{6,8},{8,6},{10,12},{12,10},{3,5},{5,3},{7,9},{9,7},{1... | collective-permute-start | bytes 331784 | tf_op jit(solution)/shard_map/ppermute | solution.py:402
  16.4 7.0 %copy-start.5 = (f32[8,64,128]{2,1,0:T(8,128)}, f32[8,64,128]{2,1,0:T(8,128)S(1)}, u32[]{:S(2)}) copy-start(f32[8,64,128]{2,1,0:T(8,128)S(1)} %get-tuple-element.27.send_ref) | copy-start | bytes 786436
  16.4 7.0 %collective-permute-start.4 = (f32[8,64,128]{2,1,0:T(8,128)S(1)}, f32[8,64,128]{2,1,0:T(8,128)S(1)}, u32[]{:S(2)}, u32[]{:S(2)}) collective-permute-start(f32[8,64,128]{2,1,0:T(8,128)S(1)} %get-tuple-element.27.send_ref), channel_id=1, source_target_pairs={{0,1},{1,0},{2,3},{3,2},{4,5},{5,4},{6,7},{7,6},{8,9},{9,8},{10,11... | collective-permute-start | bytes 786440 | tf_op jit(solution)/shard_map/ppermute | solution.py:406
  21.2 3.8 %copy-start = (bf16[128,8192]{1,0:T(8,128)(2,1)}, bf16[128,8192]{1,0:T(8,128)(2,1)S(1)}, u32[]{:S(2)}) copy-start(bf16[128,8192]{1,0:T(8,128)(2,1)S(1)} %shard_map.46.order_ref.far_ref) | copy-start | bytes 6291460
  23.5 1.6 %copy-start.2 = (f32[8,64,128]{2,1,0:T(8,128)}, f32[8,64,128]{2,1,0:T(8,128)S(1)}, u32[]{:S(2)}) copy-start(f32[8,64,128]{2,1,0:T(8,128)S(1)} %collective-permute-done.4.other_ref.here_ref) | copy-start | bytes 786436
  25.0 4.5 %collective-permute-start.5 = (f32[16,128]{1,0:T(8,128)S(1)}, f32[16,128]{1,0:T(8,128)S(1)}, u32[]{:S(2)}, u32[]{:S(2)}) collective-permute-start(f32[16,128]{1,0:T(8,128)S(1)} %get-tuple-element.31), channel_id=1, source_target_pairs={{0,16},{16,0},{1,17},{17,1},{2,18},{18,2},{3,19},{19,3},{4,20},{20... | collective-permute-start | bytes 24584 | tf_op jit(solution)/shard_map/ppermute | solution.py:406
  29.6 0.7 copy-start.4
  30.2 14.1 %all-to-all-start = ((f32[16,16,128]{2,1,0:T(8,128)}), f32[16,16,128]{2,1,0:T(8,128)S(1)}, u32[]{:S(2)}, u32[]{:S(2)}) async-start(f32[16,16,128]{2,1,0:T(8,128)} %copy-done.4), calls=%async_computation | async-start | bytes 262144 | tf_op jit(solution)/shard_map/all_to_all | solution.py:410
  37.3 30.4 %collective-permute-start.6 = (f32[8,64,128]{2,1,0:T(8,128)S(1)}, f32[8,64,128]{2,1,0:T(8,128)}, u32[]{:S(2)}, u32[]{:S(2)}) collective-permute-start(f32[8,64,128]{2,1,0:T(8,128)S(1)} %get-tuple-element.25.mine_ref.order_ref.keep_ref), channel_id=1, source_target_pairs={{0,1},{1,0},{2,3},{3,2},{4,5},{5,4},{6,7},{7,6},{8,9},{9,8},{10,11... | collective-permute-start | bytes 786440 | tf_op jit(solution)/shard_map/ppermute | solution.py:406
  67.6 1.6 %copy-start.1 = (bf16[128,8192]{1,0:T(8,128)(2,1)S(1)}, bf16[128,8192]{1,0:T(8,128)(2,1)}, u32[]{:S(2)}) copy-start(bf16[128,8192]{1,0:T(8,128)(2,1)} %copy-done) | copy-start | bytes 6291460
  69.2 0.9 %copy-start.3 = (f32[8,64,128]{2,1,0:T(8,128)S(1)}, f32[8,64,128]{2,1,0:T(8,128)}, u32[]{:S(2)}) copy-start(f32[8,64,128]{2,1,0:T(8,128)} %copy-done.2) | copy-start | bytes 786436
  70.2 0.9 %copy-start.6 = (f32[8,64,128]{2,1,0:T(8,128)S(1)}, f32[8,64,128]{2,1,0:T(8,128)}, u32[]{:S(2)}) copy-start(f32[8,64,128]{2,1,0:T(8,128)} %copy-done.5) | copy-start | bytes 786436

commit v7 on v6

--- a/solution.py
+++ b/solution.py
@@ -52,13 +52,9 @@
     )
 
 
-def pack_kernel(fields_ref, packed_ref, x_ref, sems):
-    copies = [pltpu.make_async_copy(fields_ref.at[snap], x_ref.at[snap], sems.at[snap]) for snap in range(SNAPS)]
-    for copy in copies:
-        copy.start()
+def pack_kernel(x_ref, packed_ref):
     lane = lanes_of((ROWS, LANES))
-    for snap, copy in enumerate(copies):
-        copy.wait()
+    for snap in range(SNAPS):
         packed = jnp.zeros((ROWS, LANES), F32)
         for level in range(LEVELS):
             turned = pltpu.roll(x_ref[snap, level], 16 * level + 3, 1)
@@ -415,17 +411,12 @@
     cells = CELL_ROWS * LANES * lat_count * lax.axis_size(LON)
     q = pltpu.with_memory_space_constraint(basis.reshape(EOFS, CELL_ROWS, LANES), pltpu.HBM)
 
-    packed, x = call(
-        pack_kernel,
-        [ANY],
-        (shape(CELL_ROWS, LANES), shape(*snapshots.shape)),
-        [pltpu.SemaphoreType.DMA((SNAPS,))],
-    )(pltpu.with_memory_space_constraint(snapshots, pltpu.HBM))
+    packed = call(pack_kernel, [VMEM], shape(CELL_ROWS, LANES))(snapshots)
     chip = swapped(packed, LON, 1)
     beside = across(packed, "core")
     seam, one, two = call(
         seam_kernel, [VMEM] * 4, (shape(CELL_ROWS, LANES), shape(27, 8, LANES), shape(27, 8, LANES))
-    )(x, packed, chip, beside)
+    )(snapshots, packed, chip, beside)
     one, two = swapped(one, "lat", 0), swapped(two, "lat", 1)
     parts = HALF_ROWS // QROWS
     stack, gram = call(
@@ -440,7 +431,7 @@
         [VMEM] * 5,
         (shape(SNAPS, HALF_ROWS, LANES),) * 2,
         [pltpu.VMEM((SNAPS, CELL_ROWS, LANES), F32), pltpu.VMEM((SNAPS, 8, LANES), F32)],
-    )(x, seam, one, two, gram)
+    )(snapshots, seam, one, two, gram)
     here = across(send, "tm")
     far = call(
         basis_stack_kernel,

time: 74.9 us -> 74.6 us (level)
  Pallas kernels: 19.9 us -> 18.5 us
  local copies, waits for them, and re-layouts: 4.16 us -> 5.2 us
    pallas_call x1, Pallas kernels: 1.59 us -> 0.19 us  [update(): packed = call(pack_kernel, [VMEM], shape(CELL_ROWS, LANES))(snapshots)]
    unnamed x14 -> x18, local copies, waits for them, and re-layouts: 4.16 us -> 5.2 us
where the time goes in v7:
time: 74.6 us; the launch traced here: 74.1 us
  starting transfers between devices  20.6 us (28%)
  blocking collectives  20.3 us (27%)
  Pallas kernels  18.5 us (25%)
  waiting for transfers between devices  8.73 us (12%)
  local copies, waits for them, and re-layouts  5.2 us (7%)
  between operations  0.81 us (1%)
    all_to_all x1, blocking collectives, gathered(): return lax.all_to_all(values, axes, 0, 0)  20.3 us
    ppermute x4, starting transfers between devices, across(): return lax.ppermute(values, axis, [(0, 1), (1, 0)])  12.8 us
    all_to_all x1, starting transfers between devices, gathered(): return lax.all_to_all(values, axes, 0, 0)  7.03 us
    unnamed x18, local copies, waits for them, and re-layouts  5.2 us
    all_to_all x1, waiting for transfers between devices, gathered(): return lax.all_to_all(values, axes, 0, 0)  4.2 us
    pallas_call x1, Pallas kernels, update(): call(basis_gram_kernel, [VMEM, ANY], (shape(3 * EOFS, HALF_CELLS, dtype=B...  3.56 us
    pallas_call x1, Pallas kernels, update(): pl.pallas_call(final_kernel, out_shape=shape(EOFS, CELL_ROWS, LANES), in_...  3.37 us
    pallas_call x1, Pallas kernels, update(): call(functools.partial(factor_kernel, cells), [VMEM], (shape(2 * EOFS, 16...  2.94 us
  transfers between devices with their start and end apart: 8, of which 4 were waited for; matrix products, arithmetic and copies ran while one was open for 0% of the time, Pallas kernels for 14%

profile of v7, /device:TPU:1, one launch (start us, length us, event | category | flops | bytes accessed | tf_op | source)
XLA Modules:
  0.0 74.1 jit_solution(2957432037561782579)
XLA Ops:
  0.6 1.0 %copy-done.2 = f32[8,8,16,128]{3,2,1,0:T(8,128)S(1)} copy-done((f32[8,8,16,128]{3,2,1,0:T(8,128)S(1)}, f32[8,8,16,128]{3,2,1,0:T(8,128)}, u32[]{:S(2)}) %copy-start.2) | copy-done | bytes 524312
  1.7 0.2 shard_map.41.packed_ref
  1.9 3.3 %collective-permute-start.1 = (f32[128,128]{1,0:T(8,128)S(1)}, f32[128,128]{1,0:T(8,128)S(1)}, u32[]{:S(2)}, u32[]{:S(2)}) collective-permute-start(f32[128,128]{1,0:T(8,128)S(1)} %shard_map.41.packed_ref), channel_id=1, source_target_pairs={{0,16},{16,0},{1,17},{17,1},{2,18},{18,2},{3,19},{19,3},{4,20},{20... | collective-permute-start | bytes 196616 | tf_op jit(solution)/shard_map/ppermute | solution.py:402
  5.2 0.9 %collective-permute-done.1.beside_ref = f32[128,128]{1,0:T(8,128)S(1)} collective-permute-done((f32[128,128]{1,0:T(8,128)S(1)}, f32[128,128]{1,0:T(8,128)S(1)}, u32[]{:S(2)}, u32[]{:S(2)}) %collective-permute-start.1) | collective-permute-done | bytes 65568 | tf_op jit(solution)/shard_map/ppermute | solution.py:402
  6.1 2.8 %collective-permute-done.across_ref = f32[128,128]{1,0:T(8,128)S(1)} collective-permute-done((f32[128,128]{1,0:T(8,128)S(1)}, f32[128,128]{1,0:T(8,128)S(1)}, u32[]{:S(2)}, u32[]{:S(2)}) %collective-permute-start) | collective-permute-done | bytes 65568 | tf_op jit(solution)/shard_map/ppermute | solution.py:398
  9.1 0.7 collective-permute-start.3
  9.7 3.6 %shard_map.43 = (bf16[192,8192]{1,0:T(8,128)(2,1)S(1)}, f32[64,64]{1,0:T(8,128)S(1)}) custom-call(f32[128,128]{1,0:T(8,128)S(1)} %get-tuple-element.16.order_ref.seam_ref, f32[64,128,128]{2,1,0:T(8,128)} %bitcast.3), custom_call_target="tpu_custom_call" | custom-call | flops 1000000 | bytes 8388608 | tf_op jit(solution)/shard_map/pallas_call | solution.py:422
  13.3 2.8 %shard_map.44 = (f32[8,64,128]{2,1,0:T(8,128)S(1)}, f32[8,64,128]{2,1,0:T(8,128)S(1)}) custom-call(f32[8,8,16,128]{3,2,1,0:T(8,128)S(1)} %copy-done.3, f32[128,128]{1,0:T(8,128)S(1)} %get-tuple-element.16.order_ref.seam_ref, f32[27,8,128]{2,1,0:T(8,128)S(1)} %collective-permute-done.2.one_ref, f32[27,8,128]{2,1,0:T(8,128)S(1)} %collective-permute-done.3.two_ref, ...), custom_call_target="tpu_custom_call" | custom-call | flops 1000000 | bytes 1000000 | tf_op jit(solution)/shard_map/pallas_call | solution.py:429
  16.1 2.9 %collective-permute-start.4 = (f32[8,64,128]{2,1,0:T(8,128)S(1)}, f32[8,64,128]{2,1,0:T(8,128)S(1)}, u32[]{:S(2)}, u32[]{:S(2)}) collective-permute-start(f32[8,64,128]{2,1,0:T(8,128)S(1)} %get-tuple-element.23.send_ref), channel_id=1, source_target_pairs={{0,1},{1,0},{2,3},{3,2},{4,5},{5,4},{6,7},{7,6},{8,9},{9,8},{10,11... | collective-permute-start | bytes 786440 | tf_op jit(solution)/shard_map/ppermute | solution.py:402
  19.0 1.9 %shard_map.46.order_ref.far_ref = bf16[128,8192]{1,0:T(8,128)(2,1)S(1)} custom-call(f32[8,64,128]{2,1,0:T(8,128)S(1)} %get-tuple-element.21.mine_ref.order_ref.keep_ref, f32[64,128,128]{2,1,0:T(8,128)} %bitcast.4), custom_call_target="tpu_custom_call" | custom-call | flops 1000000 | bytes 6291456 | tf_op jit(solution)/shard_map/pallas_call | solution.py:436
  20.9 2.2 %shard_map.45 = (f32[192,24]{1,0:T(8,128)S(1)}, f32[24,24]{1,0:T(8,128)S(1)}, bf16[24,8192]{1,0:T(8,128)(2,1)S(1)}) custom-call(bf16[192,8192]{1,0:T(8,128)(2,1)S(1)} %get-tuple-element.17.stack_ref.near_ref, f32[8,64,128]{2,1,0:T(8,128)S(1)} %get-tuple-element.21.mine_ref.order_ref.keep_ref), custom_call_target="tpu_custom_call" | custom-call | flops 1000000 | bytes 4194304 | tf_op jit(solution)/shard_map/pallas_call | solution.py:443
  23.1 1.5 %shard_map.47 = (f32[16,128]{1,0:T(8,128)S(1)}, f32[16,128]{1,0:T(8,128)S(1)}) custom-call(bf16[192,8192]{1,0:T(8,128)(2,1)S(1)} %get-tuple-element.17.stack_ref.near_ref, f32[64,64]{1,0:T(8,128)S(1)} %get-tuple-element.18.order_ref.gram_ref, bf16[24,8192]{1,0:T(8,128)(2,1)S(1)} %get-tuple-element.22.pieces_ref, ...), custom_call_target="tpu_custom_call" | custom-call | flops 1000000 | bytes 1000000 | tf_op jit(solution)/shard_map/pallas_call | solution.py:451
  24.7 3.7 %collective-permute-start.5 = (f32[16,128]{1,0:T(8,128)S(1)}, f32[16,128]{1,0:T(8,128)S(1)}, u32[]{:S(2)}, u32[]{:S(2)}) collective-permute-start(f32[16,128]{1,0:T(8,128)S(1)} %get-tuple-element.27), channel_id=1, source_target_pairs={{0,16},{16,0},{1,17},{17,1},{2,18},{18,2},{3,19},{19,3},{4,20},{20... | collective-permute-start | bytes 24584 | tf_op jit(solution)/shard_map/ppermute | solution.py:402
  28.4 0.8 %collective-permute-done.5.two_ref = f32[16,128]{1,0:T(8,128)S(1)} collective-permute-done((f32[16,128]{1,0:T(8,128)S(1)}, f32[16,128]{1,0:T(8,128)S(1)}, u32[]{:S(2)}, u32[]{:S(2)}) %collective-permute-start.5) | collective-permute-done | bytes 8224 | tf_op jit(solution)/shard_map/ppermute | solution.py:402
  29.2 0.6 copy-done.6
  29.9 7.0 %all-to-all-start = ((f32[16,16,128]{2,1,0:T(8,128)}), f32[16,16,128]{2,1,0:T(8,128)S(1)}, u32[]{:S(2)}, u32[]{:S(2)}) async-start(f32[16,16,128]{2,1,0:T(8,128)} %copy-done.6), calls=%async_computation | async-start | bytes 262144 | tf_op jit(solution)/shard_map/all_to_all | solution.py:406
  36.9 2.9 %collective-permute-start.6 = (f32[8,64,128]{2,1,0:T(8,128)S(1)}, f32[8,64,128]{2,1,0:T(8,128)}, u32[]{:S(2)}, u32[]{:S(2)}) collective-permute-start(f32[8,64,128]{2,1,0:T(8,128)S(1)} %get-tuple-element.21.mine_ref.order_ref.keep_ref), channel_id=1, source_target_pairs={{0,1},{1,0},{2,3},{3,2},{4,5},{5,4},{6,7},{7,6},{8,9},{9,8},{10,11... | collective-permute-start | bytes 786440 | tf_op jit(solution)/shard_map/ppermute | solution.py:402
  39.8 4.2 %all-to-all-done.parts_ref = f32[16,16,128]{2,1,0:T(8,128)S(1)} async-done(((f32[16,16,128]{2,1,0:T(8,128)}), f32[16,16,128]{2,1,0:T(8,128)S(1)}, u32[]{:S(2)}, u32[]{:S(2)}) %all-to-all-start) | async-done | bytes 131104 | tf_op jit(solution)/shard_map/all_to_all | solution.py:406
  44.0 20.3 %all_to_all.10.parts_ref = f32[16,16,128]{2,1,0:T(8,128)S(1)} all-to-all(f32[16,16,128]{2,1,0:T(8,128)S(1)} %shard_map.49), channel_id=1, replica_groups=mesh['pair'=8,'core'=2,'lat'=8,'tm'=2] {'core','lat'}, dimensions={0} | all-to-all | bytes 262144 | tf_op jit(solution)/shard_map/all_to_all | solution.py:406
  64.3 2.9 %shard_map.50 = (bf16[128,160]{1,0:T(8,128)(2,1)S(1)}, f32[8,64]{1,0:T(8,128)}) custom-call(f32[16,16,128]{2,1,0:T(8,128)S(1)} %all_to_all.10.parts_ref), custom_call_target="tpu_custom_call" | custom-call | flops 1000000 | bytes 1000000 | tf_op jit(solution)/shard_map/pallas_call | solution.py:459
  67.3 1.6 %copy-done.1 = bf16[128,8192]{1,0:T(8,128)(2,1)S(1)} copy-done((bf16[128,8192]{1,0:T(8,128)(2,1)S(1)}, bf16[128,8192]{1,0:T(8,128)(2,1)}, u32[]{:S(2)}) %copy-start.1) | copy-done | bytes 2097176
  68.9 0.9 %copy-done.5 = f32[8,64,128]{2,1,0:T(8,128)S(1)} copy-done((f32[8,64,128]{2,1,0:T(8,128)S(1)}, f32[8,64,128]{2,1,0:T(8,128)}, u32[]{:S(2)}) %copy-start.5) | copy-done | bytes 262168
  69.8 0.9 %copy-done.8 = f32[8,64,128]{2,1,0:T(8,128)S(1)} copy-done((f32[8,64,128]{2,1,0:T(8,128)S(1)}, f32[8,64,128]{2,1,0:T(8,128)}, u32[]{:S(2)}) %copy-start.8) | copy-done | bytes 262168
  70.8 3.4 %shard_map.51 = f32[64,128,128]{2,1,0:T(8,128)} custom-call(bf16[128,160]{1,0:T(8,128)(2,1)S(1)} %get-tuple-element.28.maps_ref, bf16[192,8192]{1,0:T(8,128)(2,1)S(1)} %get-tuple-element.17.stack_ref.near_ref, bf16[128,8192]{1,0:T(8,128)(2,1)S(1)} %copy-done.1, f32[8,64,128]{2,1,0:T(8,128)S(1)} %get-tuple-element.21.mine_ref.order_ref.keep_ref, ...), custom_call_target="tpu_custom_call" | custom-call | tf_op jit(solution)/shard_map/pallas_call | solution.py:463
  (22 shorter events, 0.3 us)
Async XLA Ops:
  0.6 1.0 %copy-start.2 = (f32[8,8,16,128]{3,2,1,0:T(8,128)S(1)}, f32[8,8,16,128]{3,2,1,0:T(8,128)}, u32[]{:S(2)}) copy-start(f32[8,8,16,128]{3,2,1,0:T(8,128)} %x_ref.5) | copy-start | bytes 1572868
  1.7 11.7 %copy-start.3 = (f32[8,8,16,128]{3,2,1,0:T(8,128)S(1)}, f32[8,8,16,128]{3,2,1,0:T(8,128)}, u32[]{:S(2)}) copy-start(f32[8,8,16,128]{3,2,1,0:T(8,128)} %x_ref.5) | copy-start | bytes 1572868
  1.9 4.2 %collective-permute-start.1 = (f32[128,128]{1,0:T(8,128)S(1)}, f32[128,128]{1,0:T(8,128)S(1)}, u32[]{:S(2)}, u32[]{:S(2)}) collective-permute-start(f32[128,128]{1,0:T(8,128)S(1)} %shard_map.41.packed_ref), channel_id=1, source_target_pairs={{0,16},{16,0},{1,17},{17,1},{2,18},{18,2},{3,19},{19,3},{4,20},{20... | collective-permute-start | bytes 196616 | tf_op jit(solution)/shard_map/ppermute | solution.py:402
  5.2 3.7 %collective-permute-start = (f32[128,128]{1,0:T(8,128)S(1)}, f32[128,128]{1,0:T(8,128)S(1)}, u32[]{:S(2)}, u32[]{:S(2)}) collective-permute-start(f32[128,128]{1,0:T(8,128)S(1)} %shard_map.41.packed_ref), channel_id=1, source_target_pairs={{16,32},{32,16},{48,64},{64,48},{80,96},{96,80},{112,128},{128,112... | collective-permute-start | bytes 196616 | tf_op jit(solution)/shard_map/ppermute | solution.py:398
  9.0 4.3 %collective-permute-start.2 = (f32[27,8,128]{2,1,0:T(8,128)S(1)}, f32[27,8,128]{2,1,0:T(8,128)S(1)}, u32[]{:S(2)}, u32[]{:S(2)}) collective-permute-start(f32[27,8,128]{2,1,0:T(8,128)S(1)} %get-tuple-element.19), channel_id=1, source_target_pairs={{0,2},{2,0},{4,6},{6,4},{8,10},{10,8},{12,14},{14,12},{1,3},{3,1},... | collective-permute-start | bytes 331784 | tf_op jit(solution)/shard_map/ppermute | solution.py:398
  9.1 4.3 %collective-permute-start.3 = (f32[27,8,128]{2,1,0:T(8,128)S(1)}, f32[27,8,128]{2,1,0:T(8,128)S(1)}, u32[]{:S(2)}, u32[]{:S(2)}) collective-permute-start(f32[27,8,128]{2,1,0:T(8,128)S(1)} %get-tuple-element.20), channel_id=1, source_target_pairs={{2,4},{4,2},{6,8},{8,6},{10,12},{12,10},{3,5},{5,3},{7,9},{9,7},{1... | collective-permute-start | bytes 331784 | tf_op jit(solution)/shard_map/ppermute | solution.py:398
  16.1 7.0 %copy-start.7 = (f32[8,64,128]{2,1,0:T(8,128)}, f32[8,64,128]{2,1,0:T(8,128)S(1)}, u32[]{:S(2)}) copy-start(f32[8,64,128]{2,1,0:T(8,128)S(1)} %get-tuple-element.23.send_ref) | copy-start | bytes 786436
  16.1 7.0 %collective-permute-start.4 = (f32[8,64,128]{2,1,0:T(8,128)S(1)}, f32[8,64,128]{2,1,0:T(8,128)S(1)}, u32[]{:S(2)}, u32[]{:S(2)}) collective-permute-start(f32[8,64,128]{2,1,0:T(8,128)S(1)} %get-tuple-element.23.send_ref), channel_id=1, source_target_pairs={{0,1},{1,0},{2,3},{3,2},{4,5},{5,4},{6,7},{7,6},{8,9},{9,8},{10,11... | collective-permute-start | bytes 786440 | tf_op jit(solution)/shard_map/ppermute | solution.py:402
  20.9 3.8 %copy-start = (bf16[128,8192]{1,0:T(8,128)(2,1)}, bf16[128,8192]{1,0:T(8,128)(2,1)S(1)}, u32[]{:S(2)}) copy-start(bf16[128,8192]{1,0:T(8,128)(2,1)S(1)} %shard_map.46.order_ref.far_ref) | copy-start | bytes 6291460
  23.1 1.6 %copy-start.4 = (f32[8,64,128]{2,1,0:T(8,128)}, f32[8,64,128]{2,1,0:T(8,128)S(1)}, u32[]{:S(2)}) copy-start(f32[8,64,128]{2,1,0:T(8,128)S(1)} %collective-permute-done.4.other_ref.here_ref) | copy-start | bytes 786436
  24.7 4.5 %collective-permute-start.5 = (f32[16,128]{1,0:T(8,128)S(1)}, f32[16,128]{1,0:T(8,128)S(1)}, u32[]{:S(2)}, u32[]{:S(2)}) collective-permute-start(f32[16,128]{1,0:T(8,128)S(1)} %get-tuple-element.27), channel_id=1, source_target_pairs={{0,16},{16,0},{1,17},{17,1},{2,18},{18,2},{3,19},{19,3},{4,20},{20... | collective-permute-start | bytes 24584 | tf_op jit(solution)/shard_map/ppermute | solution.py:402
  29.2 0.7 copy-start.6
  29.9 14.1 %all-to-all-start = ((f32[16,16,128]{2,1,0:T(8,128)}), f32[16,16,128]{2,1,0:T(8,128)S(1)}, u32[]{:S(2)}, u32[]{:S(2)}) async-start(f32[16,16,128]{2,1,0:T(8,128)} %copy-done.6), calls=%async_computation | async-start | bytes 262144 | tf_op jit(solution)/shard_map/all_to_all | solution.py:406
  36.9 30.4 %collective-permute-start.6 = (f32[8,64,128]{2,1,0:T(8,128)S(1)}, f32[8,64,128]{2,1,0:T(8,128)}, u32[]{:S(2)}, u32[]{:S(2)}) collective-permute-start(f32[8,64,128]{2,1,0:T(8,128)S(1)} %get-tuple-element.21.mine_ref.order_ref.keep_ref), channel_id=1, source_target_pairs={{0,1},{1,0},{2,3},{3,2},{4,5},{5,4},{6,7},{7,6},{8,9},{9,8},{10,11... | collective-permute-start | bytes 786440 | tf_op jit(solution)/shard_map/ppermute | solution.py:402
  67.3 1.6 %copy-start.1 = (bf16[128,8192]{1,0:T(8,128)(2,1)S(1)}, bf16[128,8192]{1,0:T(8,128)(2,1)}, u32[]{:S(2)}) copy-start(bf16[128,8192]{1,0:T(8,128)(2,1)} %copy-done) | copy-start | bytes 6291460
  68.9 0.9 %copy-start.5 = (f32[8,64,128]{2,1,0:T(8,128)S(1)}, f32[8,64,128]{2,1,0:T(8,128)}, u32[]{:S(2)}) copy-start(f32[8,64,128]{2,1,0:T(8,128)} %copy-done.4) | copy-start | bytes 786436
  69.8 0.9 %copy-start.8 = (f32[8,64,128]{2,1,0:T(8,128)S(1)}, f32[8,64,128]{2,1,0:T(8,128)}, u32[]{:S(2)}) copy-start(f32[8,64,128]{2,1,0:T(8,128)} %copy-done.7) | copy-start | bytes 786436
